TPU v7x, 128 devices: a whole 4x4x4 slice. The times are simulated.
128 devices in a mesh: lat: 32 (over y, z, core), slot: 4 (over x).
Axes of the slice: x: 4, y: 4, z: 4, core: 2. Of those that a mesh axis runs over, the one named last changes fastest.
Arguments:
- seasonal_normals: bfloat16 [64, 8, 704, 1440], P('slot', None, 'lat'), may hold values from -24 to 24
- overlay_coarse_parallels: int32 [128, 10], P('lat'), may hold values from 0 to 703, as said below
- overlay_extent_factor: float32 [128, 10], P('lat'), may hold values from 0.2 to 1
- overlay_member_number: int32 [128], P('lat'), may hold values from 7 to 10
- verifying_seasonal_bin: int32 [128, 4], P('slot'), may hold values from 0 to 63
- prognosis_grid: bfloat16 [128, 4, 8, 128, 240], P('slot', None, None, 'lat'), may hold values from -6 to 6
- observed_analysis: bfloat16 [128, 4, 8, 128, 240], P('slot', None, None, 'lat'), may hold values from -6 to 6
Outputs:
- rmse_map: float32 [4, 8, 128, 240], P('slot', None, 'lat')
- acc_map: float32 [4, 8, 128, 240], P('slot', None, 'lat')
Inputs may be any that keep to these rules, and one draw needn't show every extreme that they name: `overlay_coarse_parallels`: for k < overlay_member_number[t] the entries of row t are the consecutive source rows that target row t margins; later entries are padding and repeat live entries. With center(t) = ((2t + 1) * 704) // 256, every entry of row t lies in source rows max(center(t) - 5, 0) to min(center(t) + 4, 703).
All inputs are finite; a program needn't handle non-finite values.
Results may differ from a plain program's by a relative error of at most 0.00085.
Values may be sent and summed in bfloat16 or wider, within the bound.
No kernel may reach another device: no remote copies, remote signals or barrier semaphores. Data moves between devices by JAX's collectives and lax.ppermute only.
A program may use at most 256 MiB of HBM per device.

v0:
```python
import math

import jax
import jax.numpy as jnp
from jax import lax
from jax.sharding import PartitionSpec as P

DEST_PARALLELS = 128


RIM_ROWS = 3


def extended(value, sides, width):
    for axis, dim in sides:
        devices, length = (lax.axis_size(axis), value.shape[dim])
        up = [(i, (i + 1) % devices) for i in range(devices - 1)]
        down = [(j, i) for i, j in up]
        last = lax.slice_in_dim(value, length - width, length, axis=dim)
        initial = lax.slice_in_dim(value, 0, width, axis=dim)
        before = lax.ppermute(last, axis, up)
        after = lax.ppermute(initial, axis, down)
        value = jnp.concatenate([before, value, after], axis=dim)
    return value


def lon_average(field, meridian_refinement):
    shaped = field.reshape(
        field.shape[0],
        field.shape[1],
        field.shape[2],
        field.shape[3] // meridian_refinement,
        meridian_refinement,
    )
    return (jnp.sum(shaped, axis=-1, dtype=jnp.float32) * (1.0 / meridian_refinement)).astype(
        jnp.bfloat16
    )


def body(
    seasonal_normals,
    overlay_coarse_parallels,
    overlay_extent_factor,
    overlay_member_number,
    verifying_seasonal_bin,
    prognosis_grid,
    observed_analysis,
):
    band_rows = seasonal_normals.shape[2]
    tile_rows = overlay_coarse_parallels.shape[0]
    meridian_refinement = seasonal_normals.shape[3] // prognosis_grid.shape[4]
    lat_index = lax.axis_index("lat")
    wide_rows = extended(seasonal_normals, (("lat", 2),), RIM_ROWS)
    near_rows = lon_average(wide_rows, meridian_refinement)
    base_row = lat_index * band_rows - RIM_ROWS
    local_index = overlay_coarse_parallels - base_row
    live_slots = (
        jnp.arange(overlay_coarse_parallels.shape[1], dtype=jnp.int32)[None, :]
        < overlay_member_number[:, None]
    )
    raw_weight = jnp.where(live_slots, overlay_extent_factor, jnp.zeros_like(overlay_extent_factor))
    weight = raw_weight / jnp.sum(raw_weight, axis=1, keepdims=True)
    positions = jnp.arange(band_rows + 2 * RIM_ROWS, dtype=jnp.int32)
    dense_block = jnp.sum(
        weight[:, :, None]
        * (local_index[:, :, None] == positions[None, None, :]).astype(jnp.float32),
        axis=1,
    )
    climate = jnp.einsum(
        "tr,scrj->sctj", dense_block, near_rows.astype(jnp.float32), precision=lax.Precision.HIGHEST
    )
    all_slots = lax.all_gather(climate, "slot", axis=0, tiled=True)
    onehot = (
        verifying_seasonal_bin[:, :, None]
        == jnp.arange(all_slots.shape[0], dtype=jnp.int32)[None, None, :]
    ).astype(jnp.float32)
    clim_valid = jnp.einsum("dls,sctj->dlctj", onehot, all_slots, precision=lax.Precision.HIGHEST)
    prognosis_snapshot = prognosis_grid.astype(jnp.float32)
    observed = observed_analysis.astype(jnp.float32)
    error = prognosis_snapshot - observed
    fore_anom = prognosis_snapshot - clim_valid
    true_anom = observed - clim_valid
    totals = (
        jnp.sum(error * error, axis=0),
        jnp.sum(fore_anom * true_anom, axis=0),
        jnp.sum(fore_anom * fore_anom, axis=0),
        jnp.sum(true_anom * true_anom, axis=0),
    )
    squared_misfit, cross_sum, fore_sq, true_sq = (
        lax.psum_scatter(totals[0], "slot", scatter_dimension=0, tiled=True),
        lax.psum_scatter(totals[1], "slot", scatter_dimension=0, tiled=True),
        lax.psum_scatter(totals[2], "slot", scatter_dimension=0, tiled=True),
        lax.psum_scatter(totals[3], "slot", scatter_dimension=0, tiled=True),
    )
    latitude = (jnp.arange(DEST_PARALLELS, dtype=jnp.float32) + 0.5) * (
        math.pi / DEST_PARALLELS
    ) - 0.5 * math.pi
    cosine = jnp.cos(latitude)
    parallel_cosine_factor = lax.dynamic_slice_in_dim(
        cosine, lat_index * tile_rows, tile_rows, 0
    ) / jnp.mean(cosine)
    overall_initial_days = prognosis_grid.shape[0] * lax.axis_size("slot")
    rmse_map = jnp.sqrt(
        parallel_cosine_factor[None, None, :, None] * squared_misfit / overall_initial_days
    )
    acc_map = cross_sum / jnp.sqrt(fore_sq * true_sq + 1e-06)
    return (rmse_map, acc_map)


def solution(mesh):
    placed = (
        P("slot", None, "lat", None),
        P("lat", None),
        P("lat", None),
        P("lat"),
        P("slot", None),
        P("slot", None, None, "lat", None),
        P("slot", None, None, "lat", None),
    )
    return jax.shard_map(
        body,
        mesh=mesh,
        in_specs=placed,
        out_specs=(P("slot", None, "lat", None), P("slot", None, "lat", None)),
        check_vma=False,
    )
```

profile of v0, /device:TPU:0, one launch (start us, length us, event | category | flops | bytes accessed | tf_op | source)
XLA Modules:
  0.0 292.4 jit_solution(1181307694959368511)
XLA Ops:
  7.2 2.8 fusion.18
  10.1 1.4 collective-permute-start
  11.4 1.3 collective-permute-start.1
  12.8 0.1 copy.52
  12.9 0.8 fusion.16
  13.7 1.3 fusion.15
  15.0 0.8 copy.53
  15.8 0.7 select_reduce_fusion
  16.4 1.9 collective-permute-done.1
  18.4 12.2 %maximum_convert_fusion = f32[16,8,28,1440]{3,1,2,0:T(8,128)} fusion(bf16[16,8,3,1440]{3,1,2,0:T(8,128)(2,1)S(1)} %collective-permute-done.1, bf16[16,8,22,1440]{3,1,2,0:T(8,128)(2,1)} %param.7, bf16[16,8,3,1440]{3,1,2,0:T(8,128)(2,1)S(1)} %collective-permute-done), kind=kLoop, calls=%fused_computation | loop fusion | flops 15482880 | bytes 30965760 | tf_op jit(solution)/shard_map/convert_element_type | solution.py:35
  30.6 55.8 %copy.50 = f32[16,8,28,1440]{2,1,3,0:T(8,128)} copy(f32[16,8,28,1440]{3,1,2,0:T(8,128)} %maximum_convert_fusion) | data formatting | bytes 41287680 | tf_op jit(solution)/shard_map/convert_element_type | solution.py:35
  86.4 35.6 %reduce_sum.74 = f32[16,8,28,240]{2,1,3,0:T(8,128)} reduce(f32[16,8,28,240,6]{2,1,4,3,0:T(8,128)} %bitcast.2, f32[]{:T(128)} %constant.13.clone.1), dimensions={4}, to_apply=%region_3.4 | reduce | flops 4300800 | bytes 24084484 | tf_op jit(solution)/shard_map/reduce_sum | solution.py:35
  122.0 11.2 %copy.51 = f32[16,8,28,240]{3,1,2,0:T(8,128)} copy(f32[16,8,28,240]{2,1,3,0:T(8,128)} %reduce_sum.74) | data formatting | bytes 6881280 | tf_op jit(solution)/shard_map/reduce_sum | solution.py:35
  133.2 2.6 multiply_convert_fusion
  135.9 1.0 fusion.7
  136.8 0.9 copy.55
  137.8 46.3 %all-gather.2.cloned.1.call-done = f32[64,8,4,240]{3,1,2,0:T(8,128)} async-done(((f32[16,8,4,240]{3,1,2,0:T(8,128)}), f32[64,8,4,240]{3,1,2,0:T(8,128)}) %all-gather.2.cloned.1.call-update) | async-done | bytes 1966096 | tf_op jit(solution)/shard_map/all_gather | solution.py:72
  184.1 10.8 %multiply_reduce_fusion = (f32[4,8,4,240]{3,2,1,0:T(4,128)S(1)}, f32[4,8,4,240]{3,2,1,0:T(4,128)S(1)}, f32[4,8,4,240]{3,2,1,0:T(4,128)S(1)}, f32[4,8,4,240]{3,2,1,0:T(4,128)S(1)}) fusion(bf16[32,4,8,4,240]{4,3,2,1,0:T(4,128)(2,1)S(1)} %copy-done.3, bf16[32,4,8,4,240]{4,3,2,1,0:T(4,128)(2,1)} %param.12, f32[64,8,4,240]{3,1,2,0:T(8,128)} %all-gather.2.cloned.1.call-done, ...), kind=kOutput, calls=%fused_computation.6 | convolution fusion | flops 767639552 | bytes 6390272 | tf_op jit(solution)/shard_map/dls,sctj->dlctj/dot_general | solution.py:77
  194.9 0.7 copy.59
  195.6 0.7 copy.57
  196.4 0.7 copy.58
  197.1 0.7 fusion.17
  198.5 0.7 copy.49
  199.2 0.1 dynamic-slice_divide_fusion
  199.3 17.1 %reduce-scatter.11.cloned.1.call-done = f32[1,8,4,240]{3,1,2,0:T(8,128)} async-done(((f32[4,8,4,240]{3,1,2,0:T(8,128)}), f32[1,8,4,240]{3,1,2,0:T(8,128)}) %reduce-scatter.11.cloned.1.call-update) | async-done | bytes 30736 | tf_op jit(solution)/shard_map/reduce_scatter | solution.py:93
  216.4 22.8 %reduce-scatter.7.cloned.1.call-done = f32[1,8,4,240]{3,1,2,0:T(8,128)} async-done(((f32[4,8,4,240]{3,1,2,0:T(8,128)}), f32[1,8,4,240]{3,1,2,0:T(8,128)}) %reduce-scatter.7.cloned.1.call-update) | async-done | bytes 30736 | tf_op jit(solution)/shard_map/reduce_scatter | solution.py:91
  239.2 22.6 %reduce-scatter.9.cloned.1.call-done = f32[1,8,4,240]{3,1,2,0:T(8,128)} async-done(((f32[4,8,4,240]{3,1,2,0:T(8,128)}), f32[1,8,4,240]{3,1,2,0:T(8,128)}) %reduce-scatter.9.cloned.1.call-update) | async-done | bytes 30736 | tf_op jit(solution)/shard_map/reduce_scatter | solution.py:92
  261.8 0.8 rsqrt_multiply_fusion
  262.6 0.6 copy.61
  263.2 21.2 %reduce-scatter.5.cloned.1.call-done = f32[1,8,4,240]{3,1,2,0:T(8,128)} async-done(((f32[4,8,4,240]{3,1,2,0:T(8,128)}), f32[1,8,4,240]{3,1,2,0:T(8,128)}) %reduce-scatter.5.cloned.1.call-update) | async-done | bytes 30736 | tf_op jit(solution)/shard_map/reduce_scatter | solution.py:90
  284.4 0.8 multiply_sqrt_fusion
  285.2 0.6 copy.60
  (23 shorter events, 0.4 us)
Async XLA Ops:
  7.2 5.6 %copy-start.2 = (s32[4,10]{1,0:T(4,128)S(1)}, s32[4,10]{1,0:T(4,128)}, u32[]{:S(2)}) copy-start(s32[4,10]{1,0:T(4,128)} %param.8) | copy-start | bytes 484
  7.2 5.7 %copy-start = (f32[4,10]{1,0:T(4,128)S(1)}, f32[4,10]{1,0:T(4,128)}, u32[]{:S(2)}) copy-start(f32[4,10]{1,0:T(4,128)} %param.9) | copy-start | bytes 484
  7.2 176.9 %all-gather.2.cloned.1.call-start = ((), (), s32[]{:S(2)}) async-start(), calls=%async_computation.5 | async-start | bytes 2621440 | tf_op jit(solution)/shard_map/all_gather | solution.py:72
  10.1 6.4 %collective-permute-start = (bf16[16,8,3,1440]{3,1,2,0:T(8,128)(2,1)}, bf16[16,8,3,1440]{3,1,2,0:T(8,128)(2,1)S(1)}, u32[]{:S(2)}, u32[]{:S(2)}) collective-permute-start(bf16[16,8,3,1440]{3,1,2,0:T(8,128)(2,1)} %get-tuple-element.14), channel_id=1, source_target_pairs={{0,4},{4,8},{8,12},{12,16},{16,20},{20,24},{24,28},{28,32},{32,36}... | collective-permute-start | bytes 3317768 | tf_op jit(solution)/shard_map/ppermute | solution.py:21
  11.4 6.9 %collective-permute-start.1 = (bf16[16,8,3,1440]{3,1,2,0:T(8,128)(2,1)S(1)}, bf16[16,8,3,1440]{3,1,2,0:T(8,128)(2,1)S(1)}, u32[]{:S(2)}, u32[]{:S(2)}) collective-permute-start(bf16[16,8,3,1440]{3,1,2,0:T(8,128)(2,1)S(1)} %get-tuple-element.15), channel_id=1, source_target_pairs={{4,0},{8,4},{12,8},{16,12},{20,16},{24,20},{28,24},{32,28},{36,32}... | collective-permute-start | bytes 3317768 | tf_op jit(solution)/shard_map/ppermute | solution.py:22
  133.2 2.6 copy-start.1
  133.2 50.8 %copy-start.3 = (bf16[32,4,8,4,240]{4,3,2,1,0:T(4,128)(2,1)S(1)}, bf16[32,4,8,4,240]{4,3,2,1,0:T(4,128)(2,1)}, u32[]{:S(2)}) copy-start(bf16[32,4,8,4,240]{4,3,2,1,0:T(4,128)(2,1)} %param.13) | copy-start | bytes 5898244
  133.2 50.8 %copy-start.4 = (s32[32,4]{0,1:T(4,128)S(1)}, s32[32,4]{0,1:T(4,128)}, u32[]{:S(2)}) copy-start(s32[32,4]{0,1:T(4,128)} %param.11) | copy-start | bytes 1540
  137.7 78.6 %reduce-scatter.11.cloned.1.call-start = ((), (), s32[]{:S(2)}) async-start(), calls=%async_computation.8 | async-start | bytes 163840 | tf_op jit(solution)/shard_map/reduce_scatter | solution.py:93
  195.6 43.6 %reduce-scatter.7.cloned.1.call-start = ((), (), s32[]{:S(2)}) async-start(), calls=%async_computation.6 | async-start | bytes 163840 | tf_op jit(solution)/shard_map/reduce_scatter | solution.py:91
  196.3 65.4 %reduce-scatter.9.cloned.1.call-start = ((), (), s32[]{:S(2)}) async-start(), calls=%async_computation.7 | async-start | bytes 163840 | tf_op jit(solution)/shard_map/reduce_scatter | solution.py:92
  197.1 87.3 %reduce-scatter.5.cloned.1.call-start = ((), (), s32[]{:S(2)}) async-start(), calls=%async_computation.4 | async-start | bytes 163840 | tf_op jit(solution)/shard_map/reduce_scatter | solution.py:90
Sparse Core Ops, SparseCore 0:
  137.9 46.1 all-gather.1
  195.7 20.6 reduce-scatter.10
  218.8 20.3 reduce-scatter.6
  241.4 20.3 reduce-scatter.8
  264.0 20.3 reduce-scatter.4
where the time goes:
time: 294 us; the launch traced here: 292 us
  waiting for transfers between devices  132 us (45%)
  local copies, waits for them, and re-layouts  75.6 us (26%)
  other arithmetic  55.7 us (19%)
  between operations  14.5 us (5%)
  matrix products  11.8 us (4%)
    convert_element_type x1, local copies, waits for them, and re-layouts, lon_average(): jnp.sum(shaped, axis=-1, dtype=jnp.float32) * (1.0 / meridian_refinement)  55.8 us
    all_gather x1, waiting for transfers between devices, body(): all_slots = lax.all_gather(climate, 'slot', axis=0, tiled=True)  46.3 us
    reduce_sum x1, other arithmetic, lon_average(): jnp.sum(shaped, axis=-1, dtype=jnp.float32) * (1.0 / meridian_refinement)  35.6 us
    reduce_scatter x1, waiting for transfers between devices, body(): lax.psum_scatter(totals[1], 'slot', scatter_dimension=0, tiled=True)  22.8 us
    reduce_scatter x1, waiting for transfers between devices, body(): lax.psum_scatter(totals[2], 'slot', scatter_dimension=0, tiled=True)  22.6 us
    reduce_scatter x1, waiting for transfers between devices, body(): lax.psum_scatter(totals[0], 'slot', scatter_dimension=0, tiled=True)  21.2 us
    reduce_scatter x1, waiting for transfers between devices, body(): lax.psum_scatter(totals[3], 'slot', scatter_dimension=0, tiled=True)  17.1 us
    convert_element_type x1, other arithmetic, lon_average(): jnp.sum(shaped, axis=-1, dtype=jnp.float32) * (1.0 / meridian_refinement)  12.2 us
  transfers between devices with their start and end apart: 7, of which 6 were waited for; matrix products, arithmetic and copies ran while one was open for 3% of the time, Pallas kernels for 0%

commit v1 on v0

v1 whole, which is shorter than its diff:
```python
import math

import jax
import jax.numpy as jnp
import numpy as np
from jax import lax
from jax.experimental import pallas as pl
from jax.experimental.pallas import tpu as pltpu
from jax.sharding import PartitionSpec as P

SRC_LON = 1440
DEST_PARALLELS = 128
DEST_MERIDIANS = 240
FINE = SRC_LON // DEST_MERIDIANS
VARS = 8
BAND = 22
TILE = 4
OVER = 10
UP = 3
DOWN = 2
MID = BAND - UP - DOWN
ROWS = BAND + UP + DOWN
BINS = 16
DAYS = 32
SLOTS = 4
FLAT = VARS * TILE
CODE_RATE = 10.0
CODE_BASE = 120.0


def shifted(value, step):
    slots = lax.axis_size("slot")
    return lax.ppermute(value, "slot", [(i, (i + step) % slots) for i in range(slots)])


def lon_table():
    fine = np.arange(SRC_LON)[:, None] // FINE
    return jnp.asarray(fine == np.arange(DEST_MERIDIANS)[None, :], dtype=jnp.bfloat16)


def lon_mean(rows, table):
    flat = rows.reshape(-1, SRC_LON)
    total = jnp.dot(flat, table, preferred_element_type=jnp.float32)
    return (total * (1.0 / FINE)).astype(jnp.bfloat16).reshape(*rows.shape[:-1], DEST_MERIDIANS)


def edge_kernel(low_ref, high_ref, table_ref, down_ref, up_ref):
    table = table_ref[...]
    up_ref[...] = lon_mean(high_ref[...], table)
    down_ref[...] = lon_mean(low_ref[...], table)


def band_rows(chunk, first, count):
    sizes = (chunk, count, VARS, SRC_LON)
    return pl.BlockSpec(tuple(pl.Element(n) for n in sizes), lambda i: (i * chunk, first, 0, 0))


def edges(field, table):
    chunk = 4
    spec = lambda count: pl.BlockSpec(
        (chunk, count, VARS, DEST_MERIDIANS), lambda i: (i, 0, 0, 0)
    )
    shape = lambda count: jax.ShapeDtypeStruct((BINS, count, VARS, DEST_MERIDIANS), jnp.bfloat16)
    return pl.pallas_call(
        edge_kernel,
        grid=(BINS // chunk,),
        in_specs=[
            band_rows(chunk, 0, DOWN),
            band_rows(chunk, BAND - UP, UP),
            pl.BlockSpec((SRC_LON, DEST_MERIDIANS), lambda i: (0, 0)),
        ],
        out_specs=[spec(DOWN), spec(UP)],
        out_shape=[shape(DOWN), shape(UP)],
        name="edge_lon",
    )(field, field, table)


def mid_kernel(rows_ref, table_ref, out_ref):
    out_ref[...] = lon_mean(rows_ref[...], table_ref[...])


def middle(field, table):
    chunk = 2
    return pl.pallas_call(
        mid_kernel,
        grid=(BINS // chunk,),
        in_specs=[
            band_rows(chunk, DOWN, MID),
            pl.BlockSpec((SRC_LON, DEST_MERIDIANS), lambda i: (0, 0)),
        ],
        out_specs=pl.BlockSpec((chunk, MID, VARS, DEST_MERIDIANS), lambda i: (i, 0, 0, 0)),
        out_shape=jax.ShapeDtypeStruct((BINS, MID, VARS, DEST_MERIDIANS), jnp.bfloat16),
        name="mid_lon",
        cost_estimate=pl.CostEstimate(flops=2 * 10**9, bytes_accessed=8 * 10**6, transcendentals=0),
    )(field, table)


def encode(value):
    size = jnp.exp2(CODE_RATE * jnp.abs(value) - CODE_BASE)
    return jnp.where(value < 0, -size, size).astype(jnp.bfloat16)


def decode(code):
    wide = code.astype(jnp.float32)
    size = (jnp.log2(jnp.abs(wide)) + CODE_BASE) * (1.0 / CODE_RATE)
    return jnp.where(wide < 0, -size, size)


def weight_matrix(index_ref, extent_ref, count_ref):
    base = lax.axis_index("lat") * BAND - UP
    line = lax.broadcasted_iota(jnp.int32, (FLAT, ROWS * VARS), 0)
    lane = lax.broadcasted_iota(jnp.int32, (FLAT, ROWS * VARS), 1)
    place = jnp.where(line // TILE == lane % VARS, lane // VARS, -1)
    dense = jnp.zeros((FLAT, ROWS * VARS), jnp.float32)
    sums = jnp.ones((FLAT, ROWS * VARS), jnp.float32)
    for t in range(TILE):
        here = line % TILE == t
        spot = jnp.where(here, place, -1)
        total = jnp.float32(0.0)
        for k in range(OVER):
            value = jnp.where(k < count_ref[t], extent_ref[t, k], jnp.float32(0.0))
            total = total + value
            dense = dense + jnp.where(spot == index_ref[t, k] - base, value, 0.0)
        sums = jnp.where(here, total, sums)
    dense = dense / sums
    high = dense.astype(jnp.bfloat16)
    rest = dense - high.astype(jnp.float32)
    middle_part = rest.astype(jnp.bfloat16)
    low = (rest - middle_part.astype(jnp.float32)).astype(jnp.bfloat16)
    return jnp.concatenate([high, middle_part, low], axis=0)


def climate_kernel(
    index_ref, extent_ref, count_ref, below_ref, down_ref, mid_ref, up_ref, above_ref, code_ref
):
    weights = weight_matrix(index_ref, extent_ref, count_ref)
    for s in range(BINS):
        rows = jnp.concatenate(
            [below_ref[s], down_ref[s], mid_ref[s], up_ref[s], above_ref[s]], axis=0
        ).reshape(ROWS * VARS, DEST_MERIDIANS)
        parts = jnp.dot(weights, rows, preferred_element_type=jnp.float32)
        value = parts[:FLAT] + parts[FLAT : 2 * FLAT] + parts[2 * FLAT :]
        code_ref[s] = encode(value)


def climate_code(index, extent, count, below, down, mid, up, above):
    smem = pl.BlockSpec(memory_space=pltpu.SMEM)
    vmem = pl.BlockSpec(memory_space=pltpu.VMEM)
    return pl.pallas_call(
        climate_kernel,
        in_specs=[smem] * 3 + [vmem] * 5,
        out_specs=vmem,
        out_shape=jax.ShapeDtypeStruct((BINS, FLAT, DEST_MERIDIANS), jnp.bfloat16),
        name="climate",
    )(index, extent, count, below, down, mid, up, above)


def sums_kernel(
    bins_ref, own_ref, right_ref, far_low_ref, far_high_ref, left_ref, fore_ref, obs_ref,
    out_ref, clim_ref,
):
    slot = lax.axis_index("slot")
    lead = lax.rem(pl.program_id(0) + 1 + slot, SLOTS)

    @pl.when(pl.program_id(0) == 0)
    def _():
        half = BINS // 2
        clim_ref[:BINS] = decode(own_ref[...])
        clim_ref[BINS : 2 * BINS] = decode(right_ref[...])
        clim_ref[2 * BINS : 2 * BINS + half] = decode(far_low_ref[...])
        clim_ref[2 * BINS + half : 3 * BINS] = decode(far_high_ref[...])
        clim_ref[3 * BINS :] = decode(left_ref[...])

    half = VARS // 2
    lines = half * TILE
    for h in range(2):

        def step(d, sums):
            squared, cross, fore_sq, true_sq = sums
            fore = fore_ref[d, 0, h * half : (h + 1) * half].astype(jnp.float32)
            fore = fore.reshape(lines, DEST_MERIDIANS)
            obs = obs_ref[d, 0, h * half : (h + 1) * half].astype(jnp.float32)
            obs = obs.reshape(lines, DEST_MERIDIANS)
            wanted = bins_ref[lead, d]
            spot = (wanted // BINS - slot) % SLOTS * BINS + wanted % BINS
            clim = clim_ref[spot, h * lines : (h + 1) * lines]
            error = fore - obs
            fore_anom = fore - clim
            true_anom = obs - clim
            return (
                squared + error * error,
                cross + fore_anom * true_anom,
                fore_sq + fore_anom * fore_anom,
                true_sq + true_anom * true_anom,
            )

        zero = jnp.zeros((lines, DEST_MERIDIANS), jnp.float32)
        sums = lax.fori_loop(0, DAYS, step, (zero,) * 4, unroll=4)
        for n, value in enumerate(sums):
            out_ref[0, n, h * lines : (h + 1) * lines] = value


def skill_sums(bins, own, right, far_low, far_high, left, fore, obs):
    vmem = pl.BlockSpec(memory_space=pltpu.VMEM)
    days = pl.BlockSpec(
        (DAYS, 1, VARS, TILE, DEST_MERIDIANS),
        lambda i: (0, lax.rem(i + 1 + lax.axis_index("slot"), SLOTS), 0, 0, 0),
    )
    return pl.pallas_call(
        sums_kernel,
        grid=(SLOTS,),
        in_specs=[pl.BlockSpec(memory_space=pltpu.SMEM)] + [vmem] * 5 + [days] * 2,
        out_specs=pl.BlockSpec((1, 4, FLAT, DEST_MERIDIANS), lambda i: (i, 0, 0, 0)),
        out_shape=jax.ShapeDtypeStruct((SLOTS, 4, FLAT, DEST_MERIDIANS), jnp.float32),
        scratch_shapes=[pltpu.VMEM((SLOTS * BINS, FLAT, DEST_MERIDIANS), jnp.float32)],
        name="skill_sums",
    )(bins, own, right, far_low, far_high, left, fore, obs)


def maps_kernel(scale_ref, one_ref, two_ref, three_ref, own_ref, rmse_ref, acc_ref):
    lat = lax.axis_index("lat")
    total = own_ref[...] + one_ref[...] + two_ref[...] + three_ref[...]
    line = lax.broadcasted_iota(jnp.int32, (FLAT, DEST_MERIDIANS), 0)
    scale = jnp.zeros((FLAT, DEST_MERIDIANS), jnp.float32)
    for t in range(TILE):
        scale = jnp.where(line % TILE == t, scale_ref[lat * TILE + t], scale)
    days = DAYS * SLOTS
    rmse = jnp.sqrt(scale * total[0] / days)
    acc = total[1] / jnp.sqrt(total[2] * total[3] + 1e-06)
    rmse_ref[0] = rmse.reshape(VARS, TILE, DEST_MERIDIANS)
    acc_ref[0] = acc.reshape(VARS, TILE, DEST_MERIDIANS)


def maps(one, two, three, own):
    phi = (np.arange(DEST_PARALLELS, dtype=np.float32) + np.float32(0.5)) * np.float32(
        math.pi / DEST_PARALLELS
    ) - np.float32(0.5 * math.pi)
    cosine = np.cos(phi).astype(np.float32)
    scale = jnp.asarray(cosine / cosine.mean(dtype=np.float32))
    vmem = pl.BlockSpec(memory_space=pltpu.VMEM)
    shape = jax.ShapeDtypeStruct((1, VARS, TILE, DEST_MERIDIANS), jnp.float32)
    return pl.pallas_call(
        maps_kernel,
        in_specs=[pl.BlockSpec(memory_space=pltpu.SMEM)] + [vmem] * 4,
        out_specs=[vmem] * 2,
        out_shape=[shape] * 2,
        name="maps",
    )(scale, one, two, three, own)


def body(normals, index, extent, count, bins, prognosis, analysis):
    field = jnp.transpose(normals, (0, 2, 1, 3))
    table = lon_table()
    down, up = edges(field, table)
    devices = lax.axis_size("lat")
    below = lax.ppermute(up, "lat", [(i, i + 1) for i in range(devices - 1)])
    above = lax.ppermute(down, "lat", [(i + 1, i) for i in range(devices - 1)])
    mid = middle(field, table)
    own = climate_code(index, extent, count, below, down, mid, up, above)
    left = shifted(own, 1)
    right = shifted(own, -1)
    half = BINS // 2
    far_low = shifted(left[:half], 1)
    far_high = shifted(right[half:], -1)
    sums = skill_sums(
        jnp.transpose(bins), own, right, far_low, far_high, left, prognosis, analysis
    )
    two = shifted(sums[1], 2)
    one = shifted(sums[0], 1)
    three = shifted(sums[2], 3)
    return tuple(maps(one, two, three, sums[3]))


def solution(mesh):
    placed = (
        P("slot", None, "lat", None),
        P("lat", None),
        P("lat", None),
        P("lat"),
        P("slot", None),
        P("slot", None, None, "lat", None),
        P("slot", None, None, "lat", None),
    )
    return jax.shard_map(
        body,
        mesh=mesh,
        in_specs=placed,
        out_specs=(P("slot", None, "lat", None), P("slot", None, "lat", None)),
        check_vma=False,
    )
```

time: 294 us -> 63.1 us (0.21)
  waiting for transfers between devices: 132 us -> 18.1 us
  local copies, waits for them, and re-layouts: 75.6 us -> 4.45 us
  other arithmetic: 55.7 us -> 0 us
  Pallas kernels: 0 us -> 23.9 us
  between operations: 14.5 us -> 0.69 us
  starting transfers between devices: 2.85 us -> 15 us
  matrix products: 11.8 us -> 0 us
    reduce_scatter x4 -> x0, waiting for transfers between devices: 83.7 us -> none  [the longest x1 22.8 us: body(): lax.psum_scatter(totals[1], 'slot', scatter_dimension=0, tiled=True)]
    convert_element_type x1 -> x0, local copies, waits for them, and re-layouts: 55.8 us -> none  [lon_average(): jnp.sum(shaped, axis=-1, dtype=jnp.float32) * (1.0 / meridian_refinement)]
    all_gather x1 -> x0, waiting for transfers between devices: 46.3 us -> none  [body(): all_slots = lax.all_gather(climate, 'slot', axis=0, tiled=True)]
    reduce_sum x4 -> x0, other arithmetic: 37.8 us -> none  [the longest x1 35.6 us: lon_average(): jnp.sum(shaped, axis=-1, dtype=jnp.float32) * (1.0 / meridian_refinement)]
    pallas_call x0 -> x5, Pallas kernels: none -> 23.9 us  [the longest x1 8.03 us: middle(): pl.pallas_call(mid_kernel, grid=(BINS // chunk,), in_specs=[band_rows(chu...]
    ppermute x2 -> x9, waiting for transfers between devices: 1.91 us -> 18.1 us  [the longest x7 18.1 us: shifted(): lax.ppermute(value, 'slot', [(i, (i + step) % slots) for i in range(slots)])]
    convert_element_type x2 -> x0, other arithmetic: 14.8 us -> none  [the longest x1 12.2 us: lon_average(): jnp.sum(shaped, axis=-1, dtype=jnp.float32) * (1.0 / meridian_refinement)]
    reduce_sum x5 -> x0, local copies, waits for them, and re-layouts: 13.9 us -> none  [the longest x1 11.2 us: lon_average(): jnp.sum(shaped, axis=-1, dtype=jnp.float32) * (1.0 / meridian_refinement)]
  transfers between devices with their start and end apart: 7 -> 9, of which waited for: 6 -> 6; matrix products, arithmetic and copies ran while one was open for 3% -> 0% of each run, Pallas kernels for 0% -> 13%
where the time goes in v1:
time: 63.1 us; the launch traced here: 62.1 us
  Pallas kernels  23.9 us (38%)
  waiting for transfers between devices  18.1 us (29%)
  starting transfers between devices  15 us (24%)
  local copies, waits for them, and re-layouts  4.45 us (7%)
  between operations  0.69 us (1%)
    ppermute x7, waiting for transfers between devices, shifted(): lax.ppermute(value, 'slot', [(i, (i + step) % slots) for i in range(slots)])  18.1 us
    ppermute x7, starting transfers between devices, shifted(): lax.ppermute(value, 'slot', [(i, (i + step) % slots) for i in range(slots)])  10.6 us
    pallas_call x1, Pallas kernels, middle(): pl.pallas_call(mid_kernel, grid=(BINS // chunk,), in_specs=[band_rows(chu...  8.03 us
    pallas_call x1, Pallas kernels, skill_sums(): pl.pallas_call(sums_kernel, grid=(SLOTS,), in_specs=[pl.BlockSpec(memory_...  6.88 us
    pallas_call x1, Pallas kernels, edges(): pl.pallas_call(edge_kernel, grid=(BINS // chunk,), in_specs=[band_rows(ch...  4.44 us
    ppermute x1, starting transfers between devices, body(): below = lax.ppermute(up, 'lat', [(i, i + 1) for i in range(devices - 1)])  3.04 us
    pallas_call x1, Pallas kernels, climate_code(): pl.pallas_call(climate_kernel, in_specs=[smem] * 3 + [vmem] * 5, out_spec...  2.76 us
    unnamed x18, local copies, waits for them, and re-layouts  2.65 us
  transfers between devices with their start and end apart: 9, of which 6 were waited for; matrix products, arithmetic and copies ran while one was open for 0% of the time, Pallas kernels for 13%

profile of v1, /device:TPU:0, one launch (start us, length us, event | category | flops | bytes accessed | tf_op | source)
XLA Modules:
  0.0 62.1 jit_solution(42557024564999186)
XLA Ops:
  0.6 4.4 %edge_lon.1 = (bf16[16,2,8,240]{3,2,1,0:T(8,128)(2,1)}, bf16[16,3,8,240]{3,2,1,0:T(8,128)(2,1)}) custom-call(bf16[16,22,8,1440]{3,2,1,0:T(8,128)(2,1)} %bitcast.10, bf16[16,22,8,1440]{3,2,1,0:T(8,128)(2,1)} %bitcast.11, bf16[1440,240]{1,0:T(8,128)(2,1)} %constant.4.clone.table_ref), custom_call_target="tpu_custom_call" | custom-call | tf_op jit(solution)/shard_map/edge_lon/pallas_call | solution.py:64
  5.1 1.3 %collective-permute-start.1 = (bf16[16,2,8,240]{3,2,1,0:T(8,128)(2,1)}, bf16[16,2,8,240]{3,2,1,0:T(8,128)(2,1)S(1)}, u32[]{:S(2)}, u32[]{:S(2)}) collective-permute-start(bf16[16,2,8,240]{3,2,1,0:T(8,128)(2,1)} %get-tuple-element.5.down_ref), channel_id=1, source_target_pairs={{4,0},{8,4},{12,8},{16,12},{20,16},{24,20},{28,24},{32,28},{36,32}... | collective-permute-start | bytes 368648 | tf_op jit(solution)/shard_map/ppermute | solution.py:257
  6.4 3.0 %collective-permute-start = (bf16[16,3,8,240]{3,2,1,0:T(8,128)(2,1)}, bf16[16,3,8,240]{3,2,1,0:T(8,128)(2,1)S(1)}, u32[]{:S(2)}, u32[]{:S(2)}) collective-permute-start(bf16[16,3,8,240]{3,2,1,0:T(8,128)(2,1)} %get-tuple-element.4.up_ref), channel_id=1, source_target_pairs={{0,4},{4,8},{8,12},{12,16},{16,20},{20,24},{24,28},{28,32},{32,36}... | collective-permute-start | bytes 552968 | tf_op jit(solution)/shard_map/ppermute | solution.py:256
  9.4 8.0 %mid_lon.1.mid_ref = bf16[16,17,8,240]{3,2,1,0:T(8,128)(2,1)} custom-call(bf16[16,22,8,1440]{3,2,1,0:T(8,128)(2,1)} %bitcast.12, bf16[1440,240]{1,0:T(8,128)(2,1)} %constant.4.clone.table_ref), custom_call_target="tpu_custom_call" | custom-call | flops 2000000000 | bytes 8000000 | tf_op jit(solution)/shard_map/mid_lon/pallas_call | solution.py:84
  17.4 0.0 collective-permute-done.1.above_ref
  17.4 0.0 collective-permute-done.below_ref
  17.4 0.6 %copy-done.6 = bf16[16,2,8,240]{3,2,1,0:T(8,128)(2,1)} copy-done((bf16[16,2,8,240]{3,2,1,0:T(8,128)(2,1)}, bf16[16,2,8,240]{3,2,1,0:T(8,128)(2,1)S(1)}, u32[]{:S(2)}) %copy-start.6) | copy-done | bytes 122904
  18.1 0.7 %copy-done.2 = bf16[16,3,8,240]{3,2,1,0:T(8,128)(2,1)} copy-done((bf16[16,3,8,240]{3,2,1,0:T(8,128)(2,1)}, bf16[16,3,8,240]{3,2,1,0:T(8,128)(2,1)S(1)}, u32[]{:S(2)}) %copy-start.2) | copy-done | bytes 184344
  18.8 2.8 %climate.1.own_ref = bf16[16,32,240]{2,1,0:T(8,128)(2,1)} custom-call(s32[4,10]{1,0:T(4,128)} %index_ref.1, f32[4,10]{1,0:T(4,128)} %extent_ref.1, s32[4]{0:T(128)} %count_ref.1, bf16[16,3,8,240]{3,2,1,0:T(8,128)(2,1)} %copy-done.2, bf16[16,2,8,240]{3,2,1,0:T(8,128)(2,1)} %get-tuple-element.5.down_ref, bf16[16,17,8,240]{3,2,1,0:T(8,128)(2,1)} %mid_lon.1.mid_ref, ...), custom_call_target="tpu_custom_call" | custom-call | tf_op jit(solution)/shard_map/climate/pallas_call | solution.py:149
  21.5 1.6 %collective-permute-start.3 = (bf16[16,32,240]{2,1,0:T(8,128)(2,1)}, bf16[16,32,240]{2,1,0:T(8,128)(2,1)S(1)}, u32[]{:S(2)}, u32[]{:S(2)}) collective-permute-start(bf16[16,32,240]{2,1,0:T(8,128)(2,1)} %climate.1.own_ref), channel_id=1, source_target_pairs={{0,1},{1,2},{2,3},{3,0},{4,5},{5,6},{6,7},{7,4},{8,9},{9,10},{10,1... | collective-permute-start | bytes 737288 | tf_op jit(solution)/shard_map/ppermute | solution.py:33
  23.1 1.6 %collective-permute-start.2 = (bf16[16,32,240]{2,1,0:T(8,128)(2,1)}, bf16[16,32,240]{2,1,0:T(8,128)(2,1)S(1)}, u32[]{:S(2)}, u32[]{:S(2)}) collective-permute-start(bf16[16,32,240]{2,1,0:T(8,128)(2,1)} %climate.1.own_ref), channel_id=1, source_target_pairs={{0,3},{1,0},{2,1},{3,2},{4,7},{5,4},{6,5},{7,6},{8,11},{9,8},{10,9... | collective-permute-start | bytes 737288 | tf_op jit(solution)/shard_map/ppermute | solution.py:33
  24.8 6.7 %collective-permute-done.3.left_ref = bf16[16,32,240]{2,1,0:T(8,128)(2,1)S(1)} collective-permute-done((bf16[16,32,240]{2,1,0:T(8,128)(2,1)}, bf16[16,32,240]{2,1,0:T(8,128)(2,1)S(1)}, u32[]{:S(2)}, u32[]{:S(2)}) %collective-permute-start.3) | collective-permute-done | bytes 245792 | tf_op jit(solution)/shard_map/ppermute | solution.py:33
  31.5 0.6 collective-permute-start.4
  32.1 0.2 collective-permute-done.2.right_ref
  32.3 2.8 %collective-permute-start.5 = (bf16[8,32,240]{2,1,0:T(8,128)(2,1)S(1)}, bf16[8,32,240]{2,1,0:T(8,128)(2,1)S(1)}, u32[]{:S(2)}, u32[]{:S(2)}) collective-permute-start(bf16[8,32,240]{2,1,0:T(8,128)(2,1)S(1)} %slice.25), channel_id=1, source_target_pairs={{0,3},{1,0},{2,1},{3,2},{4,7},{5,4},{6,5},{7,6},{8,11},{9,8},{10,9... | collective-permute-start | bytes 368648 | tf_op jit(solution)/shard_map/ppermute | solution.py:33
  35.1 3.6 %collective-permute-done.4.far_low_ref = bf16[8,32,240]{2,1,0:T(8,128)(2,1)S(1)} collective-permute-done((bf16[8,32,240]{2,1,0:T(8,128)(2,1)S(1)}, bf16[8,32,240]{2,1,0:T(8,128)(2,1)S(1)}, u32[]{:S(2)}, u32[]{:S(2)}) %collective-permute-start.4) | collective-permute-done | bytes 122912 | tf_op jit(solution)/shard_map/ppermute | solution.py:33
  38.7 0.0 collective-permute-done.5.far_high_ref
  38.7 0.0 copy-done
  38.7 0.0 copy-done.1
  38.7 0.6 %copy-done.7 = bf16[8,32,240]{2,1,0:T(8,128)(2,1)} copy-done((bf16[8,32,240]{2,1,0:T(8,128)(2,1)}, bf16[8,32,240]{2,1,0:T(8,128)(2,1)S(1)}, u32[]{:S(2)}) %copy-start.7) | copy-done | bytes 122904
  39.3 0.0 copy-done.8
  39.3 6.9 %skill_sums.1 = f32[4,4,32,240]{3,2,1,0:T(8,128)} custom-call(s32[4,32]{1,0:T(4,128)} %bitcast.13, bf16[16,32,240]{2,1,0:T(8,128)(2,1)} %climate.1.own_ref, bf16[16,32,240]{2,1,0:T(8,128)(2,1)} %copy-done.1, bf16[8,32,240]{2,1,0:T(8,128)(2,1)} %copy-done.7, bf16[8,32,240]{2,1,0:T(8,128)(2,1)} %copy-done.8, bf16[16,32,240]{2,1,0:T(8,128)(2,1)} %copy-done, ...), custom_call_target="tpu_custom_call" | custom-call | tf_op jit(solution)/shard_map/skill_sums/pallas_call | solution.py:209
  46.2 1.8 %slice_bitcast_fusion = (f32[4,32,240]{2,1,0:T(8,128)}, f32[4,32,240]{2,1,0:T(8,128)S(1)}, f32[4,32,240]{2,1,0:T(8,128)S(1)}, f32[4,32,240]{2,1,0:T(8,128)S(1)}) fusion(f32[4,4,32,240]{3,2,1,0:T(8,128)} %skill_sums.1), kind=kLoop, calls=%fused_computation | loop fusion | bytes 983040 | tf_op jit(solution)/shard_map/squeeze | solution.py:271
  48.0 3.2 %collective-permute-start.8 = (f32[4,32,240]{2,1,0:T(8,128)S(1)}, f32[4,32,240]{2,1,0:T(8,128)S(1)}, u32[]{:S(2)}, u32[]{:S(2)}) collective-permute-start(f32[4,32,240]{2,1,0:T(8,128)S(1)} %get-tuple-element.7), channel_id=1, source_target_pairs={{0,3},{1,0},{2,1},{3,2},{4,7},{5,4},{6,5},{7,6},{8,11},{9,8},{10,9... | collective-permute-start | bytes 368648 | tf_op jit(solution)/shard_map/ppermute | solution.py:33
  51.2 0.0 collective-permute-start.7
  51.2 0.9 %collective-permute-start.6 = (f32[4,32,240]{2,1,0:T(8,128)S(1)}, f32[4,32,240]{2,1,0:T(8,128)S(1)}, u32[]{:S(2)}, u32[]{:S(2)}) collective-permute-start(f32[4,32,240]{2,1,0:T(8,128)S(1)} %get-tuple-element.9), channel_id=1, source_target_pairs={{0,1},{1,2},{2,3},{3,0},{4,5},{5,6},{6,7},{7,4},{8,9},{9,10},{10,1... | collective-permute-start | bytes 368648 | tf_op jit(solution)/shard_map/ppermute | solution.py:33
  52.0 4.2 %collective-permute-done.8.three_ref = f32[4,32,240]{2,1,0:T(8,128)S(1)} collective-permute-done((f32[4,32,240]{2,1,0:T(8,128)S(1)}, f32[4,32,240]{2,1,0:T(8,128)S(1)}, u32[]{:S(2)}, u32[]{:S(2)}) %collective-permute-start.8) | collective-permute-done | bytes 122912 | tf_op jit(solution)/shard_map/ppermute | solution.py:33
  56.2 2.3 %collective-permute-done.7.two_ref = f32[4,32,240]{2,1,0:T(8,128)S(1)} collective-permute-done((f32[4,32,240]{2,1,0:T(8,128)S(1)}, f32[4,32,240]{2,1,0:T(8,128)S(1)}, u32[]{:S(2)}, u32[]{:S(2)}) %collective-permute-start.7) | collective-permute-done | bytes 122912 | tf_op jit(solution)/shard_map/ppermute | solution.py:33
  58.6 1.1 %collective-permute-done.6.one_ref = f32[4,32,240]{2,1,0:T(8,128)S(1)} collective-permute-done((f32[4,32,240]{2,1,0:T(8,128)S(1)}, f32[4,32,240]{2,1,0:T(8,128)S(1)}, u32[]{:S(2)}, u32[]{:S(2)}) %collective-permute-start.6) | collective-permute-done | bytes 122912 | tf_op jit(solution)/shard_map/ppermute | solution.py:33
  59.7 0.0 copy-done.3
  59.7 0.6 %copy-done.5 = f32[4,32,240]{2,1,0:T(8,128)} copy-done((f32[4,32,240]{2,1,0:T(8,128)}, f32[4,32,240]{2,1,0:T(8,128)S(1)}, u32[]{:S(2)}) %copy-start.5) | copy-done | bytes 122904
  60.3 1.8 %maps.1 = (f32[1,8,4,240]{3,2,1,0:T(4,128)}, f32[1,8,4,240]{3,2,1,0:T(4,128)}) custom-call(f32[128]{0:T(128)} %constant.5.clone.scale_ref, f32[4,32,240]{2,1,0:T(8,128)} %copy-done.5, f32[4,32,240]{2,1,0:T(8,128)} %copy-done.4, f32[4,32,240]{2,1,0:T(8,128)} %copy-done.3, f32[4,32,240]{2,1,0:T(8,128)} %get-tuple-element.6.own_ref), custom_call_target="tpu_custom_call" | custom-call | tf_op jit(solution)/shard_map/maps/pallas_call | solution.py:242
  (12 shorter events, 0.0 us)
Async XLA Ops:
  5.1 12.4 %collective-permute-start.1 = (bf16[16,2,8,240]{3,2,1,0:T(8,128)(2,1)}, bf16[16,2,8,240]{3,2,1,0:T(8,128)(2,1)S(1)}, u32[]{:S(2)}, u32[]{:S(2)}) collective-permute-start(bf16[16,2,8,240]{3,2,1,0:T(8,128)(2,1)} %get-tuple-element.5.down_ref), channel_id=1, source_target_pairs={{4,0},{8,4},{12,8},{16,12},{20,16},{24,20},{28,24},{32,28},{36,32}... | collective-permute-start | bytes 368648 | tf_op jit(solution)/shard_map/ppermute | solution.py:257
  6.4 11.1 %collective-permute-start = (bf16[16,3,8,240]{3,2,1,0:T(8,128)(2,1)}, bf16[16,3,8,240]{3,2,1,0:T(8,128)(2,1)S(1)}, u32[]{:S(2)}, u32[]{:S(2)}) collective-permute-start(bf16[16,3,8,240]{3,2,1,0:T(8,128)(2,1)} %get-tuple-element.4.up_ref), channel_id=1, source_target_pairs={{0,4},{4,8},{8,12},{12,16},{16,20},{20,24},{24,28},{28,32},{32,36}... | collective-permute-start | bytes 552968 | tf_op jit(solution)/shard_map/ppermute | solution.py:256
  17.4 0.6 %copy-start.6 = (bf16[16,2,8,240]{3,2,1,0:T(8,128)(2,1)}, bf16[16,2,8,240]{3,2,1,0:T(8,128)(2,1)S(1)}, u32[]{:S(2)}) copy-start(bf16[16,2,8,240]{3,2,1,0:T(8,128)(2,1)S(1)} %collective-permute-done.1.above_ref) | copy-start | bytes 368644
  18.1 0.7 %copy-start.2 = (bf16[16,3,8,240]{3,2,1,0:T(8,128)(2,1)}, bf16[16,3,8,240]{3,2,1,0:T(8,128)(2,1)S(1)}, u32[]{:S(2)}) copy-start(bf16[16,3,8,240]{3,2,1,0:T(8,128)(2,1)S(1)} %collective-permute-done.below_ref) | copy-start | bytes 552964
  21.5 9.9 %collective-permute-start.3 = (bf16[16,32,240]{2,1,0:T(8,128)(2,1)}, bf16[16,32,240]{2,1,0:T(8,128)(2,1)S(1)}, u32[]{:S(2)}, u32[]{:S(2)}) collective-permute-start(bf16[16,32,240]{2,1,0:T(8,128)(2,1)} %climate.1.own_ref), channel_id=1, source_target_pairs={{0,1},{1,2},{2,3},{3,0},{4,5},{5,6},{6,7},{7,4},{8,9},{9,10},{10,1... | collective-permute-start | bytes 737288 | tf_op jit(solution)/shard_map/ppermute | solution.py:33
  23.1 9.1 %collective-permute-start.2 = (bf16[16,32,240]{2,1,0:T(8,128)(2,1)}, bf16[16,32,240]{2,1,0:T(8,128)(2,1)S(1)}, u32[]{:S(2)}, u32[]{:S(2)}) collective-permute-start(bf16[16,32,240]{2,1,0:T(8,128)(2,1)} %climate.1.own_ref), channel_id=1, source_target_pairs={{0,3},{1,0},{2,1},{3,2},{4,7},{5,4},{6,5},{7,6},{8,11},{9,8},{10,9... | collective-permute-start | bytes 737288 | tf_op jit(solution)/shard_map/ppermute | solution.py:33
  31.5 7.2 %copy-start = (bf16[16,32,240]{2,1,0:T(8,128)(2,1)}, bf16[16,32,240]{2,1,0:T(8,128)(2,1)S(1)}, u32[]{:S(2)}) copy-start(bf16[16,32,240]{2,1,0:T(8,128)(2,1)S(1)} %collective-permute-done.3.left_ref) | copy-start | bytes 737284
  31.5 7.2 %collective-permute-start.4 = (bf16[8,32,240]{2,1,0:T(8,128)(2,1)S(1)}, bf16[8,32,240]{2,1,0:T(8,128)(2,1)S(1)}, u32[]{:S(2)}, u32[]{:S(2)}) collective-permute-start(bf16[8,32,240]{2,1,0:T(8,128)(2,1)S(1)} %slice.24), channel_id=1, source_target_pairs={{0,1},{1,2},{2,3},{3,0},{4,5},{5,6},{6,7},{7,4},{8,9},{9,10},{10,1... | collective-permute-start | bytes 368648 | tf_op jit(solution)/shard_map/ppermute | solution.py:33
  32.2 6.4 %copy-start.1 = (bf16[16,32,240]{2,1,0:T(8,128)(2,1)}, bf16[16,32,240]{2,1,0:T(8,128)(2,1)S(1)}, u32[]{:S(2)}) copy-start(bf16[16,32,240]{2,1,0:T(8,128)(2,1)S(1)} %collective-permute-done.2.right_ref) | copy-start | bytes 737284
  32.3 6.4 %collective-permute-start.5 = (bf16[8,32,240]{2,1,0:T(8,128)(2,1)S(1)}, bf16[8,32,240]{2,1,0:T(8,128)(2,1)S(1)}, u32[]{:S(2)}, u32[]{:S(2)}) collective-permute-start(bf16[8,32,240]{2,1,0:T(8,128)(2,1)S(1)} %slice.25), channel_id=1, source_target_pairs={{0,3},{1,0},{2,1},{3,2},{4,7},{5,4},{6,5},{7,6},{8,11},{9,8},{10,9... | collective-permute-start | bytes 368648 | tf_op jit(solution)/shard_map/ppermute | solution.py:33
  38.7 0.7 %copy-start.7 = (bf16[8,32,240]{2,1,0:T(8,128)(2,1)}, bf16[8,32,240]{2,1,0:T(8,128)(2,1)S(1)}, u32[]{:S(2)}) copy-start(bf16[8,32,240]{2,1,0:T(8,128)(2,1)S(1)} %collective-permute-done.4.far_low_ref) | copy-start | bytes 368644
  38.7 0.7 %copy-start.8 = (bf16[8,32,240]{2,1,0:T(8,128)(2,1)}, bf16[8,32,240]{2,1,0:T(8,128)(2,1)S(1)}, u32[]{:S(2)}) copy-start(bf16[8,32,240]{2,1,0:T(8,128)(2,1)S(1)} %collective-permute-done.5.far_high_ref) | copy-start | bytes 368644
  48.0 8.3 %collective-permute-start.8 = (f32[4,32,240]{2,1,0:T(8,128)S(1)}, f32[4,32,240]{2,1,0:T(8,128)S(1)}, u32[]{:S(2)}, u32[]{:S(2)}) collective-permute-start(f32[4,32,240]{2,1,0:T(8,128)S(1)} %get-tuple-element.7), channel_id=1, source_target_pairs={{0,3},{1,0},{2,1},{3,2},{4,7},{5,4},{6,5},{7,6},{8,11},{9,8},{10,9... | collective-permute-start | bytes 368648 | tf_op jit(solution)/shard_map/ppermute | solution.py:33
  51.2 7.4 %collective-permute-start.7 = (f32[4,32,240]{2,1,0:T(8,128)S(1)}, f32[4,32,240]{2,1,0:T(8,128)S(1)}, u32[]{:S(2)}, u32[]{:S(2)}) collective-permute-start(f32[4,32,240]{2,1,0:T(8,128)S(1)} %get-tuple-element.8), channel_id=1, source_target_pairs={{0,2},{1,3},{2,0},{3,1},{4,6},{5,7},{6,4},{7,5},{8,10},{9,11},{10,... | collective-permute-start | bytes 368648 | tf_op jit(solution)/shard_map/ppermute | solution.py:33
  51.2 8.5 %collective-permute-start.6 = (f32[4,32,240]{2,1,0:T(8,128)S(1)}, f32[4,32,240]{2,1,0:T(8,128)S(1)}, u32[]{:S(2)}, u32[]{:S(2)}) collective-permute-start(f32[4,32,240]{2,1,0:T(8,128)S(1)} %get-tuple-element.9), channel_id=1, source_target_pairs={{0,1},{1,2},{2,3},{3,0},{4,5},{5,6},{6,7},{7,4},{8,9},{9,10},{10,1... | collective-permute-start | bytes 368648 | tf_op jit(solution)/shard_map/ppermute | solution.py:33
  56.2 3.4 %copy-start.3 = (f32[4,32,240]{2,1,0:T(8,128)}, f32[4,32,240]{2,1,0:T(8,128)S(1)}, u32[]{:S(2)}) copy-start(f32[4,32,240]{2,1,0:T(8,128)S(1)} %collective-permute-done.8.three_ref) | copy-start | bytes 368644
  58.6 1.1 %copy-start.4 = (f32[4,32,240]{2,1,0:T(8,128)}, f32[4,32,240]{2,1,0:T(8,128)S(1)}, u32[]{:S(2)}) copy-start(f32[4,32,240]{2,1,0:T(8,128)S(1)} %collective-permute-done.7.two_ref) | copy-start | bytes 368644
  59.7 0.7 %copy-start.5 = (f32[4,32,240]{2,1,0:T(8,128)}, f32[4,32,240]{2,1,0:T(8,128)S(1)}, u32[]{:S(2)}) copy-start(f32[4,32,240]{2,1,0:T(8,128)S(1)} %collective-permute-done.6.one_ref) | copy-start | bytes 368644

commit v2 on v1

--- a/solution.py
+++ b/solution.py
@@ -1,3 +1,4 @@
+import functools
 import math
 
 import jax
@@ -44,54 +45,96 @@
     return (total * (1.0 / FINE)).astype(jnp.bfloat16).reshape(*rows.shape[:-1], DEST_MERIDIANS)
 
 
-def edge_kernel(low_ref, high_ref, table_ref, down_ref, up_ref):
-    table = table_ref[...]
-    up_ref[...] = lon_mean(high_ref[...], table)
-    down_ref[...] = lon_mean(low_ref[...], table)
-
-
-def band_rows(chunk, first, count):
-    sizes = (chunk, count, VARS, SRC_LON)
-    return pl.BlockSpec(tuple(pl.Element(n) for n in sizes), lambda i: (i * chunk, first, 0, 0))
+def params(mebibytes):
+    return pltpu.CompilerParams(vmem_limit_bytes=mebibytes * 1024 * 1024)
+
+
+def cost(microseconds):
+    return pl.CostEstimate(
+        flops=0, bytes_accessed=int(microseconds * 3 * 10**6), transcendentals=0
+    )
+
+
+def edge_kernel(field_ref, table_ref, down_ref, up_ref, low_buf, high_buf, table_buf, sems):
+    parts = low_buf.shape[0]
+    size = BINS // parts
+    load = pltpu.make_async_copy(table_ref, table_buf, sems.at[2 * parts])
+    load.start()
+    copies = []
+    for n in range(parts):
+        some = pl.ds(n * size, size)
+        low = pltpu.make_async_copy(field_ref.at[some, pl.ds(0, DOWN)], low_buf.at[n], sems.at[n])
+        high = pltpu.make_async_copy(
+            field_ref.at[some, pl.ds(BAND - UP, UP)], high_buf.at[n], sems.at[parts + n]
+        )
+        low.start()
+        high.start()
+        copies.append((low, high))
+    load.wait()
+    for n in range(parts):
+        low, high = copies[n]
+        low.wait()
+        down_ref[n * size : (n + 1) * size] = lon_mean(low_buf[n], table_buf[...])
+        high.wait()
+        up_ref[n * size : (n + 1) * size] = lon_mean(high_buf[n], table_buf[...])
 
 
 def edges(field, table):
-    chunk = 4
-    spec = lambda count: pl.BlockSpec(
-        (chunk, count, VARS, DEST_MERIDIANS), lambda i: (i, 0, 0, 0)
-    )
+    parts = 2
+    vmem = pl.BlockSpec(memory_space=pltpu.VMEM)
+    hbm = pl.BlockSpec(memory_space=pl.ANY)
     shape = lambda count: jax.ShapeDtypeStruct((BINS, count, VARS, DEST_MERIDIANS), jnp.bfloat16)
     return pl.pallas_call(
         edge_kernel,
-        grid=(BINS // chunk,),
-        in_specs=[
-            band_rows(chunk, 0, DOWN),
-            band_rows(chunk, BAND - UP, UP),
-            pl.BlockSpec((SRC_LON, DEST_MERIDIANS), lambda i: (0, 0)),
+        in_specs=[hbm, hbm],
+        out_specs=[vmem, vmem],
+        out_shape=[shape(DOWN), shape(UP)],
+        scratch_shapes=[
+            pltpu.VMEM((parts, BINS // parts, DOWN, VARS, SRC_LON), jnp.bfloat16),
+            pltpu.VMEM((parts, BINS // parts, UP, VARS, SRC_LON), jnp.bfloat16),
+            pltpu.VMEM((SRC_LON, DEST_MERIDIANS), jnp.bfloat16),
+            pltpu.SemaphoreType.DMA((2 * parts + 1,)),
         ],
-        out_specs=[spec(DOWN), spec(UP)],
-        out_shape=[shape(DOWN), shape(UP)],
+        compiler_params=params(57),
+        cost_estimate=cost(2),
         name="edge_lon",
-    )(field, field, table)
-
-
-def mid_kernel(rows_ref, table_ref, out_ref):
-    out_ref[...] = lon_mean(rows_ref[...], table_ref[...])
+    )(field, table)
+
+
+def mid_kernel(field_ref, table_ref, out_ref, buf, table_buf, sems):
+    parts = buf.shape[0]
+    size = BINS // parts
+    load = pltpu.make_async_copy(table_ref, table_buf, sems.at[parts])
+    load.start()
+    copies = []
+    for n in range(parts):
+        copy = pltpu.make_async_copy(
+            field_ref.at[pl.ds(n * size, size), pl.ds(DOWN, MID)], buf.at[n], sems.at[n]
+        )
+        copy.start()
+        copies.append(copy)
+    load.wait()
+    for n in range(parts):
+        copies[n].wait()
+        out_ref[n * size : (n + 1) * size] = lon_mean(buf[n], table_buf[...])
 
 
 def middle(field, table):
-    chunk = 2
+    parts = 4
+    hbm = pl.BlockSpec(memory_space=pl.ANY)
     return pl.pallas_call(
         mid_kernel,
-        grid=(BINS // chunk,),
-        in_specs=[
-            band_rows(chunk, DOWN, MID),
-            pl.BlockSpec((SRC_LON, DEST_MERIDIANS), lambda i: (0, 0)),
+        in_specs=[hbm, hbm],
+        out_specs=pl.BlockSpec(memory_space=pltpu.VMEM),
+        out_shape=jax.ShapeDtypeStruct((BINS, MID, VARS, DEST_MERIDIANS), jnp.bfloat16),
+        scratch_shapes=[
+            pltpu.VMEM((parts, BINS // parts, MID, VARS, SRC_LON), jnp.bfloat16),
+            pltpu.VMEM((SRC_LON, DEST_MERIDIANS), jnp.bfloat16),
+            pltpu.SemaphoreType.DMA((parts + 1,)),
         ],
-        out_specs=pl.BlockSpec((chunk, MID, VARS, DEST_MERIDIANS), lambda i: (i, 0, 0, 0)),
-        out_shape=jax.ShapeDtypeStruct((BINS, MID, VARS, DEST_MERIDIANS), jnp.bfloat16),
+        compiler_params=params(54),
+        cost_estimate=cost(4),
         name="mid_lon",
-        cost_estimate=pl.CostEstimate(flops=2 * 10**9, bytes_accessed=8 * 10**6, transcendentals=0),
     )(field, table)
 
 
@@ -151,70 +194,112 @@
         in_specs=[smem] * 3 + [vmem] * 5,
         out_specs=vmem,
         out_shape=jax.ShapeDtypeStruct((BINS, FLAT, DEST_MERIDIANS), jnp.bfloat16),
+        compiler_params=params(8),
+        cost_estimate=cost(2),
         name="climate",
     )(index, extent, count, below, down, mid, up, above)
 
 
-def sums_kernel(
-    bins_ref, own_ref, right_ref, far_low_ref, far_high_ref, left_ref, fore_ref, obs_ref,
-    out_ref, clim_ref,
-):
+def days_kernel(fore_ref, obs_ref, fore_out, obs_out, error_out):
     slot = lax.axis_index("slot")
-    lead = lax.rem(pl.program_id(0) + 1 + slot, SLOTS)
-
-    @pl.when(pl.program_id(0) == 0)
-    def _():
-        half = BINS // 2
-        clim_ref[:BINS] = decode(own_ref[...])
-        clim_ref[BINS : 2 * BINS] = decode(right_ref[...])
-        clim_ref[2 * BINS : 2 * BINS + half] = decode(far_low_ref[...])
-        clim_ref[2 * BINS + half : 3 * BINS] = decode(far_high_ref[...])
-        clim_ref[3 * BINS :] = decode(left_ref[...])
-
-    half = VARS // 2
-    lines = half * TILE
+    for k in range(SLOTS):
+        lead = lax.rem(slot + k, SLOTS)
+
+        def step(d, squared):
+            fore = fore_ref[d, lead].astype(jnp.float32).reshape(FLAT, DEST_MERIDIANS)
+            obs = obs_ref[d, lead].astype(jnp.float32).reshape(FLAT, DEST_MERIDIANS)
+            fore_out[k, d] = fore.astype(jnp.bfloat16)
+            obs_out[k, d] = obs.astype(jnp.bfloat16)
+            error = fore - obs
+            return squared + error * error
+
+        zero = jnp.zeros((FLAT, DEST_MERIDIANS), jnp.float32)
+        error_out[k] = lax.fori_loop(0, DAYS, step, zero, unroll=2)
+
+
+def relaid_days(fore, obs):
+    vmem = pl.BlockSpec(memory_space=pltpu.VMEM)
+    grid = jax.ShapeDtypeStruct((SLOTS, DAYS, FLAT, DEST_MERIDIANS), jnp.bfloat16)
+    return pl.pallas_call(
+        days_kernel,
+        in_specs=[vmem] * 2,
+        out_specs=[vmem] * 3,
+        out_shape=[grid, grid, jax.ShapeDtypeStruct((SLOTS, FLAT, DEST_MERIDIANS), jnp.float32)],
+        compiler_params=params(16),
+        cost_estimate=cost(5),
+        name="days",
+    )(fore, obs)
+
+
+def decode_kernel(own_ref, right_ref, left_ref, near_ref):
+    near_ref[:BINS] = decode(own_ref[...])
+    near_ref[BINS : 2 * BINS] = decode(right_ref[...])
+    near_ref[2 * BINS :] = decode(left_ref[...])
+
+
+def decoded(own, right, left):
+    vmem = pl.BlockSpec(memory_space=pltpu.VMEM)
+    return pl.pallas_call(
+        decode_kernel,
+        in_specs=[vmem] * 3,
+        out_specs=vmem,
+        out_shape=jax.ShapeDtypeStruct((3 * BINS, FLAT, DEST_MERIDIANS), jnp.float32),
+        compiler_params=params(8),
+        cost_estimate=cost(1),
+        name="decode",
+    )(own, right, left)
+
+
+def lead_sums(k, bins_ref, near_ref, far_ref, fore_ref, obs_ref, error_ref, out_ref):
+    slot = lax.axis_index("slot")
+    lead = lax.rem(slot + k, SLOTS)
+    half = FLAT // 2
     for h in range(2):
+        some = slice(h * half, (h + 1) * half)
 
         def step(d, sums):
-            squared, cross, fore_sq, true_sq = sums
-            fore = fore_ref[d, 0, h * half : (h + 1) * half].astype(jnp.float32)
-            fore = fore.reshape(lines, DEST_MERIDIANS)
-            obs = obs_ref[d, 0, h * half : (h + 1) * half].astype(jnp.float32)
-            obs = obs.reshape(lines, DEST_MERIDIANS)
+            cross, fore_sq, true_sq = sums
             wanted = bins_ref[lead, d]
-            spot = (wanted // BINS - slot) % SLOTS * BINS + wanted % BINS
-            clim = clim_ref[spot, h * lines : (h + 1) * lines]
-            error = fore - obs
-            fore_anom = fore - clim
-            true_anom = obs - clim
+            turn = (wanted // BINS - slot) % SLOTS
+            place = wanted % BINS
+            near = jnp.where(turn == 3, 2, jnp.minimum(turn, 1)) * BINS + place
+            clim = jnp.where(turn == 2, far_ref[place, some], near_ref[near, some])
+            fore_anom = fore_ref[k, d, some].astype(jnp.float32) - clim
+            true_anom = obs_ref[k, d, some].astype(jnp.float32) - clim
             return (
-                squared + error * error,
                 cross + fore_anom * true_anom,
                 fore_sq + fore_anom * fore_anom,
                 true_sq + true_anom * true_anom,
             )
 
-        zero = jnp.zeros((lines, DEST_MERIDIANS), jnp.float32)
-        sums = lax.fori_loop(0, DAYS, step, (zero,) * 4, unroll=4)
+        zero = jnp.zeros((half, DEST_MERIDIANS), jnp.float32)
+        sums = lax.fori_loop(0, DAYS, step, (zero,) * 3, unroll=4)
         for n, value in enumerate(sums):
-            out_ref[0, n, h * lines : (h + 1) * lines] = value
-
-
-def skill_sums(bins, own, right, far_low, far_high, left, fore, obs):
-    vmem = pl.BlockSpec(memory_space=pltpu.VMEM)
-    days = pl.BlockSpec(
-        (DAYS, 1, VARS, TILE, DEST_MERIDIANS),
-        lambda i: (0, lax.rem(i + 1 + lax.axis_index("slot"), SLOTS), 0, 0, 0),
-    )
-    return pl.pallas_call(
-        sums_kernel,
-        grid=(SLOTS,),
-        in_specs=[pl.BlockSpec(memory_space=pltpu.SMEM)] + [vmem] * 5 + [days] * 2,
-        out_specs=pl.BlockSpec((1, 4, FLAT, DEST_MERIDIANS), lambda i: (i, 0, 0, 0)),
-        out_shape=jax.ShapeDtypeStruct((SLOTS, 4, FLAT, DEST_MERIDIANS), jnp.float32),
-        scratch_shapes=[pltpu.VMEM((SLOTS * BINS, FLAT, DEST_MERIDIANS), jnp.float32)],
-        name="skill_sums",
-    )(bins, own, right, far_low, far_high, left, fore, obs)
+            out_ref[n + 1, some] = value
+    out_ref[0] = error_ref[k]
+
+
+def first_kernel(
+    k, bins_ref, near_ref, low_ref, high_ref, fore_ref, obs_ref, error_ref, out_ref, far_ref
+):
+    far_ref[: BINS // 2] = decode(low_ref[...])
+    far_ref[BINS // 2 :] = decode(high_ref[...])
+    lead_sums(k, bins_ref, near_ref, far_ref, fore_ref, obs_ref, error_ref, out_ref)
+
+
+def skill_sums(k, bins, near, far, fore, obs, error):
+    vmem = pl.BlockSpec(memory_space=pltpu.VMEM)
+    out = jax.ShapeDtypeStruct((4, FLAT, DEST_MERIDIANS), jnp.float32)
+    clim = jax.ShapeDtypeStruct((BINS, FLAT, DEST_MERIDIANS), jnp.float32)
+    first = len(far) == 2
+    return pl.pallas_call(
+        functools.partial(first_kernel if first else lead_sums, k),
+        in_specs=[pl.BlockSpec(memory_space=pltpu.SMEM)] + [vmem] * (4 + len(far)),
+        out_specs=[vmem, vmem] if first else vmem,
+        out_shape=[out, clim] if first else out,
+        compiler_params=params(16),
+        cost_estimate=cost(1),
+    )(bins, near, *far, fore, obs, error)
 
 
 def maps_kernel(scale_ref, one_ref, two_ref, three_ref, own_ref, rmse_ref, acc_ref):
@@ -244,6 +329,8 @@
         in_specs=[pl.BlockSpec(memory_space=pltpu.SMEM)] + [vmem] * 4,
         out_specs=[vmem] * 2,
         out_shape=[shape] * 2,
+        compiler_params=params(8),
+        cost_estimate=cost(1),
         name="maps",
     )(scale, one, two, three, own)
 
@@ -262,13 +349,15 @@
     half = BINS // 2
     far_low = shifted(left[:half], 1)
     far_high = shifted(right[half:], -1)
-    sums = skill_sums(
-        jnp.transpose(bins), own, right, far_low, far_high, left, prognosis, analysis
-    )
-    two = shifted(sums[1], 2)
-    one = shifted(sums[0], 1)
-    three = shifted(sums[2], 3)
-    return tuple(maps(one, two, three, sums[3]))
+    fore, obs, error = relaid_days(prognosis, analysis)
+    near = decoded(own, right, left)
+    wanted = jnp.transpose(bins)
+    to_two, far = skill_sums(2, wanted, near, (far_low, far_high), fore, obs, error)
+    two = shifted(to_two, 2)
+    one = shifted(skill_sums(1, wanted, near, (far,), fore, obs, error), 1)
+    three = shifted(skill_sums(3, wanted, near, (far,), fore, obs, error), 3)
+    mine = skill_sums(0, wanted, near, (far,), fore, obs, error)
+    return tuple(maps(one, two, three, mine))
 
 
 def solution(mesh):
@@ -281,6 +370,7 @@
         P("slot", None, None, "lat", None),
         P("slot", None, None, "lat", None),
     )
+
     return jax.shard_map(
         body,
         mesh=mesh,

time: 63.1 us -> 51.7 us (0.82)
  the two profiles are of different devices: /device:TPU:0 before, /device:TPU:40 now
where the time goes in v2:
time: 51.7 us; the launch traced here: 51.4 us
  Pallas kernels  21.1 us (41%)
  starting transfers between devices  17.2 us (33%)
  waiting for transfers between devices  11 us (21%)
  local copies, waits for them, and re-layouts  1.31 us (3%)
  between operations  0.86 us (2%)
    ppermute x7, starting transfers between devices, shifted(): lax.ppermute(value, 'slot', [(i, (i + step) % slots) for i in range(slots)])  11.5 us
    ppermute x7, waiting for transfers between devices, shifted(): lax.ppermute(value, 'slot', [(i, (i + step) % slots) for i in range(slots)])  11 us
    pallas_call x1, Pallas kernels, middle(): pl.pallas_call(mid_kernel, in_specs=[hbm, hbm], out_specs=pl.BlockSpec(me...  6.93 us
    pallas_call x4, Pallas kernels, skill_sums(): pl.pallas_call(functools.partial(first_kernel if first else lead_sums, k)...  6.49 us
    ppermute x1, starting transfers between devices, body(): above = lax.ppermute(down, 'lat', [(i + 1, i) for i in range(devices - 1)])  3.77 us
    pallas_call x1, Pallas kernels, edges(): pl.pallas_call(edge_kernel, in_specs=[hbm, hbm], out_specs=[vmem, vmem],...  3.47 us
    ppermute x1, starting transfers between devices, body(): below = lax.ppermute(up, 'lat', [(i, i + 1) for i in range(devices - 1)])  1.92 us
    pallas_call x1, Pallas kernels, relaid_days(): pl.pallas_call(days_kernel, in_specs=[vmem] * 2, out_specs=[vmem] * 3, ou...  1.44 us
  transfers between devices with their start and end apart: 9, of which 4 were waited for; matrix products, arithmetic and copies ran while one was open for 0% of the time, Pallas kernels for 20%

profile of v2, /device:TPU:40, one launch (start us, length us, event | category | flops | bytes accessed | tf_op | source)
XLA Modules:
  0.0 51.4 jit_solution(16163310922429189940)
XLA Ops:
  0.6 3.5 %edge_lon.1 = (bf16[16,2,8,240]{3,2,1,0:T(8,128)(2,1)}, bf16[16,3,8,240]{3,2,1,0:T(8,128)(2,1)}) custom-call(bf16[16,22,8,1440]{3,2,1,0:T(8,128)(2,1)} %bitcast.6, bf16[1440,240]{1,0:T(8,128)(2,1)} %constant.4.clone.table_ref), custom_call_target="tpu_custom_call" | custom-call | bytes 6000000 | tf_op jit(solution)/shard_map/edge_lon/pallas_call | solution.py:87
  4.1 1.9 %collective-permute-start = (bf16[16,3,8,240]{3,2,1,0:T(8,128)(2,1)}, bf16[16,3,8,240]{3,2,1,0:T(8,128)(2,1)S(1)}, u32[]{:S(2)}, u32[]{:S(2)}) collective-permute-start(bf16[16,3,8,240]{3,2,1,0:T(8,128)(2,1)} %get-tuple-element.9.up_ref), channel_id=1, source_target_pairs={{0,4},{4,8},{8,12},{12,16},{16,20},{20,24},{24,28},{28,32},{32,36}... | collective-permute-start | bytes 552968 | tf_op jit(solution)/shard_map/ppermute | solution.py:343
  6.1 0.0 copy-start.6
  6.1 0.0 copy-start.7
  6.1 0.0 copy-start.8
  6.1 3.8 %collective-permute-start.1 = (bf16[16,2,8,240]{3,2,1,0:T(8,128)(2,1)}, bf16[16,2,8,240]{3,2,1,0:T(8,128)(2,1)S(1)}, u32[]{:S(2)}, u32[]{:S(2)}) collective-permute-start(bf16[16,2,8,240]{3,2,1,0:T(8,128)(2,1)} %get-tuple-element.10.down_ref), channel_id=1, source_target_pairs={{4,0},{8,4},{12,8},{16,12},{20,16},{24,20},{28,24},{32,28},{36,32}... | collective-permute-start | bytes 368648 | tf_op jit(solution)/shard_map/ppermute | solution.py:344
  9.9 0.0 copy-start.1
  9.9 0.0 copy-start.2
  9.9 6.9 %mid_lon.1.mid_ref = bf16[16,17,8,240]{3,2,1,0:T(8,128)(2,1)} custom-call(bf16[16,22,8,1440]{3,2,1,0:T(8,128)(2,1)} %bitcast.7, bf16[1440,240]{1,0:T(8,128)(2,1)} %constant.4.clone.table_ref), custom_call_target="tpu_custom_call" | custom-call | bytes 12000000 | tf_op jit(solution)/shard_map/mid_lon/pallas_call | solution.py:125
  16.8 0.0 collective-permute-done.1.above_ref
  16.9 1.2 %copy-done = bf16[16,17,8,240]{3,2,1,0:T(8,128)(2,1)S(1)} copy-done((bf16[16,17,8,240]{3,2,1,0:T(8,128)(2,1)S(1)}, bf16[16,17,8,240]{3,2,1,0:T(8,128)(2,1)}, u32[]{:S(2)}) %copy-start) | copy-done | bytes 1044504
  18.2 1.1 %climate.1.own_ref = bf16[16,32,240]{2,1,0:T(8,128)(2,1)S(1)} custom-call(s32[4,10]{1,0:T(4,128)S(1)} %copy-done.6, f32[4,10]{1,0:T(4,128)S(1)} %copy-done.7, s32[4]{0:T(128)S(1)} %copy-done.8, bf16[16,3,8,240]{3,2,1,0:T(8,128)(2,1)S(1)} %collective-permute-done.below_ref, bf16[16,2,8,240]{3,2,1,0:T(8,128)(2,1)S(1)} %copy-done.4, ...), custom_call_target="tpu_custom_call" | custom-call | bytes 6000000 | tf_op jit(solution)/shard_map/climate/pallas_call | solution.py:192
  19.3 1.6 %collective-permute-start.3 = (bf16[16,32,240]{2,1,0:T(8,128)(2,1)S(1)}, bf16[16,32,240]{2,1,0:T(8,128)(2,1)S(1)}, u32[]{:S(2)}, u32[]{:S(2)}) collective-permute-start(bf16[16,32,240]{2,1,0:T(8,128)(2,1)S(1)} %climate.1.own_ref), channel_id=1, source_target_pairs={{0,1},{1,2},{2,3},{3,0},{4,5},{5,6},{6,7},{7,4},{8,9},{9,10},{10,1... | collective-permute-start | bytes 737288 | tf_op jit(solution)/shard_map/ppermute | solution.py:34
  20.9 1.7 %collective-permute-start.2 = (bf16[16,32,240]{2,1,0:T(8,128)(2,1)S(1)}, bf16[16,32,240]{2,1,0:T(8,128)(2,1)S(1)}, u32[]{:S(2)}, u32[]{:S(2)}) collective-permute-start(bf16[16,32,240]{2,1,0:T(8,128)(2,1)S(1)} %climate.1.own_ref), channel_id=1, source_target_pairs={{0,3},{1,0},{2,1},{3,2},{4,7},{5,4},{6,5},{7,6},{8,11},{9,8},{10,9... | collective-permute-start | bytes 737288 | tf_op jit(solution)/shard_map/ppermute | solution.py:34
  22.6 6.5 %collective-permute-done.3.left_ref = bf16[16,32,240]{2,1,0:T(8,128)(2,1)S(1)} collective-permute-done((bf16[16,32,240]{2,1,0:T(8,128)(2,1)S(1)}, bf16[16,32,240]{2,1,0:T(8,128)(2,1)S(1)}, u32[]{:S(2)}, u32[]{:S(2)}) %collective-permute-start.3) | collective-permute-done | bytes 245792 | tf_op jit(solution)/shard_map/ppermute | solution.py:34
  29.1 0.3 collective-permute-start.4
  29.5 0.0 collective-permute-done.2.right_ref
  29.5 3.0 %collective-permute-start.5 = (bf16[8,32,240]{2,1,0:T(8,128)(2,1)S(1)}, bf16[8,32,240]{2,1,0:T(8,128)(2,1)S(1)}, u32[]{:S(2)}, u32[]{:S(2)}) collective-permute-start(bf16[8,32,240]{2,1,0:T(8,128)(2,1)S(1)} %slice.9), channel_id=1, source_target_pairs={{0,3},{1,0},{2,1},{3,2},{4,7},{5,4},{6,5},{7,6},{8,11},{9,8},{10,9... | collective-permute-start | bytes 368648 | tf_op jit(solution)/shard_map/ppermute | solution.py:34
  32.5 1.4 %days.1 = (bf16[4,32,32,240]{3,2,1,0:T(8,128)(2,1)S(1)}, bf16[4,32,32,240]{3,2,1,0:T(8,128)(2,1)S(1)}, f32[4,32,240]{2,1,0:T(8,128)S(1)}) custom-call(bf16[32,4,8,4,240]{4,3,2,1,0:T(4,128)(2,1)S(1)} %copy-done.1, bf16[32,4,8,4,240]{4,3,2,1,0:T(4,128)(2,1)S(1)} %copy-done.2), custom_call_target="tpu_custom_call" | custom-call | bytes 15000000 | tf_op jit(solution)/shard_map/days/pallas_call | solution.py:223
  34.0 0.0 copy-start.5
  34.0 0.4 decode.1.near_ref
  34.4 1.0 %collective-permute-done.4.low_ref = bf16[8,32,240]{2,1,0:T(8,128)(2,1)S(1)} collective-permute-done((bf16[8,32,240]{2,1,0:T(8,128)(2,1)S(1)}, bf16[8,32,240]{2,1,0:T(8,128)(2,1)S(1)}, u32[]{:S(2)}, u32[]{:S(2)}) %collective-permute-start.4) | collective-permute-done | bytes 122912 | tf_op jit(solution)/shard_map/ppermute | solution.py:34
  35.4 1.7 %shard_map.104 = (f32[4,32,240]{2,1,0:T(8,128)S(1)}, f32[16,32,240]{2,1,0:T(8,128)S(1)}) custom-call(s32[4,32]{1,0:T(4,128)S(1)} %bitcast.2, f32[48,32,240]{2,1,0:T(8,128)S(1)} %decode.1.near_ref, bf16[8,32,240]{2,1,0:T(8,128)(2,1)S(1)} %collective-permute-done.4.low_ref, bf16[8,32,240]{2,1,0:T(8,128)(2,1)S(1)} %collective-permute-done.5.high_ref, ...), custom_call_target="tpu_custom_call" | custom-call | bytes 3000000 | tf_op jit(solution)/shard_map/pallas_call | solution.py:295
  37.1 1.6 %shard_map.106 = f32[4,32,240]{2,1,0:T(8,128)S(1)} custom-call(s32[4,32]{1,0:T(4,128)S(1)} %bitcast.3, f32[48,32,240]{2,1,0:T(8,128)S(1)} %decode.1.near_ref, f32[16,32,240]{2,1,0:T(8,128)S(1)} %get-tuple-element.14.far_ref, bf16[4,32,32,240]{3,2,1,0:T(8,128)(2,1)S(1)} %get-tuple-element.11.fore_ref, bf16[4,32,32,240]{3,2,1,0:T(8,128)(2,1)S(1)} %get-tuple-element.12.obs_ref, ...), custom_call_target="tpu_custom_call" | custom-call | bytes 3000000 | tf_op jit(solution)/shard_map/pallas_call | solution.py:295
  38.7 1.6 %shard_map.105 = f32[4,32,240]{2,1,0:T(8,128)S(1)} custom-call(s32[4,32]{1,0:T(4,128)S(1)} %bitcast.4, f32[48,32,240]{2,1,0:T(8,128)S(1)} %decode.1.near_ref, f32[16,32,240]{2,1,0:T(8,128)S(1)} %get-tuple-element.14.far_ref, bf16[4,32,32,240]{3,2,1,0:T(8,128)(2,1)S(1)} %get-tuple-element.11.fore_ref, bf16[4,32,32,240]{3,2,1,0:T(8,128)(2,1)S(1)} %get-tuple-element.12.obs_ref, ...), custom_call_target="tpu_custom_call" | custom-call | bytes 3000000 | tf_op jit(solution)/shard_map/pallas_call | solution.py:295
  40.3 0.7 %collective-permute-start.6 = (f32[4,32,240]{2,1,0:T(8,128)S(1)}, f32[4,32,240]{2,1,0:T(8,128)S(1)}, u32[]{:S(2)}, u32[]{:S(2)}) collective-permute-start(f32[4,32,240]{2,1,0:T(8,128)S(1)} %shard_map.105), channel_id=1, source_target_pairs={{0,1},{1,2},{2,3},{3,0},{4,5},{5,6},{6,7},{7,4},{8,9},{9,10},{10,1... | collective-permute-start | bytes 368648 | tf_op jit(solution)/shard_map/ppermute | solution.py:34
  41.0 2.8 %collective-permute-start.8 = (f32[4,32,240]{2,1,0:T(8,128)S(1)}, f32[4,32,240]{2,1,0:T(8,128)S(1)}, u32[]{:S(2)}, u32[]{:S(2)}) collective-permute-start(f32[4,32,240]{2,1,0:T(8,128)S(1)} %shard_map.106), channel_id=1, source_target_pairs={{0,3},{1,0},{2,1},{3,2},{4,7},{5,4},{6,5},{7,6},{8,11},{9,8},{10,9... | collective-permute-start | bytes 368648 | tf_op jit(solution)/shard_map/ppermute | solution.py:34
  43.8 1.4 %collective-permute-start.7 = (f32[4,32,240]{2,1,0:T(8,128)S(1)}, f32[4,32,240]{2,1,0:T(8,128)S(1)}, u32[]{:S(2)}, u32[]{:S(2)}) collective-permute-start(f32[4,32,240]{2,1,0:T(8,128)S(1)} %get-tuple-element.15), channel_id=1, source_target_pairs={{0,2},{1,3},{2,0},{3,1},{4,6},{5,7},{6,4},{7,5},{8,10},{9,11},{10,... | collective-permute-start | bytes 368648 | tf_op jit(solution)/shard_map/ppermute | solution.py:34
  45.1 1.6 %shard_map.107.own_ref = f32[4,32,240]{2,1,0:T(8,128)S(1)} custom-call(s32[4,32]{1,0:T(4,128)S(1)} %bitcast.5, f32[48,32,240]{2,1,0:T(8,128)S(1)} %decode.1.near_ref, f32[16,32,240]{2,1,0:T(8,128)S(1)} %get-tuple-element.14.far_ref, bf16[4,32,32,240]{3,2,1,0:T(8,128)(2,1)S(1)} %get-tuple-element.11.fore_ref, ...), custom_call_target="tpu_custom_call" | custom-call | bytes 3000000 | tf_op jit(solution)/shard_map/pallas_call | solution.py:295
  46.7 1.3 %collective-permute-done.6.one_ref = f32[4,32,240]{2,1,0:T(8,128)S(1)} collective-permute-done((f32[4,32,240]{2,1,0:T(8,128)S(1)}, f32[4,32,240]{2,1,0:T(8,128)S(1)}, u32[]{:S(2)}, u32[]{:S(2)}) %collective-permute-start.6) | collective-permute-done | bytes 122912 | tf_op jit(solution)/shard_map/ppermute | solution.py:34
  48.0 2.2 %collective-permute-done.7.two_ref = f32[4,32,240]{2,1,0:T(8,128)S(1)} collective-permute-done((f32[4,32,240]{2,1,0:T(8,128)S(1)}, f32[4,32,240]{2,1,0:T(8,128)S(1)}, u32[]{:S(2)}, u32[]{:S(2)}) %collective-permute-start.7) | collective-permute-done | bytes 122912 | tf_op jit(solution)/shard_map/ppermute | solution.py:34
  50.2 1.2 %maps.1 = (f32[1,8,4,240]{3,2,1,0:T(4,128)}, f32[1,8,4,240]{3,2,1,0:T(4,128)}) custom-call(f32[128]{0:T(128)S(1)} %copy-done.9, f32[4,32,240]{2,1,0:T(8,128)S(1)} %collective-permute-done.6.one_ref, f32[4,32,240]{2,1,0:T(8,128)S(1)} %collective-permute-done.7.two_ref, f32[4,32,240]{2,1,0:T(8,128)S(1)} %collective-permute-done.8.three_ref, ...), custom_call_target="tpu_custom_call" | custom-call | bytes 3000000 | tf_op jit(solution)/shard_map/maps/pallas_call | solution.py:327
  (18 shorter events, 0.1 us)
Async XLA Ops:
  4.1 12.7 %collective-permute-start = (bf16[16,3,8,240]{3,2,1,0:T(8,128)(2,1)}, bf16[16,3,8,240]{3,2,1,0:T(8,128)(2,1)S(1)}, u32[]{:S(2)}, u32[]{:S(2)}) collective-permute-start(bf16[16,3,8,240]{3,2,1,0:T(8,128)(2,1)} %get-tuple-element.9.up_ref), channel_id=1, source_target_pairs={{0,4},{4,8},{8,12},{12,16},{16,20},{20,24},{24,28},{28,32},{32,36}... | collective-permute-start | bytes 552968 | tf_op jit(solution)/shard_map/ppermute | solution.py:343
  6.0 10.8 %copy-start.3 = (bf16[16,3,8,240]{3,2,1,0:T(8,128)(2,1)S(1)}, bf16[16,3,8,240]{3,2,1,0:T(8,128)(2,1)}, u32[]{:S(2)}) copy-start(bf16[16,3,8,240]{3,2,1,0:T(8,128)(2,1)} %get-tuple-element.9.up_ref) | copy-start | bytes 552964
  6.0 10.8 %copy-start.4 = (bf16[16,2,8,240]{3,2,1,0:T(8,128)(2,1)S(1)}, bf16[16,2,8,240]{3,2,1,0:T(8,128)(2,1)}, u32[]{:S(2)}) copy-start(bf16[16,2,8,240]{3,2,1,0:T(8,128)(2,1)} %get-tuple-element.10.down_ref) | copy-start | bytes 368644
  6.1 10.8 %copy-start.6 = (s32[4,10]{1,0:T(4,128)S(1)}, s32[4,10]{1,0:T(4,128)}, u32[]{:S(2)}) copy-start(s32[4,10]{1,0:T(4,128)} %index_ref.1) | copy-start | bytes 484
  6.1 10.8 %copy-start.7 = (f32[4,10]{1,0:T(4,128)S(1)}, f32[4,10]{1,0:T(4,128)}, u32[]{:S(2)}) copy-start(f32[4,10]{1,0:T(4,128)} %extent_ref.1) | copy-start | bytes 484
  6.1 10.8 %copy-start.8 = (s32[4]{0:T(128)S(1)}, s32[4]{0:T(128)}, u32[]{:S(2)}) copy-start(s32[4]{0:T(128)} %count_ref.1) | copy-start | bytes 52
  6.1 10.7 %collective-permute-start.1 = (bf16[16,2,8,240]{3,2,1,0:T(8,128)(2,1)}, bf16[16,2,8,240]{3,2,1,0:T(8,128)(2,1)S(1)}, u32[]{:S(2)}, u32[]{:S(2)}) collective-permute-start(bf16[16,2,8,240]{3,2,1,0:T(8,128)(2,1)} %get-tuple-element.10.down_ref), channel_id=1, source_target_pairs={{4,0},{8,4},{12,8},{16,12},{20,16},{24,20},{28,24},{32,28},{36,32}... | collective-permute-start | bytes 368648 | tf_op jit(solution)/shard_map/ppermute | solution.py:344
  9.9 22.6 %copy-start.1 = (bf16[32,4,8,4,240]{4,3,2,1,0:T(4,128)(2,1)S(1)}, bf16[32,4,8,4,240]{4,3,2,1,0:T(4,128)(2,1)}, u32[]{:S(2)}) copy-start(bf16[32,4,8,4,240]{4,3,2,1,0:T(4,128)(2,1)} %fore_ref.1) | copy-start | bytes 5898244
  9.9 22.6 %copy-start.2 = (bf16[32,4,8,4,240]{4,3,2,1,0:T(4,128)(2,1)S(1)}, bf16[32,4,8,4,240]{4,3,2,1,0:T(4,128)(2,1)}, u32[]{:S(2)}) copy-start(bf16[32,4,8,4,240]{4,3,2,1,0:T(4,128)(2,1)} %obs_ref.1) | copy-start | bytes 5898244
  16.9 1.2 %copy-start = (bf16[16,17,8,240]{3,2,1,0:T(8,128)(2,1)S(1)}, bf16[16,17,8,240]{3,2,1,0:T(8,128)(2,1)}, u32[]{:S(2)}) copy-start(bf16[16,17,8,240]{3,2,1,0:T(8,128)(2,1)} %mid_lon.1.mid_ref) | copy-start | bytes 3133444
  19.3 9.8 %collective-permute-start.3 = (bf16[16,32,240]{2,1,0:T(8,128)(2,1)S(1)}, bf16[16,32,240]{2,1,0:T(8,128)(2,1)S(1)}, u32[]{:S(2)}, u32[]{:S(2)}) collective-permute-start(bf16[16,32,240]{2,1,0:T(8,128)(2,1)S(1)} %climate.1.own_ref), channel_id=1, source_target_pairs={{0,1},{1,2},{2,3},{3,0},{4,5},{5,6},{6,7},{7,4},{8,9},{9,10},{10,1... | collective-permute-start | bytes 737288 | tf_op jit(solution)/shard_map/ppermute | solution.py:34
  20.9 8.6 %collective-permute-start.2 = (bf16[16,32,240]{2,1,0:T(8,128)(2,1)S(1)}, bf16[16,32,240]{2,1,0:T(8,128)(2,1)S(1)}, u32[]{:S(2)}, u32[]{:S(2)}) collective-permute-start(bf16[16,32,240]{2,1,0:T(8,128)(2,1)S(1)} %climate.1.own_ref), channel_id=1, source_target_pairs={{0,3},{1,0},{2,1},{3,2},{4,7},{5,4},{6,5},{7,6},{8,11},{9,8},{10,9... | collective-permute-start | bytes 737288 | tf_op jit(solution)/shard_map/ppermute | solution.py:34
  29.1 6.2 %collective-permute-start.4 = (bf16[8,32,240]{2,1,0:T(8,128)(2,1)S(1)}, bf16[8,32,240]{2,1,0:T(8,128)(2,1)S(1)}, u32[]{:S(2)}, u32[]{:S(2)}) collective-permute-start(bf16[8,32,240]{2,1,0:T(8,128)(2,1)S(1)} %slice.8), channel_id=1, source_target_pairs={{0,1},{1,2},{2,3},{3,0},{4,5},{5,6},{6,7},{7,4},{8,9},{9,10},{10,1... | collective-permute-start | bytes 368648 | tf_op jit(solution)/shard_map/ppermute | solution.py:34
  29.5 5.9 %collective-permute-start.5 = (bf16[8,32,240]{2,1,0:T(8,128)(2,1)S(1)}, bf16[8,32,240]{2,1,0:T(8,128)(2,1)S(1)}, u32[]{:S(2)}, u32[]{:S(2)}) collective-permute-start(bf16[8,32,240]{2,1,0:T(8,128)(2,1)S(1)} %slice.9), channel_id=1, source_target_pairs={{0,3},{1,0},{2,1},{3,2},{4,7},{5,4},{6,5},{7,6},{8,11},{9,8},{10,9... | collective-permute-start | bytes 368648 | tf_op jit(solution)/shard_map/ppermute | solution.py:34
  34.0 1.4 %copy-start.5 = (s32[32,4]{0,1:T(4,128)S(1)}, s32[32,4]{0,1:T(4,128)}, u32[]{:S(2)}) copy-start(s32[32,4]{0,1:T(4,128)} %param.13) | copy-start | bytes 1540
  40.3 7.7 %collective-permute-start.6 = (f32[4,32,240]{2,1,0:T(8,128)S(1)}, f32[4,32,240]{2,1,0:T(8,128)S(1)}, u32[]{:S(2)}, u32[]{:S(2)}) collective-permute-start(f32[4,32,240]{2,1,0:T(8,128)S(1)} %shard_map.105), channel_id=1, source_target_pairs={{0,1},{1,2},{2,3},{3,0},{4,5},{5,6},{6,7},{7,4},{8,9},{9,10},{10,1... | collective-permute-start | bytes 368648 | tf_op jit(solution)/shard_map/ppermute | solution.py:34
  41.0 7.0 %collective-permute-start.8 = (f32[4,32,240]{2,1,0:T(8,128)S(1)}, f32[4,32,240]{2,1,0:T(8,128)S(1)}, u32[]{:S(2)}, u32[]{:S(2)}) collective-permute-start(f32[4,32,240]{2,1,0:T(8,128)S(1)} %shard_map.106), channel_id=1, source_target_pairs={{0,3},{1,0},{2,1},{3,2},{4,7},{5,4},{6,5},{7,6},{8,11},{9,8},{10,9... | collective-permute-start | bytes 368648 | tf_op jit(solution)/shard_map/ppermute | solution.py:34
  43.8 6.5 %copy-start.9 = (f32[128]{0:T(128)S(1)}, f32[128]{0:T(128)}, u32[]{:S(2)}) copy-start(f32[128]{0:T(128)} %constant.5.clone.scale_ref) | copy-start | bytes 1540
  43.8 6.5 %collective-permute-start.7 = (f32[4,32,240]{2,1,0:T(8,128)S(1)}, f32[4,32,240]{2,1,0:T(8,128)S(1)}, u32[]{:S(2)}, u32[]{:S(2)}) collective-permute-start(f32[4,32,240]{2,1,0:T(8,128)S(1)} %get-tuple-element.15), channel_id=1, source_target_pairs={{0,2},{1,3},{2,0},{3,1},{4,6},{5,7},{6,4},{7,5},{8,10},{9,11},{10,... | collective-permute-start | bytes 368648 | tf_op jit(solution)/shard_map/ppermute | solution.py:34

commit v3 on v2

v3 whole, which is shorter than its diff:
```python
import functools
import math

import jax
import jax.numpy as jnp
import numpy as np
from jax import lax
from jax.experimental import pallas as pl
from jax.experimental.pallas import tpu as pltpu
from jax.sharding import PartitionSpec as P

SRC_LON = 1440
DEST_PARALLELS = 128
DEST_MERIDIANS = 240
FINE = SRC_LON // DEST_MERIDIANS
VARS = 8
BAND = 22
TILE = 4
OVER = 10
EDGE = 3
ROWS = BAND + 2 * EDGE
BINS = 16
HALF = BINS // 2
DAYS = 32
SLOTS = 4
FLAT = VARS * TILE
LON_LIMIT = 52
CODE_RATE = 10.0
CODE_BASE = 120.0


def shifted(value, step):
    slots = lax.axis_size("slot")
    return lax.ppermute(value, "slot", [(i, (i + step) % slots) for i in range(slots)])


def fill_table(table_ref):
    lines = 96
    line = lax.broadcasted_iota(jnp.int32, (lines, DEST_MERIDIANS), 0)
    start = FINE * lax.broadcasted_iota(jnp.int32, (lines, DEST_MERIDIANS), 1)
    for first in range(0, SRC_LON, lines):
        place = line + first - start
        inside = (place >= 0) & (place < FINE)
        table_ref[first : first + lines] = jnp.where(inside, 1.0, 0.0).astype(jnp.bfloat16)


def lon_mean(rows, table):
    flat = rows.reshape(-1, SRC_LON)
    total = jnp.dot(flat, table, preferred_element_type=jnp.float32)
    return (total * (1.0 / FINE)).astype(jnp.bfloat16).reshape(*rows.shape[:-1], DEST_MERIDIANS)


def params(mebibytes):
    return pltpu.CompilerParams(vmem_limit_bytes=mebibytes * 1024 * 1024)


def cost(microseconds):
    return pl.CostEstimate(
        flops=0, bytes_accessed=int(microseconds * 3 * 10**6), transcendentals=0
    )


def lon_kernel(field_ref, own_ref, cross_ref, inner_ref, buf, table_buf, sems):
    parts = sems.shape[0]
    size = BINS // parts
    odd = lax.rem(lax.axis_index("lat"), 2)
    cross_first = odd * (BAND - EDGE)
    inner_first = (1 - odd) * (BAND - EDGE)
    copies = []
    for n in range(parts):
        some = pl.ds(n * size, size)
        copy = pltpu.make_async_copy(field_ref.at[some], buf.at[some], sems.at[n])
        copy.start()
        copies.append(copy)
    fill_table(table_buf)
    for s in range(BINS):
        if s % size == 0:
            copies[s // size].wait()
        own_ref[s] = lon_mean(buf[s], table_buf[...])
        cross_ref[s] = own_ref[s, pl.ds(cross_first, EDGE)]
        inner_ref[s] = own_ref[s, pl.ds(inner_first, EDGE)]


def lon_rows(field):
    parts = 4
    hbm = pl.BlockSpec(memory_space=pl.ANY)
    vmem = pl.BlockSpec(memory_space=pltpu.VMEM)
    shape = lambda count: jax.ShapeDtypeStruct((BINS, count, VARS, DEST_MERIDIANS), jnp.bfloat16)
    return pl.pallas_call(
        lon_kernel,
        in_specs=[hbm],
        out_specs=[vmem] * 3,
        out_shape=[shape(BAND), shape(EDGE), shape(EDGE)],
        scratch_shapes=[
            pltpu.VMEM((BINS, BAND, VARS, SRC_LON), jnp.bfloat16),
            pltpu.VMEM((SRC_LON, DEST_MERIDIANS), jnp.bfloat16),
            pltpu.SemaphoreType.DMA((parts,)),
        ],
        compiler_params=params(LON_LIMIT),
        cost_estimate=cost(6),
        name="lon_rows",
    )(field)


def encode(value):
    size = jnp.exp2(CODE_RATE * jnp.abs(value) - CODE_BASE)
    return jnp.where(value < 0, -size, size).astype(jnp.bfloat16)


def decode(code):
    wide = code.astype(jnp.float32)
    size = (jnp.log2(jnp.abs(wide)) + CODE_BASE) * (1.0 / CODE_RATE)
    return jnp.where(wide < 0, -size, size)


def weight_matrix(index_ref, extent_ref, count_ref):
    lat = lax.axis_index("lat")
    odd = lax.rem(lat, 2) == 1
    line = lax.broadcasted_iota(jnp.int32, (FLAT, ROWS * VARS), 0)
    lane = lax.broadcasted_iota(jnp.int32, (FLAT, ROWS * VARS), 1)
    place = jnp.where(line // TILE == lane % VARS, lane // VARS, -1)
    dense = jnp.zeros((FLAT, ROWS * VARS), jnp.float32)
    sums = jnp.ones((FLAT, ROWS * VARS), jnp.float32)
    for t in range(TILE):
        here = line % TILE == t
        spot = jnp.where(here, place, -1)
        total = jnp.float32(0.0)
        for k in range(OVER):
            value = jnp.where(k < count_ref[t], extent_ref[t, k], jnp.float32(0.0))
            total = total + value
            row = index_ref[t, k] - lat * BAND
            beyond = jnp.where(row >= BAND, row - BAND - EDGE, row)
            turned = jnp.where(row < 0, row + BAND + EDGE, beyond)
            column = jnp.where(odd, turned, row) + EDGE
            dense = dense + jnp.where(spot == column, value, 0.0)
        sums = jnp.where(here, total, sums)
    dense = dense / sums
    high = dense.astype(jnp.bfloat16)
    rest = dense - high.astype(jnp.float32)
    middle_part = rest.astype(jnp.bfloat16)
    low = (rest - middle_part.astype(jnp.float32)).astype(jnp.bfloat16)
    return jnp.concatenate([high, middle_part, low], axis=0)


def climate_kernel(
    index_ref, extent_ref, count_ref, cross_ref, own_ref, inner_ref, low_ref, high_ref
):
    weights = weight_matrix(index_ref, extent_ref, count_ref)
    for s in range(BINS):
        rows = jnp.concatenate([cross_ref[s], own_ref[s], inner_ref[s]], axis=0)
        rows = rows.reshape(ROWS * VARS, DEST_MERIDIANS)
        parts = jnp.dot(weights, rows, preferred_element_type=jnp.float32)
        value = parts[:FLAT] + parts[FLAT : 2 * FLAT] + parts[2 * FLAT :]
        out_ref = low_ref if s < HALF else high_ref
        out_ref[s % HALF] = encode(value)


def climate_code(index, extent, count, cross, own, inner):
    smem = pl.BlockSpec(memory_space=pltpu.SMEM)
    vmem = pl.BlockSpec(memory_space=pltpu.VMEM)
    return pl.pallas_call(
        climate_kernel,
        in_specs=[smem] * 3 + [vmem] * 3,
        out_specs=[vmem] * 2,
        out_shape=[jax.ShapeDtypeStruct((HALF, FLAT, DEST_MERIDIANS), jnp.bfloat16)] * 2,
        compiler_params=params(8),
        cost_estimate=cost(2),
        name="climate",
    )(index, extent, count, cross, own, inner)


def days_kernel(fore_ref, obs_ref, fore_out, obs_out, error_out):
    slot = lax.axis_index("slot")
    for k in range(SLOTS):
        lead = lax.rem(slot + k, SLOTS)

        def step(d, squared):
            fore = fore_ref[d, lead].astype(jnp.float32).reshape(FLAT, DEST_MERIDIANS)
            obs = obs_ref[d, lead].astype(jnp.float32).reshape(FLAT, DEST_MERIDIANS)
            fore_out[k, d] = fore.astype(jnp.bfloat16)
            obs_out[k, d] = obs.astype(jnp.bfloat16)
            error = fore - obs
            return squared + error * error

        zero = jnp.zeros((FLAT, DEST_MERIDIANS), jnp.float32)
        error_out[k] = lax.fori_loop(0, DAYS, step, zero, unroll=2)


def relaid_days(fore, obs):
    vmem = pl.BlockSpec(memory_space=pltpu.VMEM)
    grid = jax.ShapeDtypeStruct((SLOTS, DAYS, FLAT, DEST_MERIDIANS), jnp.bfloat16)
    return pl.pallas_call(
        days_kernel,
        in_specs=[vmem] * 2,
        out_specs=[vmem] * 3,
        out_shape=[grid, grid, jax.ShapeDtypeStruct((SLOTS, FLAT, DEST_MERIDIANS), jnp.float32)],
        compiler_params=params(16),
        cost_estimate=cost(5),
        name="days",
    )(fore, obs)


def decode_kernel(*refs):
    near_ref = refs[-1]
    for n, code_ref in enumerate(refs[:-1]):
        near_ref[n * HALF : (n + 1) * HALF] = decode(code_ref[...])


def decoded(*codes):
    vmem = pl.BlockSpec(memory_space=pltpu.VMEM)
    return pl.pallas_call(
        decode_kernel,
        in_specs=[vmem] * len(codes),
        out_specs=vmem,
        out_shape=jax.ShapeDtypeStruct((len(codes) * HALF, FLAT, DEST_MERIDIANS), jnp.float32),
        compiler_params=params(8),
        cost_estimate=cost(1),
        name="decode",
    )(*codes)


def lead_sums(k, bins_ref, clim_ref, fore_ref, obs_ref, error_ref, out_ref):
    slot = lax.axis_index("slot")
    lead = lax.rem(slot + k, SLOTS)
    first = slot * BINS
    half = FLAT // 2
    for h in range(2):
        some = slice(h * half, (h + 1) * half)

        def step(d, sums):
            cross, fore_sq, true_sq = sums
            clim = clim_ref[(bins_ref[lead, d] - first) & (SLOTS * BINS - 1), some]
            fore_anom = fore_ref[k, d, some].astype(jnp.float32) - clim
            true_anom = obs_ref[k, d, some].astype(jnp.float32) - clim
            return (
                cross + fore_anom * true_anom,
                fore_sq + fore_anom * fore_anom,
                true_sq + true_anom * true_anom,
            )

        zero = jnp.zeros((half, DEST_MERIDIANS), jnp.float32)
        sums = lax.fori_loop(0, DAYS, step, (zero,) * 3, unroll=4)
        for n, value in enumerate(sums):
            out_ref[n + 1, some] = value
    out_ref[0] = error_ref[k]


def first_kernel(
    k, bins_ref, near_ref, low_ref, high_ref, fore_ref, obs_ref, error_ref, out_ref, clim_ref
):
    clim_ref[: 2 * BINS] = near_ref[: 2 * BINS]
    clim_ref[3 * BINS :] = near_ref[2 * BINS :]
    clim_ref[2 * BINS : 2 * BINS + HALF] = decode(low_ref[...])
    clim_ref[2 * BINS + HALF : 3 * BINS] = decode(high_ref[...])
    lead_sums(k, bins_ref, clim_ref, fore_ref, obs_ref, error_ref, out_ref)


def skill_sums(k, bins, clim, fore, obs, error):
    vmem = pl.BlockSpec(memory_space=pltpu.VMEM)
    out = jax.ShapeDtypeStruct((4, FLAT, DEST_MERIDIANS), jnp.float32)
    whole = jax.ShapeDtypeStruct((SLOTS * BINS, FLAT, DEST_MERIDIANS), jnp.float32)
    first = len(clim) > 1
    return pl.pallas_call(
        functools.partial(first_kernel if first else lead_sums, k),
        in_specs=[pl.BlockSpec(memory_space=pltpu.SMEM)] + [vmem] * (3 + len(clim)),
        out_specs=[vmem, vmem] if first else vmem,
        out_shape=[out, whole] if first else out,
        compiler_params=params(16),
        cost_estimate=cost(1),
    )(bins, *clim, fore, obs, error)


def maps_kernel(scale_ref, one_ref, two_ref, three_ref, own_ref, rmse_ref, acc_ref):
    lat = lax.axis_index("lat")
    total = own_ref[...] + one_ref[...] + two_ref[...] + three_ref[...]
    line = lax.broadcasted_iota(jnp.int32, (FLAT, DEST_MERIDIANS), 0)
    scale = jnp.zeros((FLAT, DEST_MERIDIANS), jnp.float32)
    for t in range(TILE):
        scale = jnp.where(line % TILE == t, scale_ref[lat * TILE + t], scale)
    days = DAYS * SLOTS
    rmse = jnp.sqrt(scale * total[0] / days)
    acc = total[1] / jnp.sqrt(total[2] * total[3] + 1e-06)
    rmse_ref[0] = rmse.reshape(VARS, TILE, DEST_MERIDIANS)
    acc_ref[0] = acc.reshape(VARS, TILE, DEST_MERIDIANS)


def maps(one, two, three, own):
    phi = (np.arange(DEST_PARALLELS, dtype=np.float32) + np.float32(0.5)) * np.float32(
        math.pi / DEST_PARALLELS
    ) - np.float32(0.5 * math.pi)
    cosine = np.cos(phi).astype(np.float32)
    scale = jnp.asarray(cosine / cosine.mean(dtype=np.float32))
    vmem = pl.BlockSpec(memory_space=pltpu.VMEM)
    shape = jax.ShapeDtypeStruct((1, VARS, TILE, DEST_MERIDIANS), jnp.float32)
    return pl.pallas_call(
        maps_kernel,
        in_specs=[pl.BlockSpec(memory_space=pltpu.SMEM)] + [vmem] * 4,
        out_specs=[vmem] * 2,
        out_shape=[shape] * 2,
        compiler_params=params(8),
        cost_estimate=cost(1),
        name="maps",
    )(scale, one, two, three, own)


def body(normals, index, extent, count, bins, prognosis, analysis):
    field = jnp.transpose(normals, (0, 2, 1, 3))
    own, cross_edge, inner_edge = lon_rows(field)
    devices = lax.axis_size("lat")
    meets = [(i, i + 1) for i in range(1, devices - 1, 2)]
    meets += [(j, i) for i, j in meets]
    cross = lax.ppermute(cross_edge, "lat", meets)
    inner = lax.ppermute(inner_edge, "lat", [(i, i ^ 1) for i in range(devices)])
    fore, obs, error = relaid_days(prognosis, analysis)
    low, high = climate_code(index, extent, count, cross, own, inner)
    left_low = shifted(low, 1)
    right_high = shifted(high, -1)
    left_high = shifted(high, 1)
    right_low = shifted(low, -1)
    far_low = shifted(left_low, 1)
    far_high = shifted(right_high, -1)
    near = decoded(low, high, right_low, right_high, left_low, left_high)
    wanted = jnp.transpose(bins)
    to_two, clim = skill_sums(2, wanted, (near, far_low, far_high), fore, obs, error)
    two = shifted(to_two, 2)
    one = shifted(skill_sums(1, wanted, (clim,), fore, obs, error), 1)
    three = shifted(skill_sums(3, wanted, (clim,), fore, obs, error), 3)
    mine = skill_sums(0, wanted, (clim,), fore, obs, error)
    return tuple(maps(one, two, three, mine))


def solution(mesh):
    placed = (
        P("slot", None, "lat", None),
        P("lat", None),
        P("lat", None),
        P("lat"),
        P("slot", None),
        P("slot", None, None, "lat", None),
        P("slot", None, None, "lat", None),
    )

    return jax.shard_map(
        body,
        mesh=mesh,
        in_specs=placed,
        out_specs=(P("slot", None, "lat", None), P("slot", None, "lat", None)),
        check_vma=False,
    )
```

time: 51.7 us -> 43.7 us (0.85)
  the two profiles are of different devices: /device:TPU:40 before, /device:TPU:112 now
where the time goes in v3:
time: 43.7 us; the launch traced here: 43.6 us
  waiting for transfers between devices  15 us (34%)
  starting transfers between devices  14.4 us (33%)
  Pallas kernels  13.4 us (31%)
  between operations  0.79 us (2%)
    ppermute x9, starting transfers between devices, shifted(): lax.ppermute(value, 'slot', [(i, (i + step) % slots) for i in range(slots)])  12.4 us
    ppermute x9, waiting for transfers between devices, shifted(): lax.ppermute(value, 'slot', [(i, (i + step) % slots) for i in range(slots)])  10 us
    ppermute x1, waiting for transfers between devices, body(): cross = lax.ppermute(cross_edge, 'lat', meets)  4.96 us
    pallas_call x1, Pallas kernels, lon_rows(): pl.pallas_call(lon_kernel, in_specs=[hbm], out_specs=[vmem] * 3, out_shap...  4.78 us
    pallas_call x4, Pallas kernels, skill_sums(): pl.pallas_call(functools.partial(first_kernel if first else lead_sums, k)...  4.32 us
    ppermute x1, starting transfers between devices, body(): cross = lax.ppermute(cross_edge, 'lat', meets)  1.92 us
    pallas_call x1, Pallas kernels, relaid_days(): pl.pallas_call(days_kernel, in_specs=[vmem] * 2, out_specs=[vmem] * 3, ou...  1.44 us
    pallas_call x1, Pallas kernels, maps(): pl.pallas_call(maps_kernel, in_specs=[pl.BlockSpec(memory_space=pltpu.SME...  1.21 us
  transfers between devices with their start and end apart: 11, of which 8 were waited for; matrix products, arithmetic and copies ran while one was open for 0% of the time, Pallas kernels for 7%

profile of v3, /device:TPU:112, one launch (start us, length us, event | category | flops | bytes accessed | tf_op | source)
XLA Modules:
  0.0 43.6 jit_solution(10026776672963607712)
XLA Ops:
  0.7 4.8 %lon_rows.1 = (bf16[16,22,8,240]{3,2,1,0:T(8,128)(2,1)S(1)}, bf16[16,3,8,240]{3,2,1,0:T(8,128)(2,1)S(1)}, bf16[16,3,8,240]{3,2,1,0:T(8,128)(2,1)S(1)}) custom-call(bf16[16,22,8,1440]{3,2,1,0:T(8,128)(2,1)} %bitcast.6), custom_call_target="tpu_custom_call" | custom-call | bytes 18000000 | tf_op jit(solution)/shard_map/lon_rows/pallas_call | solution.py:89
  5.5 1.9 %collective-permute-start = (bf16[16,3,8,240]{3,2,1,0:T(8,128)(2,1)S(1)}, bf16[16,3,8,240]{3,2,1,0:T(8,128)(2,1)S(1)}, u32[]{:S(2)}, u32[]{:S(2)}) collective-permute-start(bf16[16,3,8,240]{3,2,1,0:T(8,128)(2,1)S(1)} %get-tuple-element.12), channel_id=1, source_target_pairs={{4,8},{12,16},{20,24},{28,32},{36,40},{44,48},{52,56},{60,64},{68,... | collective-permute-start | bytes 552968 | tf_op jit(solution)/shard_map/ppermute | solution.py:312
  7.4 0.1 collective-permute-start.1
  7.5 5.0 %collective-permute-done.cross_ref = bf16[16,3,8,240]{3,2,1,0:T(8,128)(2,1)S(1)} collective-permute-done((bf16[16,3,8,240]{3,2,1,0:T(8,128)(2,1)S(1)}, bf16[16,3,8,240]{3,2,1,0:T(8,128)(2,1)S(1)}, u32[]{:S(2)}, u32[]{:S(2)}) %collective-permute-start) | collective-permute-done | bytes 184352 | tf_op jit(solution)/shard_map/ppermute | solution.py:312
  12.5 0.0 collective-permute-done.1.inner_ref
  12.5 1.2 %climate.1 = (bf16[8,32,240]{2,1,0:T(8,128)(2,1)S(1)}, bf16[8,32,240]{2,1,0:T(8,128)(2,1)S(1)}) custom-call(s32[4,10]{1,0:T(4,128)S(1)} %copy-done.3, f32[4,10]{1,0:T(4,128)S(1)} %copy-done.4, s32[4]{0:T(128)S(1)} %copy-done.6, bf16[16,3,8,240]{3,2,1,0:T(8,128)(2,1)S(1)} %collective-permute-done.cross_ref, ...), custom_call_target="tpu_custom_call" | custom-call | bytes 6000000 | tf_op jit(solution)/shard_map/climate/pallas_call | solution.py:161
  13.7 1.6 %collective-permute-start.4 = (bf16[8,32,240]{2,1,0:T(8,128)(2,1)S(1)}, bf16[8,32,240]{2,1,0:T(8,128)(2,1)S(1)}, u32[]{:S(2)}, u32[]{:S(2)}) collective-permute-start(bf16[8,32,240]{2,1,0:T(8,128)(2,1)S(1)} %get-tuple-element.15.refs_0_), channel_id=1, source_target_pairs={{0,1},{1,2},{2,3},{3,0},{4,5},{5,6},{6,7},{7,4},{8,9},{9,10},{10,1... | collective-permute-start | bytes 368648 | tf_op jit(solution)/shard_map/ppermute | solution.py:34
  15.3 1.7 %collective-permute-start.3 = (bf16[8,32,240]{2,1,0:T(8,128)(2,1)S(1)}, bf16[8,32,240]{2,1,0:T(8,128)(2,1)S(1)}, u32[]{:S(2)}, u32[]{:S(2)}) collective-permute-start(bf16[8,32,240]{2,1,0:T(8,128)(2,1)S(1)} %get-tuple-element.16.refs_1_), channel_id=1, source_target_pairs={{0,3},{1,0},{2,1},{3,2},{4,7},{5,4},{6,5},{7,6},{8,11},{9,8},{10,9... | collective-permute-start | bytes 368648 | tf_op jit(solution)/shard_map/ppermute | solution.py:34
  17.0 1.5 %collective-permute-start.2 = (bf16[8,32,240]{2,1,0:T(8,128)(2,1)S(1)}, bf16[8,32,240]{2,1,0:T(8,128)(2,1)S(1)}, u32[]{:S(2)}, u32[]{:S(2)}) collective-permute-start(bf16[8,32,240]{2,1,0:T(8,128)(2,1)S(1)} %get-tuple-element.15.refs_0_), channel_id=1, source_target_pairs={{0,3},{1,0},{2,1},{3,2},{4,7},{5,4},{6,5},{7,6},{8,11},{9,8},{10,9... | collective-permute-start | bytes 368648 | tf_op jit(solution)/shard_map/ppermute | solution.py:34
  18.5 0.5 %collective-permute-start.5 = (bf16[8,32,240]{2,1,0:T(8,128)(2,1)S(1)}, bf16[8,32,240]{2,1,0:T(8,128)(2,1)S(1)}, u32[]{:S(2)}, u32[]{:S(2)}) collective-permute-start(bf16[8,32,240]{2,1,0:T(8,128)(2,1)S(1)} %get-tuple-element.16.refs_1_), channel_id=1, source_target_pairs={{0,1},{1,2},{2,3},{3,0},{4,5},{5,6},{6,7},{7,4},{8,9},{9,10},{10,1... | collective-permute-start | bytes 368648 | tf_op jit(solution)/shard_map/ppermute | solution.py:34
  19.0 1.4 %collective-permute-done.4.refs_4_ = bf16[8,32,240]{2,1,0:T(8,128)(2,1)S(1)} collective-permute-done((bf16[8,32,240]{2,1,0:T(8,128)(2,1)S(1)}, bf16[8,32,240]{2,1,0:T(8,128)(2,1)S(1)}, u32[]{:S(2)}, u32[]{:S(2)}) %collective-permute-start.4) | collective-permute-done | bytes 122912 | tf_op jit(solution)/shard_map/ppermute | solution.py:34
  20.4 0.2 collective-permute-start.6
  20.6 0.3 collective-permute-done.3.refs_3_
  20.9 3.0 %collective-permute-start.7 = (bf16[8,32,240]{2,1,0:T(8,128)(2,1)S(1)}, bf16[8,32,240]{2,1,0:T(8,128)(2,1)S(1)}, u32[]{:S(2)}, u32[]{:S(2)}) collective-permute-start(bf16[8,32,240]{2,1,0:T(8,128)(2,1)S(1)} %collective-permute-done.3.refs_3_), channel_id=1, source_target_pairs={{0,3},{1,0},{2,1},{3,2},{4,7},{5,4},{6,5},{7,6},{8,11},{9,8},{10,9... | collective-permute-start | bytes 368648 | tf_op jit(solution)/shard_map/ppermute | solution.py:34
  23.9 1.4 %days.1 = (bf16[4,32,32,240]{3,2,1,0:T(8,128)(2,1)S(1)}, bf16[4,32,32,240]{3,2,1,0:T(8,128)(2,1)S(1)}, f32[4,32,240]{2,1,0:T(8,128)S(1)}) custom-call(bf16[32,4,8,4,240]{4,3,2,1,0:T(4,128)(2,1)S(1)} %copy-done, bf16[32,4,8,4,240]{4,3,2,1,0:T(4,128)(2,1)S(1)} %copy-done.1), custom_call_target="tpu_custom_call" | custom-call | bytes 15000000 | tf_op jit(solution)/shard_map/days/pallas_call | solution.py:192
  25.4 0.0 copy-start.2
  25.4 0.0 collective-permute-done.2.refs_2_
  25.4 0.5 %collective-permute-done.5.refs_5_ = bf16[8,32,240]{2,1,0:T(8,128)(2,1)S(1)} collective-permute-done((bf16[8,32,240]{2,1,0:T(8,128)(2,1)S(1)}, bf16[8,32,240]{2,1,0:T(8,128)(2,1)S(1)}, u32[]{:S(2)}, u32[]{:S(2)}) %collective-permute-start.5) | collective-permute-done | bytes 122912 | tf_op jit(solution)/shard_map/ppermute | solution.py:34
  25.9 0.4 decode.1.near_ref
  26.4 2.4 %collective-permute-done.6.low_ref = bf16[8,32,240]{2,1,0:T(8,128)(2,1)S(1)} collective-permute-done((bf16[8,32,240]{2,1,0:T(8,128)(2,1)S(1)}, bf16[8,32,240]{2,1,0:T(8,128)(2,1)S(1)}, u32[]{:S(2)}, u32[]{:S(2)}) %collective-permute-start.6) | collective-permute-done | bytes 122912 | tf_op jit(solution)/shard_map/ppermute | solution.py:34
  28.8 0.0 collective-permute-done.7.high_ref
  28.8 1.3 %shard_map.95 = (f32[4,32,240]{2,1,0:T(8,128)S(1)}, f32[64,32,240]{2,1,0:T(8,128)S(1)}) custom-call(s32[4,32]{1,0:T(4,128)S(1)} %bitcast.2, f32[48,32,240]{2,1,0:T(8,128)S(1)} %decode.1.near_ref, bf16[8,32,240]{2,1,0:T(8,128)(2,1)S(1)} %collective-permute-done.6.low_ref, bf16[8,32,240]{2,1,0:T(8,128)(2,1)S(1)} %collective-permute-done.7.high_ref, ...), custom_call_target="tpu_custom_call" | custom-call | bytes 3000000 | tf_op jit(solution)/shard_map/pallas_call | solution.py:263
  30.0 1.0 %shard_map.97 = f32[4,32,240]{2,1,0:T(8,128)S(1)} custom-call(s32[4,32]{1,0:T(4,128)S(1)} %bitcast.3, f32[64,32,240]{2,1,0:T(8,128)S(1)} %get-tuple-element.20.clim_ref, bf16[4,32,32,240]{3,2,1,0:T(8,128)(2,1)S(1)} %get-tuple-element.17.fore_ref, bf16[4,32,32,240]{3,2,1,0:T(8,128)(2,1)S(1)} %get-tuple-element.18.obs_ref, ...), custom_call_target="tpu_custom_call" | custom-call | bytes 3000000 | tf_op jit(solution)/shard_map/pallas_call | solution.py:263
  31.0 1.0 %shard_map.96 = f32[4,32,240]{2,1,0:T(8,128)S(1)} custom-call(s32[4,32]{1,0:T(4,128)S(1)} %bitcast.4, f32[64,32,240]{2,1,0:T(8,128)S(1)} %get-tuple-element.20.clim_ref, bf16[4,32,32,240]{3,2,1,0:T(8,128)(2,1)S(1)} %get-tuple-element.17.fore_ref, bf16[4,32,32,240]{3,2,1,0:T(8,128)(2,1)S(1)} %get-tuple-element.18.obs_ref, ...), custom_call_target="tpu_custom_call" | custom-call | bytes 3000000 | tf_op jit(solution)/shard_map/pallas_call | solution.py:263
  32.1 0.1 collective-permute-start.8
  32.2 3.2 %collective-permute-start.10 = (f32[4,32,240]{2,1,0:T(8,128)S(1)}, f32[4,32,240]{2,1,0:T(8,128)S(1)}, u32[]{:S(2)}, u32[]{:S(2)}) collective-permute-start(f32[4,32,240]{2,1,0:T(8,128)S(1)} %shard_map.97), channel_id=1, source_target_pairs={{0,3},{1,0},{2,1},{3,2},{4,7},{5,4},{6,5},{7,6},{8,11},{9,8},{10,9... | collective-permute-start | bytes 368648 | tf_op jit(solution)/shard_map/ppermute | solution.py:34
  35.4 0.5 %collective-permute-start.9 = (f32[4,32,240]{2,1,0:T(8,128)S(1)}, f32[4,32,240]{2,1,0:T(8,128)S(1)}, u32[]{:S(2)}, u32[]{:S(2)}) collective-permute-start(f32[4,32,240]{2,1,0:T(8,128)S(1)} %get-tuple-element.21), channel_id=1, source_target_pairs={{0,2},{1,3},{2,0},{3,1},{4,6},{5,7},{6,4},{7,5},{8,10},{9,11},{10,... | collective-permute-start | bytes 368648 | tf_op jit(solution)/shard_map/ppermute | solution.py:34
  35.9 1.0 %shard_map.98.own_ref = f32[4,32,240]{2,1,0:T(8,128)S(1)} custom-call(s32[4,32]{1,0:T(4,128)S(1)} %bitcast.5, f32[64,32,240]{2,1,0:T(8,128)S(1)} %get-tuple-element.20.clim_ref, bf16[4,32,32,240]{3,2,1,0:T(8,128)(2,1)S(1)} %get-tuple-element.17.fore_ref, bf16[4,32,32,240]{3,2,1,0:T(8,128)(2,1)S(1)} %get-tuple-element.18.obs_ref, ...), custom_call_target="tpu_custom_call" | custom-call | bytes 3000000 | tf_op jit(solution)/shard_map/pallas_call | solution.py:263
  36.9 2.0 %collective-permute-done.8.one_ref = f32[4,32,240]{2,1,0:T(8,128)S(1)} collective-permute-done((f32[4,32,240]{2,1,0:T(8,128)S(1)}, f32[4,32,240]{2,1,0:T(8,128)S(1)}, u32[]{:S(2)}, u32[]{:S(2)}) %collective-permute-start.8) | collective-permute-done | bytes 122912 | tf_op jit(solution)/shard_map/ppermute | solution.py:34
  38.9 2.1 %collective-permute-done.10.three_ref = f32[4,32,240]{2,1,0:T(8,128)S(1)} collective-permute-done((f32[4,32,240]{2,1,0:T(8,128)S(1)}, f32[4,32,240]{2,1,0:T(8,128)S(1)}, u32[]{:S(2)}, u32[]{:S(2)}) %collective-permute-start.10) | collective-permute-done | bytes 122912 | tf_op jit(solution)/shard_map/ppermute | solution.py:34
  41.0 1.4 %collective-permute-done.9.two_ref = f32[4,32,240]{2,1,0:T(8,128)S(1)} collective-permute-done((f32[4,32,240]{2,1,0:T(8,128)S(1)}, f32[4,32,240]{2,1,0:T(8,128)S(1)}, u32[]{:S(2)}, u32[]{:S(2)}) %collective-permute-start.9) | collective-permute-done | bytes 122912 | tf_op jit(solution)/shard_map/ppermute | solution.py:34
  42.4 1.2 %maps.1 = (f32[1,8,4,240]{3,2,1,0:T(4,128)}, f32[1,8,4,240]{3,2,1,0:T(4,128)}) custom-call(f32[128]{0:T(128)S(1)} %copy-done.5, f32[4,32,240]{2,1,0:T(8,128)S(1)} %collective-permute-done.8.one_ref, f32[4,32,240]{2,1,0:T(8,128)S(1)} %collective-permute-done.9.two_ref, f32[4,32,240]{2,1,0:T(8,128)S(1)} %collective-permute-done.10.three_ref, ...), custom_call_target="tpu_custom_call" | custom-call | bytes 3000000 | tf_op jit(solution)/shard_map/maps/pallas_call | solution.py:295
  (13 shorter events, 0.0 us)
Async XLA Ops:
  0.6 11.8 %copy-start.3 = (s32[4,10]{1,0:T(4,128)S(1)}, s32[4,10]{1,0:T(4,128)}, u32[]{:S(2)}) copy-start(s32[4,10]{1,0:T(4,128)} %index_ref.1) | copy-start | bytes 484
  0.6 11.8 %copy-start.4 = (f32[4,10]{1,0:T(4,128)S(1)}, f32[4,10]{1,0:T(4,128)}, u32[]{:S(2)}) copy-start(f32[4,10]{1,0:T(4,128)} %extent_ref.1) | copy-start | bytes 484
  0.7 11.8 %copy-start.6 = (s32[4]{0:T(128)S(1)}, s32[4]{0:T(128)}, u32[]{:S(2)}) copy-start(s32[4]{0:T(128)} %count_ref.1) | copy-start | bytes 52
  0.7 23.3 %copy-start = (bf16[32,4,8,4,240]{4,3,2,1,0:T(4,128)(2,1)S(1)}, bf16[32,4,8,4,240]{4,3,2,1,0:T(4,128)(2,1)}, u32[]{:S(2)}) copy-start(bf16[32,4,8,4,240]{4,3,2,1,0:T(4,128)(2,1)} %fore_ref.1) | copy-start | bytes 5898244
  0.7 23.3 %copy-start.1 = (bf16[32,4,8,4,240]{4,3,2,1,0:T(4,128)(2,1)S(1)}, bf16[32,4,8,4,240]{4,3,2,1,0:T(4,128)(2,1)}, u32[]{:S(2)}) copy-start(bf16[32,4,8,4,240]{4,3,2,1,0:T(4,128)(2,1)} %obs_ref.1) | copy-start | bytes 5898244
  5.5 7.0 %collective-permute-start = (bf16[16,3,8,240]{3,2,1,0:T(8,128)(2,1)S(1)}, bf16[16,3,8,240]{3,2,1,0:T(8,128)(2,1)S(1)}, u32[]{:S(2)}, u32[]{:S(2)}) collective-permute-start(bf16[16,3,8,240]{3,2,1,0:T(8,128)(2,1)S(1)} %get-tuple-element.12), channel_id=1, source_target_pairs={{4,8},{12,16},{20,24},{28,32},{36,40},{44,48},{52,56},{60,64},{68,... | collective-permute-start | bytes 552968 | tf_op jit(solution)/shard_map/ppermute | solution.py:312
  7.4 5.1 %collective-permute-start.1 = (bf16[16,3,8,240]{3,2,1,0:T(8,128)(2,1)S(1)}, bf16[16,3,8,240]{3,2,1,0:T(8,128)(2,1)S(1)}, u32[]{:S(2)}, u32[]{:S(2)}) collective-permute-start(bf16[16,3,8,240]{3,2,1,0:T(8,128)(2,1)S(1)} %get-tuple-element.14), channel_id=1, source_target_pairs={{0,4},{4,0},{8,12},{12,8},{16,20},{20,16},{24,28},{28,24},{32,36},... | collective-permute-start | bytes 552968 | tf_op jit(solution)/shard_map/ppermute | solution.py:313
  13.7 6.7 %collective-permute-start.4 = (bf16[8,32,240]{2,1,0:T(8,128)(2,1)S(1)}, bf16[8,32,240]{2,1,0:T(8,128)(2,1)S(1)}, u32[]{:S(2)}, u32[]{:S(2)}) collective-permute-start(bf16[8,32,240]{2,1,0:T(8,128)(2,1)S(1)} %get-tuple-element.15.refs_0_), channel_id=1, source_target_pairs={{0,1},{1,2},{2,3},{3,0},{4,5},{5,6},{6,7},{7,4},{8,9},{9,10},{10,1... | collective-permute-start | bytes 368648 | tf_op jit(solution)/shard_map/ppermute | solution.py:34
  15.3 5.7 %collective-permute-start.3 = (bf16[8,32,240]{2,1,0:T(8,128)(2,1)S(1)}, bf16[8,32,240]{2,1,0:T(8,128)(2,1)S(1)}, u32[]{:S(2)}, u32[]{:S(2)}) collective-permute-start(bf16[8,32,240]{2,1,0:T(8,128)(2,1)S(1)} %get-tuple-element.16.refs_1_), channel_id=1, source_target_pairs={{0,3},{1,0},{2,1},{3,2},{4,7},{5,4},{6,5},{7,6},{8,11},{9,8},{10,9... | collective-permute-start | bytes 368648 | tf_op jit(solution)/shard_map/ppermute | solution.py:34
  17.0 8.4 %collective-permute-start.2 = (bf16[8,32,240]{2,1,0:T(8,128)(2,1)S(1)}, bf16[8,32,240]{2,1,0:T(8,128)(2,1)S(1)}, u32[]{:S(2)}, u32[]{:S(2)}) collective-permute-start(bf16[8,32,240]{2,1,0:T(8,128)(2,1)S(1)} %get-tuple-element.15.refs_0_), channel_id=1, source_target_pairs={{0,3},{1,0},{2,1},{3,2},{4,7},{5,4},{6,5},{7,6},{8,11},{9,8},{10,9... | collective-permute-start | bytes 368648 | tf_op jit(solution)/shard_map/ppermute | solution.py:34
  18.5 7.4 %collective-permute-start.5 = (bf16[8,32,240]{2,1,0:T(8,128)(2,1)S(1)}, bf16[8,32,240]{2,1,0:T(8,128)(2,1)S(1)}, u32[]{:S(2)}, u32[]{:S(2)}) collective-permute-start(bf16[8,32,240]{2,1,0:T(8,128)(2,1)S(1)} %get-tuple-element.16.refs_1_), channel_id=1, source_target_pairs={{0,1},{1,2},{2,3},{3,0},{4,5},{5,6},{6,7},{7,4},{8,9},{9,10},{10,1... | collective-permute-start | bytes 368648 | tf_op jit(solution)/shard_map/ppermute | solution.py:34
  20.4 8.3 %collective-permute-start.6 = (bf16[8,32,240]{2,1,0:T(8,128)(2,1)S(1)}, bf16[8,32,240]{2,1,0:T(8,128)(2,1)S(1)}, u32[]{:S(2)}, u32[]{:S(2)}) collective-permute-start(bf16[8,32,240]{2,1,0:T(8,128)(2,1)S(1)} %collective-permute-done.4.refs_4_), channel_id=1, source_target_pairs={{0,1},{1,2},{2,3},{3,0},{4,5},{5,6},{6,7},{7,4},{8,9},{9,10},{10,1... | collective-permute-start | bytes 368648 | tf_op jit(solution)/shard_map/ppermute | solution.py:34
  20.9 7.8 %collective-permute-start.7 = (bf16[8,32,240]{2,1,0:T(8,128)(2,1)S(1)}, bf16[8,32,240]{2,1,0:T(8,128)(2,1)S(1)}, u32[]{:S(2)}, u32[]{:S(2)}) collective-permute-start(bf16[8,32,240]{2,1,0:T(8,128)(2,1)S(1)} %collective-permute-done.3.refs_3_), channel_id=1, source_target_pairs={{0,3},{1,0},{2,1},{3,2},{4,7},{5,4},{6,5},{7,6},{8,11},{9,8},{10,9... | collective-permute-start | bytes 368648 | tf_op jit(solution)/shard_map/ppermute | solution.py:34
  25.4 3.4 %copy-start.2 = (s32[32,4]{0,1:T(4,128)S(1)}, s32[32,4]{0,1:T(4,128)}, u32[]{:S(2)}) copy-start(s32[32,4]{0,1:T(4,128)} %param.12) | copy-start | bytes 1540
  32.1 6.8 %collective-permute-start.8 = (f32[4,32,240]{2,1,0:T(8,128)S(1)}, f32[4,32,240]{2,1,0:T(8,128)S(1)}, u32[]{:S(2)}, u32[]{:S(2)}) collective-permute-start(f32[4,32,240]{2,1,0:T(8,128)S(1)} %shard_map.96), channel_id=1, source_target_pairs={{0,1},{1,2},{2,3},{3,0},{4,5},{5,6},{6,7},{7,4},{8,9},{9,10},{10,1... | collective-permute-start | bytes 368648 | tf_op jit(solution)/shard_map/ppermute | solution.py:34
  32.2 8.8 %collective-permute-start.10 = (f32[4,32,240]{2,1,0:T(8,128)S(1)}, f32[4,32,240]{2,1,0:T(8,128)S(1)}, u32[]{:S(2)}, u32[]{:S(2)}) collective-permute-start(f32[4,32,240]{2,1,0:T(8,128)S(1)} %shard_map.97), channel_id=1, source_target_pairs={{0,3},{1,0},{2,1},{3,2},{4,7},{5,4},{6,5},{7,6},{8,11},{9,8},{10,9... | collective-permute-start | bytes 368648 | tf_op jit(solution)/shard_map/ppermute | solution.py:34
  35.4 7.0 %copy-start.5 = (f32[128]{0:T(128)S(1)}, f32[128]{0:T(128)}, u32[]{:S(2)}) copy-start(f32[128]{0:T(128)} %constant.2.clone.scale_ref) | copy-start | bytes 1540
  35.4 7.0 %collective-permute-start.9 = (f32[4,32,240]{2,1,0:T(8,128)S(1)}, f32[4,32,240]{2,1,0:T(8,128)S(1)}, u32[]{:S(2)}, u32[]{:S(2)}) collective-permute-start(f32[4,32,240]{2,1,0:T(8,128)S(1)} %get-tuple-element.21), channel_id=1, source_target_pairs={{0,2},{1,3},{2,0},{3,1},{4,6},{5,7},{6,4},{7,5},{8,10},{9,11},{10,... | collective-permute-start | bytes 368648 | tf_op jit(solution)/shard_map/ppermute | solution.py:34

commit v4 on v3

--- a/solution.py
+++ b/solution.py
@@ -1,4 +1,3 @@
-import functools
 import math
 
 import jax
@@ -18,15 +17,20 @@
 TILE = 4
 OVER = 10
 EDGE = 3
+MID = BAND - 2 * EDGE
 ROWS = BAND + 2 * EDGE
+SPAN = BAND + EDGE
 BINS = 16
 HALF = BINS // 2
 DAYS = 32
 SLOTS = 4
 FLAT = VARS * TILE
-LON_LIMIT = 52
+EDGE_LIMIT = 57
+MID_LIMIT = 50
 CODE_RATE = 10.0
 CODE_BASE = 120.0
+SUM_SCALE = 64.0
+SUM_FLOOR = 2.0**-126
 
 
 def shifted(value, step):
@@ -60,45 +64,78 @@
     )
 
 
-def lon_kernel(field_ref, own_ref, cross_ref, inner_ref, buf, table_buf, sems):
+def edge_kernel(field_ref, cross_ref, inner_ref, buf, table_buf, sems):
+    odd = lax.rem(lax.axis_index("lat"), 2)
+    firsts = (odd * (BAND - EDGE), (1 - odd) * (BAND - EDGE))
+    outs = (cross_ref, inner_ref)
+    jobs = []
+    for n, first in enumerate(firsts):
+        for part in range(2):
+            some = pl.ds(part * HALF, HALF)
+            copy = pltpu.make_async_copy(
+                field_ref.at[some, pl.ds(first, EDGE)], buf.at[n, some], sems.at[2 * n + part]
+            )
+            copy.start()
+            jobs.append((copy, n, slice(part * HALF, (part + 1) * HALF)))
+    fill_table(table_buf)
+    for copy, n, some in jobs:
+        copy.wait()
+        outs[n][some] = lon_mean(buf[n, some], table_buf[...])
+
+
+def edge_rows(field):
+    vmem = pl.BlockSpec(memory_space=pltpu.VMEM)
+    return pl.pallas_call(
+        edge_kernel,
+        in_specs=[pl.BlockSpec(memory_space=pl.ANY)],
+        out_specs=[vmem] * 2,
+        out_shape=[jax.ShapeDtypeStruct((BINS, EDGE, VARS, DEST_MERIDIANS), jnp.bfloat16)] * 2,
+        scratch_shapes=[
+            pltpu.VMEM((2, BINS, EDGE, VARS, SRC_LON), jnp.bfloat16),
+            pltpu.VMEM((SRC_LON, DEST_MERIDIANS), jnp.bfloat16),
+            pltpu.SemaphoreType.DMA((4,)),
+        ],
+        compiler_params=params(EDGE_LIMIT),
+        cost_estimate=cost(2),
+        name="edge_rows",
+    )(field)
+
+
+def mid_kernel(field_ref, out_ref, buf, table_buf, sems):
     parts = sems.shape[0]
     size = BINS // parts
-    odd = lax.rem(lax.axis_index("lat"), 2)
-    cross_first = odd * (BAND - EDGE)
-    inner_first = (1 - odd) * (BAND - EDGE)
+    block = 2
     copies = []
     for n in range(parts):
         some = pl.ds(n * size, size)
-        copy = pltpu.make_async_copy(field_ref.at[some], buf.at[some], sems.at[n])
+        copy = pltpu.make_async_copy(
+            field_ref.at[some, pl.ds(EDGE, MID)], buf.at[some], sems.at[n]
+        )
         copy.start()
         copies.append(copy)
     fill_table(table_buf)
-    for s in range(BINS):
-        if s % size == 0:
-            copies[s // size].wait()
-        own_ref[s] = lon_mean(buf[s], table_buf[...])
-        cross_ref[s] = own_ref[s, pl.ds(cross_first, EDGE)]
-        inner_ref[s] = own_ref[s, pl.ds(inner_first, EDGE)]
-
-
-def lon_rows(field):
+    for first in range(0, BINS, block):
+        if first % size == 0:
+            copies[first // size].wait()
+        some = slice(first, first + block)
+        out_ref[some] = lon_mean(buf[some], table_buf[...])
+
+
+def mid_rows(field):
     parts = 4
-    hbm = pl.BlockSpec(memory_space=pl.ANY)
-    vmem = pl.BlockSpec(memory_space=pltpu.VMEM)
-    shape = lambda count: jax.ShapeDtypeStruct((BINS, count, VARS, DEST_MERIDIANS), jnp.bfloat16)
-    return pl.pallas_call(
-        lon_kernel,
-        in_specs=[hbm],
-        out_specs=[vmem] * 3,
-        out_shape=[shape(BAND), shape(EDGE), shape(EDGE)],
+    return pl.pallas_call(
+        mid_kernel,
+        in_specs=[pl.BlockSpec(memory_space=pl.ANY)],
+        out_specs=pl.BlockSpec(memory_space=pltpu.VMEM),
+        out_shape=jax.ShapeDtypeStruct((BINS, MID, VARS, DEST_MERIDIANS), jnp.bfloat16),
         scratch_shapes=[
-            pltpu.VMEM((BINS, BAND, VARS, SRC_LON), jnp.bfloat16),
+            pltpu.VMEM((BINS, MID, VARS, SRC_LON), jnp.bfloat16),
             pltpu.VMEM((SRC_LON, DEST_MERIDIANS), jnp.bfloat16),
             pltpu.SemaphoreType.DMA((parts,)),
         ],
-        compiler_params=params(LON_LIMIT),
-        cost_estimate=cost(6),
-        name="lon_rows",
+        compiler_params=params(MID_LIMIT),
+        cost_estimate=cost(4),
+        name="mid_rows",
     )(field)
 
 
@@ -129,9 +166,11 @@
             value = jnp.where(k < count_ref[t], extent_ref[t, k], jnp.float32(0.0))
             total = total + value
             row = index_ref[t, k] - lat * BAND
-            beyond = jnp.where(row >= BAND, row - BAND - EDGE, row)
-            turned = jnp.where(row < 0, row + BAND + EDGE, beyond)
-            column = jnp.where(odd, turned, row) + EDGE
+            inside = (row >= EDGE) & (row < BAND - EDGE)
+            shift = jnp.where(inside, 0, jnp.where(row < 0, SPAN, -SPAN))
+            shift = jnp.where((row >= 0) & (row < EDGE), BAND - EDGE, shift)
+            shift = jnp.where((row >= BAND - EDGE) & (row < BAND), EDGE - BAND, shift)
+            column = row + EDGE + jnp.where(odd, shift, 0)
             dense = dense + jnp.where(spot == column, value, 0.0)
         sums = jnp.where(here, total, sums)
     dense = dense / sums
@@ -143,11 +182,13 @@
 
 
 def climate_kernel(
-    index_ref, extent_ref, count_ref, cross_ref, own_ref, inner_ref, low_ref, high_ref
+    index_ref, extent_ref, count_ref, cross_ref, cross_own, mid_ref, inner_own, inner_ref,
+    low_ref, high_ref,
 ):
     weights = weight_matrix(index_ref, extent_ref, count_ref)
     for s in range(BINS):
-        rows = jnp.concatenate([cross_ref[s], own_ref[s], inner_ref[s]], axis=0)
+        parts = (cross_ref, cross_own, mid_ref, inner_own, inner_ref)
+        rows = jnp.concatenate([ref[s] for ref in parts], axis=0)
         rows = rows.reshape(ROWS * VARS, DEST_MERIDIANS)
         parts = jnp.dot(weights, rows, preferred_element_type=jnp.float32)
         value = parts[:FLAT] + parts[FLAT : 2 * FLAT] + parts[2 * FLAT :]
@@ -155,18 +196,18 @@
         out_ref[s % HALF] = encode(value)
 
 
-def climate_code(index, extent, count, cross, own, inner):
+def climate_code(*arrays):
     smem = pl.BlockSpec(memory_space=pltpu.SMEM)
     vmem = pl.BlockSpec(memory_space=pltpu.VMEM)
     return pl.pallas_call(
         climate_kernel,
-        in_specs=[smem] * 3 + [vmem] * 3,
+        in_specs=[smem] * 3 + [vmem] * 5,
         out_specs=[vmem] * 2,
         out_shape=[jax.ShapeDtypeStruct((HALF, FLAT, DEST_MERIDIANS), jnp.bfloat16)] * 2,
         compiler_params=params(8),
         cost_estimate=cost(2),
         name="climate",
-    )(index, extent, count, cross, own, inner)
+    )(*arrays)
 
 
 def days_kernel(fore_ref, obs_ref, fore_out, obs_out, error_out):
@@ -219,7 +260,21 @@
     )(*codes)
 
 
-def lead_sums(k, bins_ref, clim_ref, fore_ref, obs_ref, error_ref, out_ref):
+def encode_sum(value):
+    scaled = value * SUM_SCALE
+    square = scaled * scaled
+    power = square * square * square
+    return jnp.where(value < 0, -power, power).astype(jnp.bfloat16)
+
+
+def decode_sum(code):
+    wide = code.astype(jnp.float32)
+    size = jnp.maximum(jnp.abs(wide), SUM_FLOOR)
+    root = jnp.exp2(jnp.log2(size) * (1.0 / 6.0)) * (1.0 / SUM_SCALE)
+    return jnp.where(wide < 0, -root, root)
+
+
+def lead_sums(k, bins_ref, clim_ref, fore_ref, obs_ref, error_ref, out_ref, kept):
     slot = lax.axis_index("slot")
     lead = lax.rem(slot + k, SLOTS)
     first = slot * BINS
@@ -241,38 +296,59 @@
         zero = jnp.zeros((half, DEST_MERIDIANS), jnp.float32)
         sums = lax.fori_loop(0, DAYS, step, (zero,) * 3, unroll=4)
         for n, value in enumerate(sums):
-            out_ref[n + 1, some] = value
-    out_ref[0] = error_ref[k]
-
-
-def first_kernel(
-    k, bins_ref, near_ref, low_ref, high_ref, fore_ref, obs_ref, error_ref, out_ref, clim_ref
+            out_ref[n + 1, some] = kept(value)
+    out_ref[0] = kept(error_ref[k])
+
+
+def others_kernel(
+    bins_ref, near_ref, low_ref, high_ref, fore_ref, obs_ref, error_ref,
+    one_ref, two_ref, three_ref, clim_ref,
 ):
     clim_ref[: 2 * BINS] = near_ref[: 2 * BINS]
     clim_ref[3 * BINS :] = near_ref[2 * BINS :]
     clim_ref[2 * BINS : 2 * BINS + HALF] = decode(low_ref[...])
     clim_ref[2 * BINS + HALF : 3 * BINS] = decode(high_ref[...])
-    lead_sums(k, bins_ref, clim_ref, fore_ref, obs_ref, error_ref, out_ref)
-
-
-def skill_sums(k, bins, clim, fore, obs, error):
-    vmem = pl.BlockSpec(memory_space=pltpu.VMEM)
-    out = jax.ShapeDtypeStruct((4, FLAT, DEST_MERIDIANS), jnp.float32)
+    for k, out_ref in ((1, one_ref), (2, two_ref), (3, three_ref)):
+        lead_sums(k, bins_ref, clim_ref, fore_ref, obs_ref, error_ref, out_ref, encode_sum)
+
+
+def mine_kernel(bins_ref, clim_ref, fore_ref, obs_ref, error_ref, out_ref):
+    lead_sums(0, bins_ref, clim_ref, fore_ref, obs_ref, error_ref, out_ref, lambda value: value)
+
+
+def other_sums(bins, near, low, high, fore, obs, error):
+    vmem = pl.BlockSpec(memory_space=pltpu.VMEM)
+    code = jax.ShapeDtypeStruct((4, FLAT, DEST_MERIDIANS), jnp.bfloat16)
     whole = jax.ShapeDtypeStruct((SLOTS * BINS, FLAT, DEST_MERIDIANS), jnp.float32)
-    first = len(clim) > 1
-    return pl.pallas_call(
-        functools.partial(first_kernel if first else lead_sums, k),
-        in_specs=[pl.BlockSpec(memory_space=pltpu.SMEM)] + [vmem] * (3 + len(clim)),
-        out_specs=[vmem, vmem] if first else vmem,
-        out_shape=[out, whole] if first else out,
+    return pl.pallas_call(
+        others_kernel,
+        in_specs=[pl.BlockSpec(memory_space=pltpu.SMEM)] + [vmem] * 6,
+        out_specs=[vmem] * 4,
+        out_shape=[code, code, code, whole],
+        compiler_params=params(16),
+        cost_estimate=cost(3),
+        name="other_sums",
+    )(bins, near, low, high, fore, obs, error)
+
+
+def my_sums(bins, clim, fore, obs, error):
+    vmem = pl.BlockSpec(memory_space=pltpu.VMEM)
+    return pl.pallas_call(
+        mine_kernel,
+        in_specs=[pl.BlockSpec(memory_space=pltpu.SMEM)] + [vmem] * 4,
+        out_specs=vmem,
+        out_shape=jax.ShapeDtypeStruct((4, FLAT, DEST_MERIDIANS), jnp.float32),
         compiler_params=params(16),
         cost_estimate=cost(1),
-    )(bins, *clim, fore, obs, error)
+        name="my_sums",
+    )(bins, clim, fore, obs, error)
 
 
 def maps_kernel(scale_ref, one_ref, two_ref, three_ref, own_ref, rmse_ref, acc_ref):
     lat = lax.axis_index("lat")
-    total = own_ref[...] + one_ref[...] + two_ref[...] + three_ref[...]
+    total = own_ref[...]
+    for code_ref in (one_ref, two_ref, three_ref):
+        total = total + decode_sum(code_ref[...])
     line = lax.broadcasted_iota(jnp.int32, (FLAT, DEST_MERIDIANS), 0)
     scale = jnp.zeros((FLAT, DEST_MERIDIANS), jnp.float32)
     for t in range(TILE):
@@ -305,27 +381,30 @@
 
 def body(normals, index, extent, count, bins, prognosis, analysis):
     field = jnp.transpose(normals, (0, 2, 1, 3))
-    own, cross_edge, inner_edge = lon_rows(field)
+    cross_own, inner_own = edge_rows(field)
     devices = lax.axis_size("lat")
     meets = [(i, i + 1) for i in range(1, devices - 1, 2)]
     meets += [(j, i) for i, j in meets]
-    cross = lax.ppermute(cross_edge, "lat", meets)
-    inner = lax.ppermute(inner_edge, "lat", [(i, i ^ 1) for i in range(devices)])
-    fore, obs, error = relaid_days(prognosis, analysis)
-    low, high = climate_code(index, extent, count, cross, own, inner)
+    cross = lax.ppermute(cross_own, "lat", meets)
+    inner = lax.ppermute(inner_own, "lat", [(i, i ^ 1) for i in range(devices)])
+    mid = mid_rows(field)
+    low, high = climate_code(index, extent, count, cross, cross_own, mid, inner_own, inner)
     left_low = shifted(low, 1)
     right_high = shifted(high, -1)
     left_high = shifted(high, 1)
     right_low = shifted(low, -1)
     far_low = shifted(left_low, 1)
     far_high = shifted(right_high, -1)
+    fore, obs, error = relaid_days(prognosis, analysis)
     near = decoded(low, high, right_low, right_high, left_low, left_high)
     wanted = jnp.transpose(bins)
-    to_two, clim = skill_sums(2, wanted, (near, far_low, far_high), fore, obs, error)
+    to_one, to_two, to_three, clim = other_sums(
+        wanted, near, far_low, far_high, fore, obs, error
+    )
     two = shifted(to_two, 2)
-    one = shifted(skill_sums(1, wanted, (clim,), fore, obs, error), 1)
-    three = shifted(skill_sums(3, wanted, (clim,), fore, obs, error), 3)
-    mine = skill_sums(0, wanted, (clim,), fore, obs, error)
+    one = shifted(to_one, 1)
+    three = shifted(to_three, 3)
+    mine = my_sums(wanted, clim, fore, obs, error)
     return tuple(maps(one, two, three, mine))
 
 

time: 43.7 us -> 42 us (0.961)
  the two profiles are of different devices: /device:TPU:112 before, /device:TPU:24 now
where the time goes in v4:
time: 42 us; the launch traced here: 41.8 us
  starting transfers between devices  18.9 us (45%)
  Pallas kernels  15.4 us (37%)
  waiting for transfers between devices  6.67 us (16%)
  between operations  0.85 us (2%)
    ppermute x9, starting transfers between devices, shifted(): lax.ppermute(value, 'slot', [(i, (i + step) % slots) for i in range(slots)])  13.2 us
    ppermute x9, waiting for transfers between devices, shifted(): lax.ppermute(value, 'slot', [(i, (i + step) % slots) for i in range(slots)])  6.66 us
    ppermute x1, starting transfers between devices, body(): cross = lax.ppermute(cross_own, 'lat', meets)  5.56 us
    pallas_call x1, Pallas kernels, mid_rows(): pl.pallas_call(mid_kernel, in_specs=[pl.BlockSpec(memory_space=pl.ANY)],...  3.89 us
    pallas_call x1, Pallas kernels, edge_rows(): pl.pallas_call(edge_kernel, in_specs=[pl.BlockSpec(memory_space=pl.ANY)],...  3.6 us
    pallas_call x1, Pallas kernels, other_sums(): pl.pallas_call(others_kernel, in_specs=[pl.BlockSpec(memory_space=pltpu.S...  2.33 us
    pallas_call x1, Pallas kernels, relaid_days(): pl.pallas_call(days_kernel, in_specs=[vmem] * 2, out_specs=[vmem] * 3, ou...  1.44 us
    pallas_call x1, Pallas kernels, maps(): pl.pallas_call(maps_kernel, in_specs=[pl.BlockSpec(memory_space=pltpu.SME...  1.35 us
  transfers between devices with their start and end apart: 11, of which 5 were waited for; matrix products, arithmetic and copies ran while one was open for 0% of the time, Pallas kernels for 16%

profile of v4, /device:TPU:24, one launch (start us, length us, event | category | flops | bytes accessed | tf_op | source)
XLA Modules:
  0.0 41.8 jit_solution(11506715970140466346)
XLA Ops:
  0.6 3.6 %edge_rows.1 = (bf16[16,3,8,240]{3,2,1,0:T(8,128)(2,1)}, bf16[16,3,8,240]{3,2,1,0:T(8,128)(2,1)}) custom-call(bf16[16,22,8,1440]{3,2,1,0:T(8,128)(2,1)} %bitcast.4), custom_call_target="tpu_custom_call" | custom-call | bytes 6000000 | tf_op jit(solution)/shard_map/edge_rows/pallas_call | solution.py:88
  4.2 5.6 %collective-permute-start = (bf16[16,3,8,240]{3,2,1,0:T(8,128)(2,1)}, bf16[16,3,8,240]{3,2,1,0:T(8,128)(2,1)S(1)}, u32[]{:S(2)}, u32[]{:S(2)}) collective-permute-start(bf16[16,3,8,240]{3,2,1,0:T(8,128)(2,1)} %get-tuple-element.13.cross_own), channel_id=1, source_target_pairs={{4,8},{12,16},{20,24},{28,32},{36,40},{44,48},{52,56},{60,64},{68,... | collective-permute-start | bytes 552968 | tf_op jit(solution)/shard_map/ppermute | solution.py:388
  9.8 0.0 copy-start.5
  9.8 0.0 copy-start.6
  9.9 0.0 copy-start.8
  9.9 0.1 collective-permute-start.1
  10.0 0.0 copy-start
  10.0 0.0 copy-start.1
  10.0 3.9 %mid_rows.1.mid_ref = bf16[16,16,8,240]{3,2,1,0:T(8,128)(2,1)S(1)} custom-call(bf16[16,22,8,1440]{3,2,1,0:T(8,128)(2,1)} %bitcast.5), custom_call_target="tpu_custom_call" | custom-call | bytes 12000000 | tf_op jit(solution)/shard_map/mid_rows/pallas_call | solution.py:126
  13.9 0.0 collective-permute-done.cross_ref
  13.9 0.0 collective-permute-done.1.inner_ref
  14.0 1.3 %climate.1 = (bf16[8,32,240]{2,1,0:T(8,128)(2,1)S(1)}, bf16[8,32,240]{2,1,0:T(8,128)(2,1)S(1)}) custom-call(s32[4,10]{1,0:T(4,128)S(1)} %copy-done.5, f32[4,10]{1,0:T(4,128)S(1)} %copy-done.6, s32[4]{0:T(128)S(1)} %copy-done.8, bf16[16,3,8,240]{3,2,1,0:T(8,128)(2,1)S(1)} %collective-permute-done.cross_ref, bf16[16,3,8,240]{3,2,1,0:T(8,128)(2,1)S(1)} %copy-done.2, ...), custom_call_target="tpu_custom_call" | custom-call | bytes 6000000 | tf_op jit(solution)/shard_map/climate/pallas_call | solution.py:202
  15.3 1.6 %collective-permute-start.4 = (bf16[8,32,240]{2,1,0:T(8,128)(2,1)S(1)}, bf16[8,32,240]{2,1,0:T(8,128)(2,1)S(1)}, u32[]{:S(2)}, u32[]{:S(2)}) collective-permute-start(bf16[8,32,240]{2,1,0:T(8,128)(2,1)S(1)} %get-tuple-element.15.refs_0_), channel_id=1, source_target_pairs={{0,1},{1,2},{2,3},{3,0},{4,5},{5,6},{6,7},{7,4},{8,9},{9,10},{10,1... | collective-permute-start | bytes 368648 | tf_op jit(solution)/shard_map/ppermute | solution.py:38
  16.9 1.7 %collective-permute-start.3 = (bf16[8,32,240]{2,1,0:T(8,128)(2,1)S(1)}, bf16[8,32,240]{2,1,0:T(8,128)(2,1)S(1)}, u32[]{:S(2)}, u32[]{:S(2)}) collective-permute-start(bf16[8,32,240]{2,1,0:T(8,128)(2,1)S(1)} %get-tuple-element.16.refs_1_), channel_id=1, source_target_pairs={{0,3},{1,0},{2,1},{3,2},{4,7},{5,4},{6,5},{7,6},{8,11},{9,8},{10,9... | collective-permute-start | bytes 368648 | tf_op jit(solution)/shard_map/ppermute | solution.py:38
  18.6 1.5 %collective-permute-start.2 = (bf16[8,32,240]{2,1,0:T(8,128)(2,1)S(1)}, bf16[8,32,240]{2,1,0:T(8,128)(2,1)S(1)}, u32[]{:S(2)}, u32[]{:S(2)}) collective-permute-start(bf16[8,32,240]{2,1,0:T(8,128)(2,1)S(1)} %get-tuple-element.15.refs_0_), channel_id=1, source_target_pairs={{0,3},{1,0},{2,1},{3,2},{4,7},{5,4},{6,5},{7,6},{8,11},{9,8},{10,9... | collective-permute-start | bytes 368648 | tf_op jit(solution)/shard_map/ppermute | solution.py:38
  20.1 0.5 %collective-permute-start.5 = (bf16[8,32,240]{2,1,0:T(8,128)(2,1)S(1)}, bf16[8,32,240]{2,1,0:T(8,128)(2,1)S(1)}, u32[]{:S(2)}, u32[]{:S(2)}) collective-permute-start(bf16[8,32,240]{2,1,0:T(8,128)(2,1)S(1)} %get-tuple-element.16.refs_1_), channel_id=1, source_target_pairs={{0,1},{1,2},{2,3},{3,0},{4,5},{5,6},{6,7},{7,4},{8,9},{9,10},{10,1... | collective-permute-start | bytes 368648 | tf_op jit(solution)/shard_map/ppermute | solution.py:38
  20.6 1.8 %collective-permute-done.4.refs_4_ = bf16[8,32,240]{2,1,0:T(8,128)(2,1)S(1)} collective-permute-done((bf16[8,32,240]{2,1,0:T(8,128)(2,1)S(1)}, bf16[8,32,240]{2,1,0:T(8,128)(2,1)S(1)}, u32[]{:S(2)}, u32[]{:S(2)}) %collective-permute-start.4) | collective-permute-done | bytes 122912 | tf_op jit(solution)/shard_map/ppermute | solution.py:38
  22.4 0.3 collective-permute-start.6
  22.7 0.5 %collective-permute-done.3.refs_3_ = bf16[8,32,240]{2,1,0:T(8,128)(2,1)S(1)} collective-permute-done((bf16[8,32,240]{2,1,0:T(8,128)(2,1)S(1)}, bf16[8,32,240]{2,1,0:T(8,128)(2,1)S(1)}, u32[]{:S(2)}, u32[]{:S(2)}) %collective-permute-start.3) | collective-permute-done | bytes 122912 | tf_op jit(solution)/shard_map/ppermute | solution.py:38
  23.2 2.9 %collective-permute-start.7 = (bf16[8,32,240]{2,1,0:T(8,128)(2,1)S(1)}, bf16[8,32,240]{2,1,0:T(8,128)(2,1)S(1)}, u32[]{:S(2)}, u32[]{:S(2)}) collective-permute-start(bf16[8,32,240]{2,1,0:T(8,128)(2,1)S(1)} %collective-permute-done.3.refs_3_), channel_id=1, source_target_pairs={{0,3},{1,0},{2,1},{3,2},{4,7},{5,4},{6,5},{7,6},{8,11},{9,8},{10,9... | collective-permute-start | bytes 368648 | tf_op jit(solution)/shard_map/ppermute | solution.py:38
  26.2 1.4 %days.1 = (bf16[4,32,32,240]{3,2,1,0:T(8,128)(2,1)S(1)}, bf16[4,32,32,240]{3,2,1,0:T(8,128)(2,1)S(1)}, f32[4,32,240]{2,1,0:T(8,128)S(1)}) custom-call(bf16[32,4,8,4,240]{4,3,2,1,0:T(4,128)(2,1)S(1)} %copy-done, bf16[32,4,8,4,240]{4,3,2,1,0:T(4,128)(2,1)S(1)} %copy-done.1), custom_call_target="tpu_custom_call" | custom-call | bytes 15000000 | tf_op jit(solution)/shard_map/days/pallas_call | solution.py:233
  27.6 0.0 copy-start.4
  27.6 0.0 collective-permute-done.2.refs_2_
  27.7 0.4 decode.1.near_ref
  28.1 1.1 %collective-permute-done.6.low_ref = bf16[8,32,240]{2,1,0:T(8,128)(2,1)S(1)} collective-permute-done((bf16[8,32,240]{2,1,0:T(8,128)(2,1)S(1)}, bf16[8,32,240]{2,1,0:T(8,128)(2,1)S(1)}, u32[]{:S(2)}, u32[]{:S(2)}) %collective-permute-start.6) | collective-permute-done | bytes 122912 | tf_op jit(solution)/shard_map/ppermute | solution.py:38
  29.2 2.3 %other_sums.1 = (bf16[4,32,240]{2,1,0:T(8,128)(2,1)S(1)}, bf16[4,32,240]{2,1,0:T(8,128)(2,1)S(1)}, bf16[4,32,240]{2,1,0:T(8,128)(2,1)S(1)}, f32[64,32,240]{2,1,0:T(8,128)S(1)}) custom-call(s32[4,32]{1,0:T(4,128)S(1)} %bitcast.2, f32[48,32,240]{2,1,0:T(8,128)S(1)} %decode.1.near_ref, bf16[8,32,240]{2,1,0:T(8,128)(2,1)S(1)} %collective-permute-done.6.low_ref, ...), custom_call_target="tpu_custom_call" | custom-call | bytes 9000000 | tf_op jit(solution)/shard_map/other_sums/pallas_call | solution.py:323
  31.5 0.5 %collective-permute-start.8 = (bf16[4,32,240]{2,1,0:T(8,128)(2,1)S(1)}, bf16[4,32,240]{2,1,0:T(8,128)(2,1)S(1)}, u32[]{:S(2)}, u32[]{:S(2)}) collective-permute-start(bf16[4,32,240]{2,1,0:T(8,128)(2,1)S(1)} %get-tuple-element.20), channel_id=1, source_target_pairs={{0,1},{1,2},{2,3},{3,0},{4,5},{5,6},{6,7},{7,4},{8,9},{9,10},{10,1... | collective-permute-start | bytes 184328 | tf_op jit(solution)/shard_map/ppermute | solution.py:38
  32.1 4.1 %collective-permute-start.9 = (bf16[4,32,240]{2,1,0:T(8,128)(2,1)S(1)}, bf16[4,32,240]{2,1,0:T(8,128)(2,1)S(1)}, u32[]{:S(2)}, u32[]{:S(2)}) collective-permute-start(bf16[4,32,240]{2,1,0:T(8,128)(2,1)S(1)} %get-tuple-element.21), channel_id=1, source_target_pairs={{0,2},{1,3},{2,0},{3,1},{4,6},{5,7},{6,4},{7,5},{8,10},{9,11},{10,... | collective-permute-start | bytes 184328 | tf_op jit(solution)/shard_map/ppermute | solution.py:38
  36.2 1.0 %my_sums.1.own_ref = f32[4,32,240]{2,1,0:T(8,128)S(1)} custom-call(s32[4,32]{1,0:T(4,128)S(1)} %bitcast.3, f32[64,32,240]{2,1,0:T(8,128)S(1)} %get-tuple-element.23.clim_ref, bf16[4,32,32,240]{3,2,1,0:T(8,128)(2,1)S(1)} %get-tuple-element.17.fore_ref, bf16[4,32,32,240]{3,2,1,0:T(8,128)(2,1)S(1)} %get-tuple-element.18.obs_ref, ...), custom_call_target="tpu_custom_call" | custom-call | bytes 3000000 | tf_op jit(solution)/shard_map/my_sums/pallas_call | solution.py:336
  37.3 1.9 %collective-permute-done.9.two_ref = bf16[4,32,240]{2,1,0:T(8,128)(2,1)S(1)} collective-permute-done((bf16[4,32,240]{2,1,0:T(8,128)(2,1)S(1)}, bf16[4,32,240]{2,1,0:T(8,128)(2,1)S(1)}, u32[]{:S(2)}, u32[]{:S(2)}) %collective-permute-start.9) | collective-permute-done | bytes 61472 | tf_op jit(solution)/shard_map/ppermute | solution.py:38
  39.2 1.3 %collective-permute-done.10.three_ref = bf16[4,32,240]{2,1,0:T(8,128)(2,1)S(1)} collective-permute-done((bf16[4,32,240]{2,1,0:T(8,128)(2,1)S(1)}, bf16[4,32,240]{2,1,0:T(8,128)(2,1)S(1)}, u32[]{:S(2)}, u32[]{:S(2)}) %collective-permute-start.10) | collective-permute-done | bytes 61472 | tf_op jit(solution)/shard_map/ppermute | solution.py:38
  40.5 1.3 %maps.1 = (f32[1,8,4,240]{3,2,1,0:T(4,128)}, f32[1,8,4,240]{3,2,1,0:T(4,128)}) custom-call(f32[128]{0:T(128)S(1)} %copy-done.7, bf16[4,32,240]{2,1,0:T(8,128)(2,1)S(1)} %collective-permute-done.8.one_ref, bf16[4,32,240]{2,1,0:T(8,128)(2,1)S(1)} %collective-permute-done.9.two_ref, bf16[4,32,240]{2,1,0:T(8,128)(2,1)S(1)} %collective-permute-done.10.three_ref, ...), custom_call_target="tpu_custom_call" | custom-call | bytes 3000000 | tf_op jit(solution)/shard_map/maps/pallas_call | solution.py:371
  (16 shorter events, 0.0 us)
Async XLA Ops:
  4.2 9.6 %collective-permute-start = (bf16[16,3,8,240]{3,2,1,0:T(8,128)(2,1)}, bf16[16,3,8,240]{3,2,1,0:T(8,128)(2,1)S(1)}, u32[]{:S(2)}, u32[]{:S(2)}) collective-permute-start(bf16[16,3,8,240]{3,2,1,0:T(8,128)(2,1)} %get-tuple-element.13.cross_own), channel_id=1, source_target_pairs={{4,8},{12,16},{20,24},{28,32},{36,40},{44,48},{52,56},{60,64},{68,... | collective-permute-start | bytes 552968 | tf_op jit(solution)/shard_map/ppermute | solution.py:388
  9.8 4.1 %copy-start.2 = (bf16[16,3,8,240]{3,2,1,0:T(8,128)(2,1)S(1)}, bf16[16,3,8,240]{3,2,1,0:T(8,128)(2,1)}, u32[]{:S(2)}) copy-start(bf16[16,3,8,240]{3,2,1,0:T(8,128)(2,1)} %get-tuple-element.13.cross_own) | copy-start | bytes 552964
  9.8 4.1 %copy-start.3 = (bf16[16,3,8,240]{3,2,1,0:T(8,128)(2,1)S(1)}, bf16[16,3,8,240]{3,2,1,0:T(8,128)(2,1)}, u32[]{:S(2)}) copy-start(bf16[16,3,8,240]{3,2,1,0:T(8,128)(2,1)} %get-tuple-element.14.inner_own) | copy-start | bytes 552964
  9.8 4.1 %copy-start.5 = (s32[4,10]{1,0:T(4,128)S(1)}, s32[4,10]{1,0:T(4,128)}, u32[]{:S(2)}) copy-start(s32[4,10]{1,0:T(4,128)} %index_ref.1) | copy-start | bytes 484
  9.8 4.1 %copy-start.6 = (f32[4,10]{1,0:T(4,128)S(1)}, f32[4,10]{1,0:T(4,128)}, u32[]{:S(2)}) copy-start(f32[4,10]{1,0:T(4,128)} %extent_ref.1) | copy-start | bytes 484
  9.9 4.1 %copy-start.8 = (s32[4]{0:T(128)S(1)}, s32[4]{0:T(128)}, u32[]{:S(2)}) copy-start(s32[4]{0:T(128)} %count_ref.1) | copy-start | bytes 52
  9.9 4.0 %collective-permute-start.1 = (bf16[16,3,8,240]{3,2,1,0:T(8,128)(2,1)}, bf16[16,3,8,240]{3,2,1,0:T(8,128)(2,1)S(1)}, u32[]{:S(2)}, u32[]{:S(2)}) collective-permute-start(bf16[16,3,8,240]{3,2,1,0:T(8,128)(2,1)} %get-tuple-element.14.inner_own), channel_id=1, source_target_pairs={{0,4},{4,0},{8,12},{12,8},{16,20},{20,16},{24,28},{28,24},{32,36},... | collective-permute-start | bytes 552968 | tf_op jit(solution)/shard_map/ppermute | solution.py:389
  10.0 16.2 %copy-start = (bf16[32,4,8,4,240]{4,3,2,1,0:T(4,128)(2,1)S(1)}, bf16[32,4,8,4,240]{4,3,2,1,0:T(4,128)(2,1)}, u32[]{:S(2)}) copy-start(bf16[32,4,8,4,240]{4,3,2,1,0:T(4,128)(2,1)} %fore_ref.1) | copy-start | bytes 5898244
  10.0 16.2 %copy-start.1 = (bf16[32,4,8,4,240]{4,3,2,1,0:T(4,128)(2,1)S(1)}, bf16[32,4,8,4,240]{4,3,2,1,0:T(4,128)(2,1)}, u32[]{:S(2)}) copy-start(bf16[32,4,8,4,240]{4,3,2,1,0:T(4,128)(2,1)} %obs_ref.1) | copy-start | bytes 5898244
  15.3 7.2 %collective-permute-start.4 = (bf16[8,32,240]{2,1,0:T(8,128)(2,1)S(1)}, bf16[8,32,240]{2,1,0:T(8,128)(2,1)S(1)}, u32[]{:S(2)}, u32[]{:S(2)}) collective-permute-start(bf16[8,32,240]{2,1,0:T(8,128)(2,1)S(1)} %get-tuple-element.15.refs_0_), channel_id=1, source_target_pairs={{0,1},{1,2},{2,3},{3,0},{4,5},{5,6},{6,7},{7,4},{8,9},{9,10},{10,1... | collective-permute-start | bytes 368648 | tf_op jit(solution)/shard_map/ppermute | solution.py:38
  16.9 6.4 %collective-permute-start.3 = (bf16[8,32,240]{2,1,0:T(8,128)(2,1)S(1)}, bf16[8,32,240]{2,1,0:T(8,128)(2,1)S(1)}, u32[]{:S(2)}, u32[]{:S(2)}) collective-permute-start(bf16[8,32,240]{2,1,0:T(8,128)(2,1)S(1)} %get-tuple-element.16.refs_1_), channel_id=1, source_target_pairs={{0,3},{1,0},{2,1},{3,2},{4,7},{5,4},{6,5},{7,6},{8,11},{9,8},{10,9... | collective-permute-start | bytes 368648 | tf_op jit(solution)/shard_map/ppermute | solution.py:38
  18.6 9.0 %collective-permute-start.2 = (bf16[8,32,240]{2,1,0:T(8,128)(2,1)S(1)}, bf16[8,32,240]{2,1,0:T(8,128)(2,1)S(1)}, u32[]{:S(2)}, u32[]{:S(2)}) collective-permute-start(bf16[8,32,240]{2,1,0:T(8,128)(2,1)S(1)} %get-tuple-element.15.refs_0_), channel_id=1, source_target_pairs={{0,3},{1,0},{2,1},{3,2},{4,7},{5,4},{6,5},{7,6},{8,11},{9,8},{10,9... | collective-permute-start | bytes 368648 | tf_op jit(solution)/shard_map/ppermute | solution.py:38
  20.1 7.5 %collective-permute-start.5 = (bf16[8,32,240]{2,1,0:T(8,128)(2,1)S(1)}, bf16[8,32,240]{2,1,0:T(8,128)(2,1)S(1)}, u32[]{:S(2)}, u32[]{:S(2)}) collective-permute-start(bf16[8,32,240]{2,1,0:T(8,128)(2,1)S(1)} %get-tuple-element.16.refs_1_), channel_id=1, source_target_pairs={{0,1},{1,2},{2,3},{3,0},{4,5},{5,6},{6,7},{7,4},{8,9},{9,10},{10,1... | collective-permute-start | bytes 368648 | tf_op jit(solution)/shard_map/ppermute | solution.py:38
  22.4 6.8 %collective-permute-start.6 = (bf16[8,32,240]{2,1,0:T(8,128)(2,1)S(1)}, bf16[8,32,240]{2,1,0:T(8,128)(2,1)S(1)}, u32[]{:S(2)}, u32[]{:S(2)}) collective-permute-start(bf16[8,32,240]{2,1,0:T(8,128)(2,1)S(1)} %collective-permute-done.4.refs_4_), channel_id=1, source_target_pairs={{0,1},{1,2},{2,3},{3,0},{4,5},{5,6},{6,7},{7,4},{8,9},{9,10},{10,1... | collective-permute-start | bytes 368648 | tf_op jit(solution)/shard_map/ppermute | solution.py:38
  23.2 6.0 %collective-permute-start.7 = (bf16[8,32,240]{2,1,0:T(8,128)(2,1)S(1)}, bf16[8,32,240]{2,1,0:T(8,128)(2,1)S(1)}, u32[]{:S(2)}, u32[]{:S(2)}) collective-permute-start(bf16[8,32,240]{2,1,0:T(8,128)(2,1)S(1)} %collective-permute-done.3.refs_3_), channel_id=1, source_target_pairs={{0,3},{1,0},{2,1},{3,2},{4,7},{5,4},{6,5},{7,6},{8,11},{9,8},{10,9... | collective-permute-start | bytes 368648 | tf_op jit(solution)/shard_map/ppermute | solution.py:38
  27.6 1.6 %copy-start.4 = (s32[32,4]{0,1:T(4,128)S(1)}, s32[32,4]{0,1:T(4,128)}, u32[]{:S(2)}) copy-start(s32[32,4]{0,1:T(4,128)} %param.12) | copy-start | bytes 1540
  31.5 5.7 %collective-permute-start.8 = (bf16[4,32,240]{2,1,0:T(8,128)(2,1)S(1)}, bf16[4,32,240]{2,1,0:T(8,128)(2,1)S(1)}, u32[]{:S(2)}, u32[]{:S(2)}) collective-permute-start(bf16[4,32,240]{2,1,0:T(8,128)(2,1)S(1)} %get-tuple-element.20), channel_id=1, source_target_pairs={{0,1},{1,2},{2,3},{3,0},{4,5},{5,6},{6,7},{7,4},{8,9},{9,10},{10,1... | collective-permute-start | bytes 184328 | tf_op jit(solution)/shard_map/ppermute | solution.py:38
  32.1 7.1 %collective-permute-start.9 = (bf16[4,32,240]{2,1,0:T(8,128)(2,1)S(1)}, bf16[4,32,240]{2,1,0:T(8,128)(2,1)S(1)}, u32[]{:S(2)}, u32[]{:S(2)}) collective-permute-start(bf16[4,32,240]{2,1,0:T(8,128)(2,1)S(1)} %get-tuple-element.21), channel_id=1, source_target_pairs={{0,2},{1,3},{2,0},{3,1},{4,6},{5,7},{6,4},{7,5},{8,10},{9,11},{10,... | collective-permute-start | bytes 184328 | tf_op jit(solution)/shard_map/ppermute | solution.py:38
  36.2 4.3 %collective-permute-start.10 = (bf16[4,32,240]{2,1,0:T(8,128)(2,1)S(1)}, bf16[4,32,240]{2,1,0:T(8,128)(2,1)S(1)}, u32[]{:S(2)}, u32[]{:S(2)}) collective-permute-start(bf16[4,32,240]{2,1,0:T(8,128)(2,1)S(1)} %get-tuple-element.22), channel_id=1, source_target_pairs={{0,3},{1,0},{2,1},{3,2},{4,7},{5,4},{6,5},{7,6},{8,11},{9,8},{10,9... | collective-permute-start | bytes 184328 | tf_op jit(solution)/shard_map/ppermute | solution.py:38
  36.2 4.3 %copy-start.7 = (f32[128]{0:T(128)S(1)}, f32[128]{0:T(128)}, u32[]{:S(2)}) copy-start(f32[128]{0:T(128)} %constant.2.clone.scale_ref) | copy-start | bytes 1540

commit v5 on v3

--- a/solution.py
+++ b/solution.py
@@ -1,4 +1,3 @@
-import functools
 import math
 
 import jax
@@ -27,6 +26,8 @@
 LON_LIMIT = 52
 CODE_RATE = 10.0
 CODE_BASE = 120.0
+SUM_SCALE = 64.0
+SUM_FLOOR = 2.0**-126
 
 
 def shifted(value, step):
@@ -142,10 +143,8 @@
     return jnp.concatenate([high, middle_part, low], axis=0)
 
 
-def climate_kernel(
-    index_ref, extent_ref, count_ref, cross_ref, own_ref, inner_ref, low_ref, high_ref
-):
-    weights = weight_matrix(index_ref, extent_ref, count_ref)
+def climate_kernel(weights_ref, cross_ref, own_ref, inner_ref, low_ref, high_ref):
+    weights = weights_ref[...]
     for s in range(BINS):
         rows = jnp.concatenate([cross_ref[s], own_ref[s], inner_ref[s]], axis=0)
         rows = rows.reshape(ROWS * VARS, DEST_MERIDIANS)
@@ -155,21 +154,23 @@
         out_ref[s % HALF] = encode(value)
 
 
-def climate_code(index, extent, count, cross, own, inner):
-    smem = pl.BlockSpec(memory_space=pltpu.SMEM)
+def climate_code(*arrays):
     vmem = pl.BlockSpec(memory_space=pltpu.VMEM)
     return pl.pallas_call(
         climate_kernel,
-        in_specs=[smem] * 3 + [vmem] * 3,
+        in_specs=[vmem] * 4,
         out_specs=[vmem] * 2,
         out_shape=[jax.ShapeDtypeStruct((HALF, FLAT, DEST_MERIDIANS), jnp.bfloat16)] * 2,
         compiler_params=params(8),
         cost_estimate=cost(2),
         name="climate",
-    )(index, extent, count, cross, own, inner)
-
-
-def days_kernel(fore_ref, obs_ref, fore_out, obs_out, error_out):
+    )(*arrays)
+
+
+def days_kernel(
+    index_ref, extent_ref, count_ref, fore_ref, obs_ref, fore_out, obs_out, error_out, weights_out
+):
+    weights_out[...] = weight_matrix(index_ref, extent_ref, count_ref)
     slot = lax.axis_index("slot")
     for k in range(SLOTS):
         lead = lax.rem(slot + k, SLOTS)
@@ -186,18 +187,21 @@
         error_out[k] = lax.fori_loop(0, DAYS, step, zero, unroll=2)
 
 
-def relaid_days(fore, obs):
+def relaid_days(index, extent, count, fore, obs):
+    smem = pl.BlockSpec(memory_space=pltpu.SMEM)
     vmem = pl.BlockSpec(memory_space=pltpu.VMEM)
     grid = jax.ShapeDtypeStruct((SLOTS, DAYS, FLAT, DEST_MERIDIANS), jnp.bfloat16)
+    error = jax.ShapeDtypeStruct((SLOTS, FLAT, DEST_MERIDIANS), jnp.float32)
+    weights = jax.ShapeDtypeStruct((3 * FLAT, ROWS * VARS), jnp.bfloat16)
     return pl.pallas_call(
         days_kernel,
-        in_specs=[vmem] * 2,
-        out_specs=[vmem] * 3,
-        out_shape=[grid, grid, jax.ShapeDtypeStruct((SLOTS, FLAT, DEST_MERIDIANS), jnp.float32)],
+        in_specs=[smem] * 3 + [vmem] * 2,
+        out_specs=[vmem] * 4,
+        out_shape=[grid, grid, error, weights],
         compiler_params=params(16),
-        cost_estimate=cost(5),
+        cost_estimate=cost(2),
         name="days",
-    )(fore, obs)
+    )(index, extent, count, fore, obs)
 
 
 def decode_kernel(*refs):
@@ -219,7 +223,21 @@
     )(*codes)
 
 
-def lead_sums(k, bins_ref, clim_ref, fore_ref, obs_ref, error_ref, out_ref):
+def encode_sum(value):
+    scaled = value * SUM_SCALE
+    square = scaled * scaled
+    power = square * square * square
+    return jnp.where(value < 0, -power, power).astype(jnp.bfloat16)
+
+
+def decode_sum(code):
+    wide = code.astype(jnp.float32)
+    size = jnp.maximum(jnp.abs(wide), SUM_FLOOR)
+    root = jnp.exp2(jnp.log2(size) * (1.0 / 6.0)) * (1.0 / SUM_SCALE)
+    return jnp.where(wide < 0, -root, root)
+
+
+def lead_sums(k, bins_ref, clim_ref, fore_ref, obs_ref, error_ref, out_ref, kept):
     slot = lax.axis_index("slot")
     lead = lax.rem(slot + k, SLOTS)
     first = slot * BINS
@@ -239,40 +257,61 @@
             )
 
         zero = jnp.zeros((half, DEST_MERIDIANS), jnp.float32)
-        sums = lax.fori_loop(0, DAYS, step, (zero,) * 3, unroll=4)
+        sums = lax.fori_loop(0, DAYS, step, (zero,) * 3, unroll=8)
         for n, value in enumerate(sums):
-            out_ref[n + 1, some] = value
-    out_ref[0] = error_ref[k]
-
-
-def first_kernel(
-    k, bins_ref, near_ref, low_ref, high_ref, fore_ref, obs_ref, error_ref, out_ref, clim_ref
+            out_ref[n + 1, some] = kept(value)
+    out_ref[0] = kept(error_ref[k])
+
+
+def others_kernel(
+    bins_ref, near_ref, low_ref, high_ref, fore_ref, obs_ref, error_ref,
+    one_ref, two_ref, three_ref, clim_ref,
 ):
     clim_ref[: 2 * BINS] = near_ref[: 2 * BINS]
     clim_ref[3 * BINS :] = near_ref[2 * BINS :]
     clim_ref[2 * BINS : 2 * BINS + HALF] = decode(low_ref[...])
     clim_ref[2 * BINS + HALF : 3 * BINS] = decode(high_ref[...])
-    lead_sums(k, bins_ref, clim_ref, fore_ref, obs_ref, error_ref, out_ref)
-
-
-def skill_sums(k, bins, clim, fore, obs, error):
-    vmem = pl.BlockSpec(memory_space=pltpu.VMEM)
-    out = jax.ShapeDtypeStruct((4, FLAT, DEST_MERIDIANS), jnp.float32)
+    for k, out_ref in ((1, one_ref), (2, two_ref), (3, three_ref)):
+        lead_sums(k, bins_ref, clim_ref, fore_ref, obs_ref, error_ref, out_ref, encode_sum)
+
+
+def mine_kernel(bins_ref, clim_ref, fore_ref, obs_ref, error_ref, out_ref):
+    lead_sums(0, bins_ref, clim_ref, fore_ref, obs_ref, error_ref, out_ref, lambda value: value)
+
+
+def other_sums(bins, near, low, high, fore, obs, error):
+    vmem = pl.BlockSpec(memory_space=pltpu.VMEM)
+    code = jax.ShapeDtypeStruct((4, FLAT, DEST_MERIDIANS), jnp.bfloat16)
     whole = jax.ShapeDtypeStruct((SLOTS * BINS, FLAT, DEST_MERIDIANS), jnp.float32)
-    first = len(clim) > 1
-    return pl.pallas_call(
-        functools.partial(first_kernel if first else lead_sums, k),
-        in_specs=[pl.BlockSpec(memory_space=pltpu.SMEM)] + [vmem] * (3 + len(clim)),
-        out_specs=[vmem, vmem] if first else vmem,
-        out_shape=[out, whole] if first else out,
+    return pl.pallas_call(
+        others_kernel,
+        in_specs=[pl.BlockSpec(memory_space=pltpu.SMEM)] + [vmem] * 6,
+        out_specs=[vmem] * 4,
+        out_shape=[code, code, code, whole],
+        compiler_params=params(16),
+        cost_estimate=cost(3),
+        name="other_sums",
+    )(bins, near, low, high, fore, obs, error)
+
+
+def my_sums(bins, clim, fore, obs, error):
+    vmem = pl.BlockSpec(memory_space=pltpu.VMEM)
+    return pl.pallas_call(
+        mine_kernel,
+        in_specs=[pl.BlockSpec(memory_space=pltpu.SMEM)] + [vmem] * 4,
+        out_specs=vmem,
+        out_shape=jax.ShapeDtypeStruct((4, FLAT, DEST_MERIDIANS), jnp.float32),
         compiler_params=params(16),
         cost_estimate=cost(1),
-    )(bins, *clim, fore, obs, error)
+        name="my_sums",
+    )(bins, clim, fore, obs, error)
 
 
 def maps_kernel(scale_ref, one_ref, two_ref, three_ref, own_ref, rmse_ref, acc_ref):
     lat = lax.axis_index("lat")
-    total = own_ref[...] + one_ref[...] + two_ref[...] + three_ref[...]
+    total = own_ref[...]
+    for code_ref in (one_ref, two_ref, three_ref):
+        total = total + decode_sum(code_ref[...])
     line = lax.broadcasted_iota(jnp.int32, (FLAT, DEST_MERIDIANS), 0)
     scale = jnp.zeros((FLAT, DEST_MERIDIANS), jnp.float32)
     for t in range(TILE):
@@ -306,13 +345,14 @@
 def body(normals, index, extent, count, bins, prognosis, analysis):
     field = jnp.transpose(normals, (0, 2, 1, 3))
     own, cross_edge, inner_edge = lon_rows(field)
-    devices = lax.axis_size("lat")
-    meets = [(i, i + 1) for i in range(1, devices - 1, 2)]
-    meets += [(j, i) for i, j in meets]
-    cross = lax.ppermute(cross_edge, "lat", meets)
+    devices, slots = lax.axis_size("lat"), lax.axis_size("slot")
+    meets = [(i * slots + x, (i + 1) * slots + x) for i in range(1, devices - 1, 2) for x in range(slots)]
+    ends = [(i * slots + x, i * slots + x + 1) for i in (0, devices - 1) for x in range(0, slots, 2)]
+    meets = [pair for i, j in meets + ends for pair in ((i, j), (j, i))]
+    cross = lax.ppermute(cross_edge, ("lat", "slot"), meets)
     inner = lax.ppermute(inner_edge, "lat", [(i, i ^ 1) for i in range(devices)])
-    fore, obs, error = relaid_days(prognosis, analysis)
-    low, high = climate_code(index, extent, count, cross, own, inner)
+    fore, obs, error, weights = relaid_days(index, extent, count, prognosis, analysis)
+    low, high = climate_code(weights, cross, own, inner)
     left_low = shifted(low, 1)
     right_high = shifted(high, -1)
     left_high = shifted(high, 1)
@@ -321,11 +361,13 @@
     far_high = shifted(right_high, -1)
     near = decoded(low, high, right_low, right_high, left_low, left_high)
     wanted = jnp.transpose(bins)
-    to_two, clim = skill_sums(2, wanted, (near, far_low, far_high), fore, obs, error)
+    to_one, to_two, to_three, clim = other_sums(
+        wanted, near, far_low, far_high, fore, obs, error
+    )
     two = shifted(to_two, 2)
-    one = shifted(skill_sums(1, wanted, (clim,), fore, obs, error), 1)
-    three = shifted(skill_sums(3, wanted, (clim,), fore, obs, error), 3)
-    mine = skill_sums(0, wanted, (clim,), fore, obs, error)
+    one = shifted(to_one, 1)
+    three = shifted(to_three, 3)
+    mine = my_sums(wanted, clim, fore, obs, error)
     return tuple(maps(one, two, three, mine))
 
 

time: 43.7 us -> 39.3 us (0.90)
  the two profiles are of different devices: /device:TPU:112 before, /device:TPU:24 now
where the time goes in v5:
time: 39.3 us; the launch traced here: 39.2 us
  starting transfers between devices  17.3 us (44%)
  Pallas kernels  12.5 us (32%)
  waiting for transfers between devices  8.55 us (22%)
  between operations  0.76 us (2%)
    ppermute x9, starting transfers between devices, shifted(): lax.ppermute(value, 'slot', [(i, (i + step) % slots) for i in range(slots)])  13.6 us
    ppermute x9, waiting for transfers between devices, shifted(): lax.ppermute(value, 'slot', [(i, (i + step) % slots) for i in range(slots)])  7.47 us
    pallas_call x1, Pallas kernels, lon_rows(): pl.pallas_call(lon_kernel, in_specs=[hbm], out_specs=[vmem] * 3, out_shap...  4.78 us
    ppermute x1, starting transfers between devices, body(): cross = lax.ppermute(cross_edge, ('lat', 'slot'), meets)  3.74 us
    pallas_call x1, Pallas kernels, relaid_days(): pl.pallas_call(days_kernel, in_specs=[smem] * 3 + [vmem] * 2, out_specs=[...  2.41 us
    pallas_call x1, Pallas kernels, other_sums(): pl.pallas_call(others_kernel, in_specs=[pl.BlockSpec(memory_space=pltpu.S...  2.14 us
    pallas_call x1, Pallas kernels, maps(): pl.pallas_call(maps_kernel, in_specs=[pl.BlockSpec(memory_space=pltpu.SME...  1.35 us
    ppermute x1, waiting for transfers between devices, body(): cross = lax.ppermute(cross_edge, ('lat', 'slot'), meets)  1.08 us
  transfers between devices with their start and end apart: 11, of which 8 were waited for; matrix products, arithmetic and copies ran while one was open for 0% of the time, Pallas kernels for 10%

profile of v5, /device:TPU:24, one launch (start us, length us, event | category | flops | bytes accessed | tf_op | source)
XLA Modules:
  0.0 39.2 jit_solution(713802679411978841)
XLA Ops:
  0.7 4.8 %lon_rows.1 = (bf16[16,22,8,240]{3,2,1,0:T(8,128)(2,1)S(1)}, bf16[16,3,8,240]{3,2,1,0:T(8,128)(2,1)S(1)}, bf16[16,3,8,240]{3,2,1,0:T(8,128)(2,1)S(1)}) custom-call(bf16[16,22,8,1440]{3,2,1,0:T(8,128)(2,1)} %bitcast.4), custom_call_target="tpu_custom_call" | custom-call | bytes 18000000 | tf_op jit(solution)/shard_map/lon_rows/pallas_call | solution.py:90
  5.5 3.7 %collective-permute-start = (bf16[16,3,8,240]{3,2,1,0:T(8,128)(2,1)S(1)}, bf16[16,3,8,240]{3,2,1,0:T(8,128)(2,1)S(1)}, u32[]{:S(2)}, u32[]{:S(2)}) collective-permute-start(bf16[16,3,8,240]{3,2,1,0:T(8,128)(2,1)S(1)} %get-tuple-element.16), channel_id=1, source_target_pairs={{4,8},{8,4},{5,9},{9,5},{6,10},{10,6},{7,11},{11,7},{12,16},{16,12... | collective-permute-start | bytes 552968 | tf_op jit(solution)/shard_map/ppermute | solution.py:352
  9.2 0.0 collective-permute-start.1
  9.2 0.0 copy-done.3
  9.2 0.0 copy-done.4
  9.2 0.0 copy-done.5
  9.2 2.4 %days.1 = (bf16[4,32,32,240]{3,2,1,0:T(8,128)(2,1)S(1)}, bf16[4,32,32,240]{3,2,1,0:T(8,128)(2,1)S(1)}, f32[4,32,240]{2,1,0:T(8,128)S(1)}, bf16[96,224]{1,0:T(8,128)(2,1)S(1)}) custom-call(s32[4,10]{1,0:T(4,128)S(1)} %copy-done.3, f32[4,10]{1,0:T(4,128)S(1)} %copy-done.4, s32[4]{0:T(128)S(1)} %copy-done.5, bf16[32,4,8,4,240]{4,3,2,1,0:T(4,128)(2,1)S(1)} %copy-done, ...), custom_call_target="tpu_custom_call" | custom-call | bytes 6000000 | tf_op jit(solution)/shard_map/days/pallas_call | solution.py:196
  11.7 1.1 %collective-permute-done.cross_ref = bf16[16,3,8,240]{3,2,1,0:T(8,128)(2,1)S(1)} collective-permute-done((bf16[16,3,8,240]{3,2,1,0:T(8,128)(2,1)S(1)}, bf16[16,3,8,240]{3,2,1,0:T(8,128)(2,1)S(1)}, u32[]{:S(2)}, u32[]{:S(2)}) %collective-permute-start) | collective-permute-done | bytes 184352 | tf_op jit(solution)/shard_map/ppermute | solution.py:352
  12.7 0.0 collective-permute-done.1.inner_ref
  12.8 0.4 %climate.1 = (bf16[8,32,240]{2,1,0:T(8,128)(2,1)S(1)}, bf16[8,32,240]{2,1,0:T(8,128)(2,1)S(1)}) custom-call(bf16[96,224]{1,0:T(8,128)(2,1)S(1)} %get-tuple-element.15.weights_ref, bf16[16,3,8,240]{3,2,1,0:T(8,128)(2,1)S(1)} %collective-permute-done.cross_ref, bf16[16,22,8,240]{3,2,1,0:T(8,128)(2,1)S(1)} %get-tuple-element.17.own_ref, ...), custom_call_target="tpu_custom_call" | custom-call | bytes 6000000 | tf_op jit(solution)/shard_map/climate/pallas_call | solution.py:159
  13.2 1.6 %collective-permute-start.4 = (bf16[8,32,240]{2,1,0:T(8,128)(2,1)S(1)}, bf16[8,32,240]{2,1,0:T(8,128)(2,1)S(1)}, u32[]{:S(2)}, u32[]{:S(2)}) collective-permute-start(bf16[8,32,240]{2,1,0:T(8,128)(2,1)S(1)} %get-tuple-element.19.refs_0_), channel_id=1, source_target_pairs={{0,1},{1,2},{2,3},{3,0},{4,5},{5,6},{6,7},{7,4},{8,9},{9,10},{10,1... | collective-permute-start | bytes 368648 | tf_op jit(solution)/shard_map/ppermute | solution.py:35
  14.8 1.7 %collective-permute-start.3 = (bf16[8,32,240]{2,1,0:T(8,128)(2,1)S(1)}, bf16[8,32,240]{2,1,0:T(8,128)(2,1)S(1)}, u32[]{:S(2)}, u32[]{:S(2)}) collective-permute-start(bf16[8,32,240]{2,1,0:T(8,128)(2,1)S(1)} %get-tuple-element.20.refs_1_), channel_id=1, source_target_pairs={{0,3},{1,0},{2,1},{3,2},{4,7},{5,4},{6,5},{7,6},{8,11},{9,8},{10,9... | collective-permute-start | bytes 368648 | tf_op jit(solution)/shard_map/ppermute | solution.py:35
  16.5 1.5 %collective-permute-start.2 = (bf16[8,32,240]{2,1,0:T(8,128)(2,1)S(1)}, bf16[8,32,240]{2,1,0:T(8,128)(2,1)S(1)}, u32[]{:S(2)}, u32[]{:S(2)}) collective-permute-start(bf16[8,32,240]{2,1,0:T(8,128)(2,1)S(1)} %get-tuple-element.19.refs_0_), channel_id=1, source_target_pairs={{0,3},{1,0},{2,1},{3,2},{4,7},{5,4},{6,5},{7,6},{8,11},{9,8},{10,9... | collective-permute-start | bytes 368648 | tf_op jit(solution)/shard_map/ppermute | solution.py:35
  18.1 0.5 %collective-permute-start.5 = (bf16[8,32,240]{2,1,0:T(8,128)(2,1)S(1)}, bf16[8,32,240]{2,1,0:T(8,128)(2,1)S(1)}, u32[]{:S(2)}, u32[]{:S(2)}) collective-permute-start(bf16[8,32,240]{2,1,0:T(8,128)(2,1)S(1)} %get-tuple-element.20.refs_1_), channel_id=1, source_target_pairs={{0,1},{1,2},{2,3},{3,0},{4,5},{5,6},{6,7},{7,4},{8,9},{9,10},{10,1... | collective-permute-start | bytes 368648 | tf_op jit(solution)/shard_map/ppermute | solution.py:35
  18.5 0.9 %collective-permute-done.4.refs_4_ = bf16[8,32,240]{2,1,0:T(8,128)(2,1)S(1)} collective-permute-done((bf16[8,32,240]{2,1,0:T(8,128)(2,1)S(1)}, bf16[8,32,240]{2,1,0:T(8,128)(2,1)S(1)}, u32[]{:S(2)}, u32[]{:S(2)}) %collective-permute-start.4) | collective-permute-done | bytes 122912 | tf_op jit(solution)/shard_map/ppermute | solution.py:35
  19.5 0.5 %collective-permute-start.6 = (bf16[8,32,240]{2,1,0:T(8,128)(2,1)S(1)}, bf16[8,32,240]{2,1,0:T(8,128)(2,1)S(1)}, u32[]{:S(2)}, u32[]{:S(2)}) collective-permute-start(bf16[8,32,240]{2,1,0:T(8,128)(2,1)S(1)} %collective-permute-done.4.refs_4_), channel_id=1, source_target_pairs={{0,1},{1,2},{2,3},{3,0},{4,5},{5,6},{6,7},{7,4},{8,9},{9,10},{10,1... | collective-permute-start | bytes 368648 | tf_op jit(solution)/shard_map/ppermute | solution.py:35
  20.0 1.2 %collective-permute-done.3.refs_3_ = bf16[8,32,240]{2,1,0:T(8,128)(2,1)S(1)} collective-permute-done((bf16[8,32,240]{2,1,0:T(8,128)(2,1)S(1)}, bf16[8,32,240]{2,1,0:T(8,128)(2,1)S(1)}, u32[]{:S(2)}, u32[]{:S(2)}) %collective-permute-start.3) | collective-permute-done | bytes 122912 | tf_op jit(solution)/shard_map/ppermute | solution.py:35
  21.1 2.5 %collective-permute-start.7 = (bf16[8,32,240]{2,1,0:T(8,128)(2,1)S(1)}, bf16[8,32,240]{2,1,0:T(8,128)(2,1)S(1)}, u32[]{:S(2)}, u32[]{:S(2)}) collective-permute-start(bf16[8,32,240]{2,1,0:T(8,128)(2,1)S(1)} %collective-permute-done.3.refs_3_), channel_id=1, source_target_pairs={{0,3},{1,0},{2,1},{3,2},{4,7},{5,4},{6,5},{7,6},{8,11},{9,8},{10,9... | collective-permute-start | bytes 368648 | tf_op jit(solution)/shard_map/ppermute | solution.py:35
  23.7 0.0 collective-permute-done.2.refs_2_
  23.7 1.0 %collective-permute-done.5.refs_5_ = bf16[8,32,240]{2,1,0:T(8,128)(2,1)S(1)} collective-permute-done((bf16[8,32,240]{2,1,0:T(8,128)(2,1)S(1)}, bf16[8,32,240]{2,1,0:T(8,128)(2,1)S(1)}, u32[]{:S(2)}, u32[]{:S(2)}) %collective-permute-start.5) | collective-permute-done | bytes 122912 | tf_op jit(solution)/shard_map/ppermute | solution.py:35
  24.7 0.4 %decode.1.near_ref = f32[48,32,240]{2,1,0:T(8,128)S(1)} custom-call(bf16[8,32,240]{2,1,0:T(8,128)(2,1)S(1)} %get-tuple-element.19.refs_0_, bf16[8,32,240]{2,1,0:T(8,128)(2,1)S(1)} %get-tuple-element.20.refs_1_, bf16[8,32,240]{2,1,0:T(8,128)(2,1)S(1)} %collective-permute-done.2.refs_2_, bf16[8,32,240]{2,1,0:T(8,128)(2,1)S(1)} %collective-permute-done.3.refs_3_, ...), custom_call_target="tpu_custom_call" | custom-call | bytes 3000000 | tf_op jit(solution)/shard_map/decode/pallas_call | solution.py:215
  25.1 1.0 %collective-permute-done.6.low_ref = bf16[8,32,240]{2,1,0:T(8,128)(2,1)S(1)} collective-permute-done((bf16[8,32,240]{2,1,0:T(8,128)(2,1)S(1)}, bf16[8,32,240]{2,1,0:T(8,128)(2,1)S(1)}, u32[]{:S(2)}, u32[]{:S(2)}) %collective-permute-start.6) | collective-permute-done | bytes 122912 | tf_op jit(solution)/shard_map/ppermute | solution.py:35
  26.1 0.1 collective-permute-done.7.high_ref
  26.2 2.1 %other_sums.1 = (bf16[4,32,240]{2,1,0:T(8,128)(2,1)S(1)}, bf16[4,32,240]{2,1,0:T(8,128)(2,1)S(1)}, bf16[4,32,240]{2,1,0:T(8,128)(2,1)S(1)}, f32[64,32,240]{2,1,0:T(8,128)S(1)}) custom-call(s32[4,32]{1,0:T(4,128)S(1)} %bitcast.2, f32[48,32,240]{2,1,0:T(8,128)S(1)} %decode.1.near_ref, bf16[8,32,240]{2,1,0:T(8,128)(2,1)S(1)} %collective-permute-done.6.low_ref, ...), custom_call_target="tpu_custom_call" | custom-call | bytes 9000000 | tf_op jit(solution)/shard_map/other_sums/pallas_call | solution.py:286
  28.4 1.3 %collective-permute-start.8 = (bf16[4,32,240]{2,1,0:T(8,128)(2,1)S(1)}, bf16[4,32,240]{2,1,0:T(8,128)(2,1)S(1)}, u32[]{:S(2)}, u32[]{:S(2)}) collective-permute-start(bf16[4,32,240]{2,1,0:T(8,128)(2,1)S(1)} %get-tuple-element.24), channel_id=1, source_target_pairs={{0,1},{1,2},{2,3},{3,0},{4,5},{5,6},{6,7},{7,4},{8,9},{9,10},{10,1... | collective-permute-start | bytes 184328 | tf_op jit(solution)/shard_map/ppermute | solution.py:35
  29.6 3.9 %collective-permute-start.9 = (bf16[4,32,240]{2,1,0:T(8,128)(2,1)S(1)}, bf16[4,32,240]{2,1,0:T(8,128)(2,1)S(1)}, u32[]{:S(2)}, u32[]{:S(2)}) collective-permute-start(bf16[4,32,240]{2,1,0:T(8,128)(2,1)S(1)} %get-tuple-element.25), channel_id=1, source_target_pairs={{0,2},{1,3},{2,0},{3,1},{4,6},{5,7},{6,4},{7,5},{8,10},{9,11},{10,... | collective-permute-start | bytes 184328 | tf_op jit(solution)/shard_map/ppermute | solution.py:35
  33.6 0.0 collective-permute-start.10
  33.6 1.0 %my_sums.1.own_ref = f32[4,32,240]{2,1,0:T(8,128)S(1)} custom-call(s32[4,32]{1,0:T(4,128)S(1)} %bitcast.3, f32[64,32,240]{2,1,0:T(8,128)S(1)} %get-tuple-element.27.clim_ref, bf16[4,32,32,240]{3,2,1,0:T(8,128)(2,1)S(1)} %get-tuple-element.21.fore_ref, bf16[4,32,32,240]{3,2,1,0:T(8,128)(2,1)S(1)} %get-tuple-element.22.obs_ref, ...), custom_call_target="tpu_custom_call" | custom-call | bytes 3000000 | tf_op jit(solution)/shard_map/my_sums/pallas_call | solution.py:299
  34.5 0.0 collective-permute-done.8.one_ref
  34.5 1.9 %collective-permute-done.9.two_ref = bf16[4,32,240]{2,1,0:T(8,128)(2,1)S(1)} collective-permute-done((bf16[4,32,240]{2,1,0:T(8,128)(2,1)S(1)}, bf16[4,32,240]{2,1,0:T(8,128)(2,1)S(1)}, u32[]{:S(2)}, u32[]{:S(2)}) %collective-permute-start.9) | collective-permute-done | bytes 61472 | tf_op jit(solution)/shard_map/ppermute | solution.py:35
  36.5 1.3 %collective-permute-done.10.three_ref = bf16[4,32,240]{2,1,0:T(8,128)(2,1)S(1)} collective-permute-done((bf16[4,32,240]{2,1,0:T(8,128)(2,1)S(1)}, bf16[4,32,240]{2,1,0:T(8,128)(2,1)S(1)}, u32[]{:S(2)}, u32[]{:S(2)}) %collective-permute-start.10) | collective-permute-done | bytes 61472 | tf_op jit(solution)/shard_map/ppermute | solution.py:35
  37.8 1.3 %maps.1 = (f32[1,8,4,240]{3,2,1,0:T(4,128)}, f32[1,8,4,240]{3,2,1,0:T(4,128)}) custom-call(f32[128]{0:T(128)S(1)} %copy-done.6, bf16[4,32,240]{2,1,0:T(8,128)(2,1)S(1)} %collective-permute-done.8.one_ref, bf16[4,32,240]{2,1,0:T(8,128)(2,1)S(1)} %collective-permute-done.9.two_ref, bf16[4,32,240]{2,1,0:T(8,128)(2,1)S(1)} %collective-permute-done.10.three_ref, ...), custom_call_target="tpu_custom_call" | custom-call | bytes 3000000 | tf_op jit(solution)/shard_map/maps/pallas_call | solution.py:334
  (11 shorter events, 0.0 us)
Async XLA Ops:
  0.6 8.6 %copy-start = (bf16[32,4,8,4,240]{4,3,2,1,0:T(4,128)(2,1)S(1)}, bf16[32,4,8,4,240]{4,3,2,1,0:T(4,128)(2,1)}, u32[]{:S(2)}) copy-start(bf16[32,4,8,4,240]{4,3,2,1,0:T(4,128)(2,1)} %fore_ref.1) | copy-start | bytes 5898244
  0.6 8.6 %copy-start.1 = (bf16[32,4,8,4,240]{4,3,2,1,0:T(4,128)(2,1)S(1)}, bf16[32,4,8,4,240]{4,3,2,1,0:T(4,128)(2,1)}, u32[]{:S(2)}) copy-start(bf16[32,4,8,4,240]{4,3,2,1,0:T(4,128)(2,1)} %obs_ref.1) | copy-start | bytes 5898244
  0.7 8.6 %copy-start.3 = (s32[4,10]{1,0:T(4,128)S(1)}, s32[4,10]{1,0:T(4,128)}, u32[]{:S(2)}) copy-start(s32[4,10]{1,0:T(4,128)} %index_ref.1) | copy-start | bytes 484
  0.7 8.6 %copy-start.4 = (f32[4,10]{1,0:T(4,128)S(1)}, f32[4,10]{1,0:T(4,128)}, u32[]{:S(2)}) copy-start(f32[4,10]{1,0:T(4,128)} %extent_ref.1) | copy-start | bytes 484
  0.7 8.6 %copy-start.5 = (s32[4]{0:T(128)S(1)}, s32[4]{0:T(128)}, u32[]{:S(2)}) copy-start(s32[4]{0:T(128)} %count_ref.1) | copy-start | bytes 52
  5.5 7.3 %collective-permute-start = (bf16[16,3,8,240]{3,2,1,0:T(8,128)(2,1)S(1)}, bf16[16,3,8,240]{3,2,1,0:T(8,128)(2,1)S(1)}, u32[]{:S(2)}, u32[]{:S(2)}) collective-permute-start(bf16[16,3,8,240]{3,2,1,0:T(8,128)(2,1)S(1)} %get-tuple-element.16), channel_id=1, source_target_pairs={{4,8},{8,4},{5,9},{9,5},{6,10},{10,6},{7,11},{11,7},{12,16},{16,12... | collective-permute-start | bytes 552968 | tf_op jit(solution)/shard_map/ppermute | solution.py:352
  9.2 3.5 %collective-permute-start.1 = (bf16[16,3,8,240]{3,2,1,0:T(8,128)(2,1)S(1)}, bf16[16,3,8,240]{3,2,1,0:T(8,128)(2,1)S(1)}, u32[]{:S(2)}, u32[]{:S(2)}) collective-permute-start(bf16[16,3,8,240]{3,2,1,0:T(8,128)(2,1)S(1)} %get-tuple-element.18), channel_id=1, source_target_pairs={{0,4},{4,0},{8,12},{12,8},{16,20},{20,16},{24,28},{28,24},{32,36},... | collective-permute-start | bytes 552968 | tf_op jit(solution)/shard_map/ppermute | solution.py:353
  12.8 13.5 %copy-start.2 = (s32[32,4]{0,1:T(4,128)S(1)}, s32[32,4]{0,1:T(4,128)}, u32[]{:S(2)}) copy-start(s32[32,4]{0,1:T(4,128)} %param.12) | copy-start | bytes 1540
  13.2 6.2 %collective-permute-start.4 = (bf16[8,32,240]{2,1,0:T(8,128)(2,1)S(1)}, bf16[8,32,240]{2,1,0:T(8,128)(2,1)S(1)}, u32[]{:S(2)}, u32[]{:S(2)}) collective-permute-start(bf16[8,32,240]{2,1,0:T(8,128)(2,1)S(1)} %get-tuple-element.19.refs_0_), channel_id=1, source_target_pairs={{0,1},{1,2},{2,3},{3,0},{4,5},{5,6},{6,7},{7,4},{8,9},{9,10},{10,1... | collective-permute-start | bytes 368648 | tf_op jit(solution)/shard_map/ppermute | solution.py:35
  14.8 6.4 %collective-permute-start.3 = (bf16[8,32,240]{2,1,0:T(8,128)(2,1)S(1)}, bf16[8,32,240]{2,1,0:T(8,128)(2,1)S(1)}, u32[]{:S(2)}, u32[]{:S(2)}) collective-permute-start(bf16[8,32,240]{2,1,0:T(8,128)(2,1)S(1)} %get-tuple-element.20.refs_1_), channel_id=1, source_target_pairs={{0,3},{1,0},{2,1},{3,2},{4,7},{5,4},{6,5},{7,6},{8,11},{9,8},{10,9... | collective-permute-start | bytes 368648 | tf_op jit(solution)/shard_map/ppermute | solution.py:35
  16.5 7.2 %collective-permute-start.2 = (bf16[8,32,240]{2,1,0:T(8,128)(2,1)S(1)}, bf16[8,32,240]{2,1,0:T(8,128)(2,1)S(1)}, u32[]{:S(2)}, u32[]{:S(2)}) collective-permute-start(bf16[8,32,240]{2,1,0:T(8,128)(2,1)S(1)} %get-tuple-element.19.refs_0_), channel_id=1, source_target_pairs={{0,3},{1,0},{2,1},{3,2},{4,7},{5,4},{6,5},{7,6},{8,11},{9,8},{10,9... | collective-permute-start | bytes 368648 | tf_op jit(solution)/shard_map/ppermute | solution.py:35
  18.1 6.6 %collective-permute-start.5 = (bf16[8,32,240]{2,1,0:T(8,128)(2,1)S(1)}, bf16[8,32,240]{2,1,0:T(8,128)(2,1)S(1)}, u32[]{:S(2)}, u32[]{:S(2)}) collective-permute-start(bf16[8,32,240]{2,1,0:T(8,128)(2,1)S(1)} %get-tuple-element.20.refs_1_), channel_id=1, source_target_pairs={{0,1},{1,2},{2,3},{3,0},{4,5},{5,6},{6,7},{7,4},{8,9},{9,10},{10,1... | collective-permute-start | bytes 368648 | tf_op jit(solution)/shard_map/ppermute | solution.py:35
  19.5 6.6 %collective-permute-start.6 = (bf16[8,32,240]{2,1,0:T(8,128)(2,1)S(1)}, bf16[8,32,240]{2,1,0:T(8,128)(2,1)S(1)}, u32[]{:S(2)}, u32[]{:S(2)}) collective-permute-start(bf16[8,32,240]{2,1,0:T(8,128)(2,1)S(1)} %collective-permute-done.4.refs_4_), channel_id=1, source_target_pairs={{0,1},{1,2},{2,3},{3,0},{4,5},{5,6},{6,7},{7,4},{8,9},{9,10},{10,1... | collective-permute-start | bytes 368648 | tf_op jit(solution)/shard_map/ppermute | solution.py:35
  21.1 5.1 %collective-permute-start.7 = (bf16[8,32,240]{2,1,0:T(8,128)(2,1)S(1)}, bf16[8,32,240]{2,1,0:T(8,128)(2,1)S(1)}, u32[]{:S(2)}, u32[]{:S(2)}) collective-permute-start(bf16[8,32,240]{2,1,0:T(8,128)(2,1)S(1)} %collective-permute-done.3.refs_3_), channel_id=1, source_target_pairs={{0,3},{1,0},{2,1},{3,2},{4,7},{5,4},{6,5},{7,6},{8,11},{9,8},{10,9... | collective-permute-start | bytes 368648 | tf_op jit(solution)/shard_map/ppermute | solution.py:35
  28.4 6.2 %collective-permute-start.8 = (bf16[4,32,240]{2,1,0:T(8,128)(2,1)S(1)}, bf16[4,32,240]{2,1,0:T(8,128)(2,1)S(1)}, u32[]{:S(2)}, u32[]{:S(2)}) collective-permute-start(bf16[4,32,240]{2,1,0:T(8,128)(2,1)S(1)} %get-tuple-element.24), channel_id=1, source_target_pairs={{0,1},{1,2},{2,3},{3,0},{4,5},{5,6},{6,7},{7,4},{8,9},{9,10},{10,1... | collective-permute-start | bytes 184328 | tf_op jit(solution)/shard_map/ppermute | solution.py:35
  29.6 6.9 %collective-permute-start.9 = (bf16[4,32,240]{2,1,0:T(8,128)(2,1)S(1)}, bf16[4,32,240]{2,1,0:T(8,128)(2,1)S(1)}, u32[]{:S(2)}, u32[]{:S(2)}) collective-permute-start(bf16[4,32,240]{2,1,0:T(8,128)(2,1)S(1)} %get-tuple-element.25), channel_id=1, source_target_pairs={{0,2},{1,3},{2,0},{3,1},{4,6},{5,7},{6,4},{7,5},{8,10},{9,11},{10,... | collective-permute-start | bytes 184328 | tf_op jit(solution)/shard_map/ppermute | solution.py:35
  33.6 4.3 %collective-permute-start.10 = (bf16[4,32,240]{2,1,0:T(8,128)(2,1)S(1)}, bf16[4,32,240]{2,1,0:T(8,128)(2,1)S(1)}, u32[]{:S(2)}, u32[]{:S(2)}) collective-permute-start(bf16[4,32,240]{2,1,0:T(8,128)(2,1)S(1)} %get-tuple-element.26), channel_id=1, source_target_pairs={{0,3},{1,0},{2,1},{3,2},{4,7},{5,4},{6,5},{7,6},{8,11},{9,8},{10,9... | collective-permute-start | bytes 184328 | tf_op jit(solution)/shard_map/ppermute | solution.py:35
  33.6 4.3 %copy-start.6 = (f32[128]{0:T(128)S(1)}, f32[128]{0:T(128)}, u32[]{:S(2)}) copy-start(f32[128]{0:T(128)} %constant.2.clone.scale_ref) | copy-start | bytes 1540

commit v6 on v4

--- a/solution.py
+++ b/solution.py
@@ -80,7 +80,8 @@
     fill_table(table_buf)
     for copy, n, some in jobs:
         copy.wait()
-        outs[n][some] = lon_mean(buf[n, some], table_buf[...])
+        for s in range(some.start, some.stop, 4):
+            outs[n][s : s + 4] = lon_mean(buf[n, s : s + 4], table_buf[...])
 
 
 def edge_rows(field):
@@ -101,19 +102,27 @@
     )(field)
 
 
-def mid_kernel(field_ref, out_ref, buf, table_buf, sems):
+def mid_kernel(
+    field_ref, index_ref, extent_ref, count_ref, out_ref, weights_ref,
+    buf, table_buf, index_buf, extent_buf, count_buf, sems, small_sems,
+):
     parts = sems.shape[0]
     size = BINS // parts
     block = 2
+    lists = ((index_ref, index_buf), (extent_ref, extent_buf), (count_ref, count_buf))
+    loads = [pltpu.make_async_copy(a, b, small_sems.at[n]) for n, (a, b) in enumerate(lists)]
     copies = []
     for n in range(parts):
         some = pl.ds(n * size, size)
-        copy = pltpu.make_async_copy(
-            field_ref.at[some, pl.ds(EDGE, MID)], buf.at[some], sems.at[n]
+        copies.append(
+            pltpu.make_async_copy(field_ref.at[some, pl.ds(EDGE, MID)], buf.at[some], sems.at[n])
         )
+    for copy in loads + copies:
         copy.start()
-        copies.append(copy)
     fill_table(table_buf)
+    for copy in loads:
+        copy.wait()
+    weights_ref[...] = weight_matrix(index_buf, extent_buf, count_buf)
     for first in range(0, BINS, block):
         if first % size == 0:
             copies[first // size].wait()
@@ -121,22 +130,31 @@
         out_ref[some] = lon_mean(buf[some], table_buf[...])
 
 
-def mid_rows(field):
+def mid_rows(field, index, extent, count):
     parts = 4
+    hbm = pl.BlockSpec(memory_space=pl.ANY)
+    vmem = pl.BlockSpec(memory_space=pltpu.VMEM)
     return pl.pallas_call(
         mid_kernel,
-        in_specs=[pl.BlockSpec(memory_space=pl.ANY)],
-        out_specs=pl.BlockSpec(memory_space=pltpu.VMEM),
-        out_shape=jax.ShapeDtypeStruct((BINS, MID, VARS, DEST_MERIDIANS), jnp.bfloat16),
+        in_specs=[hbm] * 4,
+        out_specs=[vmem] * 2,
+        out_shape=[
+            jax.ShapeDtypeStruct((BINS, MID, VARS, DEST_MERIDIANS), jnp.bfloat16),
+            jax.ShapeDtypeStruct((3 * FLAT, ROWS * VARS), jnp.bfloat16),
+        ],
         scratch_shapes=[
             pltpu.VMEM((BINS, MID, VARS, SRC_LON), jnp.bfloat16),
             pltpu.VMEM((SRC_LON, DEST_MERIDIANS), jnp.bfloat16),
+            pltpu.SMEM((TILE, OVER), jnp.int32),
+            pltpu.SMEM((TILE, OVER), jnp.float32),
+            pltpu.SMEM((TILE,), jnp.int32),
             pltpu.SemaphoreType.DMA((parts,)),
+            pltpu.SemaphoreType.DMA((3,)),
         ],
         compiler_params=params(MID_LIMIT),
         cost_estimate=cost(4),
         name="mid_rows",
-    )(field)
+    )(field, index, extent, count)
 
 
 def encode(value):
@@ -182,13 +200,12 @@
 
 
 def climate_kernel(
-    index_ref, extent_ref, count_ref, cross_ref, cross_own, mid_ref, inner_own, inner_ref,
-    low_ref, high_ref,
+    weights_ref, cross_ref, cross_own, mid_ref, inner_own, inner_ref, low_ref, high_ref
 ):
-    weights = weight_matrix(index_ref, extent_ref, count_ref)
+    weights = weights_ref[...]
+    refs = (cross_ref, cross_own, mid_ref, inner_own, inner_ref)
     for s in range(BINS):
-        parts = (cross_ref, cross_own, mid_ref, inner_own, inner_ref)
-        rows = jnp.concatenate([ref[s] for ref in parts], axis=0)
+        rows = jnp.concatenate([ref[s] for ref in refs], axis=0)
         rows = rows.reshape(ROWS * VARS, DEST_MERIDIANS)
         parts = jnp.dot(weights, rows, preferred_element_type=jnp.float32)
         value = parts[:FLAT] + parts[FLAT : 2 * FLAT] + parts[2 * FLAT :]
@@ -197,15 +214,14 @@
 
 
 def climate_code(*arrays):
-    smem = pl.BlockSpec(memory_space=pltpu.SMEM)
     vmem = pl.BlockSpec(memory_space=pltpu.VMEM)
     return pl.pallas_call(
         climate_kernel,
-        in_specs=[smem] * 3 + [vmem] * 5,
+        in_specs=[vmem] * 6,
         out_specs=[vmem] * 2,
         out_shape=[jax.ShapeDtypeStruct((HALF, FLAT, DEST_MERIDIANS), jnp.bfloat16)] * 2,
         compiler_params=params(8),
-        cost_estimate=cost(2),
+        cost_estimate=cost(1),
         name="climate",
     )(*arrays)
 
@@ -218,8 +234,8 @@
         def step(d, squared):
             fore = fore_ref[d, lead].astype(jnp.float32).reshape(FLAT, DEST_MERIDIANS)
             obs = obs_ref[d, lead].astype(jnp.float32).reshape(FLAT, DEST_MERIDIANS)
-            fore_out[k, d] = fore.astype(jnp.bfloat16)
-            obs_out[k, d] = obs.astype(jnp.bfloat16)
+            fore_out[k, d] = fore
+            obs_out[k, d] = obs
             error = fore - obs
             return squared + error * error
 
@@ -229,14 +245,14 @@
 
 def relaid_days(fore, obs):
     vmem = pl.BlockSpec(memory_space=pltpu.VMEM)
-    grid = jax.ShapeDtypeStruct((SLOTS, DAYS, FLAT, DEST_MERIDIANS), jnp.bfloat16)
+    grid = jax.ShapeDtypeStruct((SLOTS, DAYS, FLAT, DEST_MERIDIANS), jnp.float32)
     return pl.pallas_call(
         days_kernel,
         in_specs=[vmem] * 2,
         out_specs=[vmem] * 3,
         out_shape=[grid, grid, jax.ShapeDtypeStruct((SLOTS, FLAT, DEST_MERIDIANS), jnp.float32)],
-        compiler_params=params(16),
-        cost_estimate=cost(5),
+        compiler_params=params(20),
+        cost_estimate=cost(2),
         name="days",
     )(fore, obs)
 
@@ -285,8 +301,8 @@
         def step(d, sums):
             cross, fore_sq, true_sq = sums
             clim = clim_ref[(bins_ref[lead, d] - first) & (SLOTS * BINS - 1), some]
-            fore_anom = fore_ref[k, d, some].astype(jnp.float32) - clim
-            true_anom = obs_ref[k, d, some].astype(jnp.float32) - clim
+            fore_anom = fore_ref[k, d, some] - clim
+            true_anom = obs_ref[k, d, some] - clim
             return (
                 cross + fore_anom * true_anom,
                 fore_sq + fore_anom * fore_anom,
@@ -294,7 +310,7 @@
             )
 
         zero = jnp.zeros((half, DEST_MERIDIANS), jnp.float32)
-        sums = lax.fori_loop(0, DAYS, step, (zero,) * 3, unroll=4)
+        sums = lax.fori_loop(0, DAYS, step, (zero,) * 3, unroll=8)
         for n, value in enumerate(sums):
             out_ref[n + 1, some] = kept(value)
     out_ref[0] = kept(error_ref[k])
@@ -382,13 +398,14 @@
 def body(normals, index, extent, count, bins, prognosis, analysis):
     field = jnp.transpose(normals, (0, 2, 1, 3))
     cross_own, inner_own = edge_rows(field)
-    devices = lax.axis_size("lat")
-    meets = [(i, i + 1) for i in range(1, devices - 1, 2)]
-    meets += [(j, i) for i, j in meets]
-    cross = lax.ppermute(cross_own, "lat", meets)
+    devices, slots = lax.axis_size("lat"), lax.axis_size("slot")
+    meets = [(i * slots + x, (i + 1) * slots + x) for i in range(1, devices - 1, 2) for x in range(slots)]
+    meets += [(i * slots + x, i * slots + x + 1) for i in (0, devices - 1) for x in range(0, slots, 2)]
+    meets = [pair for i, j in meets for pair in ((i, j), (j, i))]
+    cross = lax.ppermute(cross_own, ("lat", "slot"), meets)
     inner = lax.ppermute(inner_own, "lat", [(i, i ^ 1) for i in range(devices)])
-    mid = mid_rows(field)
-    low, high = climate_code(index, extent, count, cross, cross_own, mid, inner_own, inner)
+    mid, weights = mid_rows(field, index, extent, count)
+    low, high = climate_code(weights, cross, cross_own, mid, inner_own, inner)
     left_low = shifted(low, 1)
     right_high = shifted(high, -1)
     left_high = shifted(high, 1)

time: 42 us -> 38.6 us (0.919)
  starting transfers between devices: 18.9 us -> 17 us
  Pallas kernels: 15.4 us -> 13.7 us
    ppermute x1, starting transfers between devices: 5.56 us -> 3.74 us  [body(): cross = lax.ppermute(cross_own, ('lat', 'slot'), meets)]
    pallas_call x2, Pallas kernels: 5.22 us -> 4.37 us  [the longest x1 3.92 us: mid_rows(): pl.pallas_call(mid_kernel, in_specs=[hbm] * 4, out_specs=[vmem] * 2, out_...]
  transfers between devices with their start and end apart: 11 -> 11, of which waited for: 5 -> 5; matrix products, arithmetic and copies ran while one was open for 0% -> 0% of each run, Pallas kernels for 16% -> 17%
where the time goes in v6:
time: 38.6 us; the launch traced here: 38.4 us
  starting transfers between devices  17 us (44%)
  Pallas kernels  13.7 us (35%)
  waiting for transfers between devices  6.91 us (18%)
  between operations  0.82 us (2%)
    ppermute x9, starting transfers between devices, shifted(): lax.ppermute(value, 'slot', [(i, (i + step) % slots) for i in range(slots)])  13.2 us
    ppermute x9, waiting for transfers between devices, shifted(): lax.ppermute(value, 'slot', [(i, (i + step) % slots) for i in range(slots)])  6.91 us
    pallas_call x1, Pallas kernels, mid_rows(): pl.pallas_call(mid_kernel, in_specs=[hbm] * 4, out_specs=[vmem] * 2, out_...  3.92 us
    ppermute x1, starting transfers between devices, body(): cross = lax.ppermute(cross_own, ('lat', 'slot'), meets)  3.74 us
    pallas_call x1, Pallas kernels, edge_rows(): pl.pallas_call(edge_kernel, in_specs=[pl.BlockSpec(memory_space=pl.ANY)],...  3.31 us
    pallas_call x1, Pallas kernels, other_sums(): pl.pallas_call(others_kernel, in_specs=[pl.BlockSpec(memory_space=pltpu.S...  2 us
    pallas_call x1, Pallas kernels, maps(): pl.pallas_call(maps_kernel, in_specs=[pl.BlockSpec(memory_space=pltpu.SME...  1.35 us
    pallas_call x1, Pallas kernels, relaid_days(): pl.pallas_call(days_kernel, in_specs=[vmem] * 2, out_specs=[vmem] * 3, ou...  1.31 us
  transfers between devices with their start and end apart: 11, of which 5 were waited for; matrix products, arithmetic and copies ran while one was open for 0% of the time, Pallas kernels for 17%

profile of v6, /device:TPU:24, one launch (start us, length us, event | category | flops | bytes accessed | tf_op | source)
XLA Modules:
  0.0 38.4 jit_solution(481985708853703876)
XLA Ops:
  0.7 3.3 %edge_rows.1 = (bf16[16,3,8,240]{3,2,1,0:T(8,128)(2,1)}, bf16[16,3,8,240]{3,2,1,0:T(8,128)(2,1)}) custom-call(bf16[16,22,8,1440]{3,2,1,0:T(8,128)(2,1)} %bitcast.4), custom_call_target="tpu_custom_call" | custom-call | bytes 6000000 | tf_op jit(solution)/shard_map/edge_rows/pallas_call | solution.py:89
  4.0 3.7 %collective-permute-start = (bf16[16,3,8,240]{3,2,1,0:T(8,128)(2,1)}, bf16[16,3,8,240]{3,2,1,0:T(8,128)(2,1)S(1)}, u32[]{:S(2)}, u32[]{:S(2)}) collective-permute-start(bf16[16,3,8,240]{3,2,1,0:T(8,128)(2,1)} %get-tuple-element.16.cross_own), channel_id=1, source_target_pairs={{4,8},{8,4},{5,9},{9,5},{6,10},{10,6},{7,11},{11,7},{12,16},{16,12... | collective-permute-start | bytes 552968 | tf_op jit(solution)/shard_map/ppermute | solution.py:405
  7.7 0.0 collective-permute-start.1
  7.7 0.0 copy-start
  7.8 0.0 copy-start.1
  7.8 3.9 %mid_rows.1 = (bf16[16,16,8,240]{3,2,1,0:T(8,128)(2,1)S(1)}, bf16[96,224]{1,0:T(8,128)(2,1)S(1)}) custom-call(bf16[16,22,8,1440]{3,2,1,0:T(8,128)(2,1)} %bitcast.5, s32[4,10]{1,0:T(4,128)S(1)} %copy-done.5, f32[4,10]{1,0:T(4,128)S(1)} %copy-done.6, s32[4]{0:T(128)S(1)} %copy-done.7), custom_call_target="tpu_custom_call" | custom-call | bytes 12000000 | tf_op jit(solution)/shard_map/mid_rows/pallas_call | solution.py:137
  11.7 0.0 collective-permute-done.cross_ref
  11.7 0.0 collective-permute-done.1.inner_ref
  11.7 0.5 %climate.1 = (bf16[8,32,240]{2,1,0:T(8,128)(2,1)S(1)}, bf16[8,32,240]{2,1,0:T(8,128)(2,1)S(1)}) custom-call(bf16[96,224]{1,0:T(8,128)(2,1)S(1)} %get-tuple-element.15.weights_ref, bf16[16,3,8,240]{3,2,1,0:T(8,128)(2,1)S(1)} %collective-permute-done.cross_ref, bf16[16,3,8,240]{3,2,1,0:T(8,128)(2,1)S(1)} %copy-done.2, ...), custom_call_target="tpu_custom_call" | custom-call | bytes 3000000 | tf_op jit(solution)/shard_map/climate/pallas_call | solution.py:218
  12.2 1.6 %collective-permute-start.4 = (bf16[8,32,240]{2,1,0:T(8,128)(2,1)S(1)}, bf16[8,32,240]{2,1,0:T(8,128)(2,1)S(1)}, u32[]{:S(2)}, u32[]{:S(2)}) collective-permute-start(bf16[8,32,240]{2,1,0:T(8,128)(2,1)S(1)} %get-tuple-element.19.refs_0_), channel_id=1, source_target_pairs={{0,1},{1,2},{2,3},{3,0},{4,5},{5,6},{6,7},{7,4},{8,9},{9,10},{10,1... | collective-permute-start | bytes 368648 | tf_op jit(solution)/shard_map/ppermute | solution.py:38
  13.8 1.8 %collective-permute-start.3 = (bf16[8,32,240]{2,1,0:T(8,128)(2,1)S(1)}, bf16[8,32,240]{2,1,0:T(8,128)(2,1)S(1)}, u32[]{:S(2)}, u32[]{:S(2)}) collective-permute-start(bf16[8,32,240]{2,1,0:T(8,128)(2,1)S(1)} %get-tuple-element.20.refs_1_), channel_id=1, source_target_pairs={{0,3},{1,0},{2,1},{3,2},{4,7},{5,4},{6,5},{7,6},{8,11},{9,8},{10,9... | collective-permute-start | bytes 368648 | tf_op jit(solution)/shard_map/ppermute | solution.py:38
  15.5 1.5 %collective-permute-start.2 = (bf16[8,32,240]{2,1,0:T(8,128)(2,1)S(1)}, bf16[8,32,240]{2,1,0:T(8,128)(2,1)S(1)}, u32[]{:S(2)}, u32[]{:S(2)}) collective-permute-start(bf16[8,32,240]{2,1,0:T(8,128)(2,1)S(1)} %get-tuple-element.19.refs_0_), channel_id=1, source_target_pairs={{0,3},{1,0},{2,1},{3,2},{4,7},{5,4},{6,5},{7,6},{8,11},{9,8},{10,9... | collective-permute-start | bytes 368648 | tf_op jit(solution)/shard_map/ppermute | solution.py:38
  17.1 0.5 %collective-permute-start.5 = (bf16[8,32,240]{2,1,0:T(8,128)(2,1)S(1)}, bf16[8,32,240]{2,1,0:T(8,128)(2,1)S(1)}, u32[]{:S(2)}, u32[]{:S(2)}) collective-permute-start(bf16[8,32,240]{2,1,0:T(8,128)(2,1)S(1)} %get-tuple-element.20.refs_1_), channel_id=1, source_target_pairs={{0,1},{1,2},{2,3},{3,0},{4,5},{5,6},{6,7},{7,4},{8,9},{9,10},{10,1... | collective-permute-start | bytes 368648 | tf_op jit(solution)/shard_map/ppermute | solution.py:38
  17.5 1.8 %collective-permute-done.4.refs_4_ = bf16[8,32,240]{2,1,0:T(8,128)(2,1)S(1)} collective-permute-done((bf16[8,32,240]{2,1,0:T(8,128)(2,1)S(1)}, bf16[8,32,240]{2,1,0:T(8,128)(2,1)S(1)}, u32[]{:S(2)}, u32[]{:S(2)}) %collective-permute-start.4) | collective-permute-done | bytes 122912 | tf_op jit(solution)/shard_map/ppermute | solution.py:38
  19.4 0.3 collective-permute-start.6
  19.6 0.5 %collective-permute-done.3.refs_3_ = bf16[8,32,240]{2,1,0:T(8,128)(2,1)S(1)} collective-permute-done((bf16[8,32,240]{2,1,0:T(8,128)(2,1)S(1)}, bf16[8,32,240]{2,1,0:T(8,128)(2,1)S(1)}, u32[]{:S(2)}, u32[]{:S(2)}) %collective-permute-start.3) | collective-permute-done | bytes 122912 | tf_op jit(solution)/shard_map/ppermute | solution.py:38
  20.1 3.0 %collective-permute-start.7 = (bf16[8,32,240]{2,1,0:T(8,128)(2,1)S(1)}, bf16[8,32,240]{2,1,0:T(8,128)(2,1)S(1)}, u32[]{:S(2)}, u32[]{:S(2)}) collective-permute-start(bf16[8,32,240]{2,1,0:T(8,128)(2,1)S(1)} %collective-permute-done.3.refs_3_), channel_id=1, source_target_pairs={{0,3},{1,0},{2,1},{3,2},{4,7},{5,4},{6,5},{7,6},{8,11},{9,8},{10,9... | collective-permute-start | bytes 368648 | tf_op jit(solution)/shard_map/ppermute | solution.py:38
  23.1 1.3 %days.1 = (f32[4,32,32,240]{3,2,1,0:T(8,128)S(1)}, f32[4,32,32,240]{3,2,1,0:T(8,128)S(1)}, f32[4,32,240]{2,1,0:T(8,128)S(1)}) custom-call(bf16[32,4,8,4,240]{4,3,2,1,0:T(4,128)(2,1)S(1)} %copy-done, bf16[32,4,8,4,240]{4,3,2,1,0:T(4,128)(2,1)S(1)} %copy-done.1), custom_call_target="tpu_custom_call" | custom-call | bytes 6000000 | tf_op jit(solution)/shard_map/days/pallas_call | solution.py:249
  24.4 0.0 copy-start.4
  24.4 0.0 collective-permute-done.2.refs_2_
  24.4 0.0 collective-permute-done.5.refs_5_
  24.4 0.4 %decode.1.near_ref = f32[48,32,240]{2,1,0:T(8,128)S(1)} custom-call(bf16[8,32,240]{2,1,0:T(8,128)(2,1)S(1)} %get-tuple-element.19.refs_0_, bf16[8,32,240]{2,1,0:T(8,128)(2,1)S(1)} %get-tuple-element.20.refs_1_, bf16[8,32,240]{2,1,0:T(8,128)(2,1)S(1)} %collective-permute-done.2.refs_2_, bf16[8,32,240]{2,1,0:T(8,128)(2,1)S(1)} %collective-permute-done.3.refs_3_, ...), custom_call_target="tpu_custom_call" | custom-call | bytes 3000000 | tf_op jit(solution)/shard_map/decode/pallas_call | solution.py:268
  24.9 1.3 %collective-permute-done.6.low_ref = bf16[8,32,240]{2,1,0:T(8,128)(2,1)S(1)} collective-permute-done((bf16[8,32,240]{2,1,0:T(8,128)(2,1)S(1)}, bf16[8,32,240]{2,1,0:T(8,128)(2,1)S(1)}, u32[]{:S(2)}, u32[]{:S(2)}) %collective-permute-start.6) | collective-permute-done | bytes 122912 | tf_op jit(solution)/shard_map/ppermute | solution.py:38
  26.1 0.0 collective-permute-done.7.high_ref
  26.1 2.0 %other_sums.1 = (bf16[4,32,240]{2,1,0:T(8,128)(2,1)S(1)}, bf16[4,32,240]{2,1,0:T(8,128)(2,1)S(1)}, bf16[4,32,240]{2,1,0:T(8,128)(2,1)S(1)}, f32[64,32,240]{2,1,0:T(8,128)S(1)}) custom-call(s32[4,32]{1,0:T(4,128)S(1)} %bitcast.2, f32[48,32,240]{2,1,0:T(8,128)S(1)} %decode.1.near_ref, bf16[8,32,240]{2,1,0:T(8,128)(2,1)S(1)} %collective-permute-done.6.low_ref, ...), custom_call_target="tpu_custom_call" | custom-call | bytes 9000000 | tf_op jit(solution)/shard_map/other_sums/pallas_call | solution.py:339
  28.1 0.5 %collective-permute-start.8 = (bf16[4,32,240]{2,1,0:T(8,128)(2,1)S(1)}, bf16[4,32,240]{2,1,0:T(8,128)(2,1)S(1)}, u32[]{:S(2)}, u32[]{:S(2)}) collective-permute-start(bf16[4,32,240]{2,1,0:T(8,128)(2,1)S(1)} %get-tuple-element.24), channel_id=1, source_target_pairs={{0,1},{1,2},{2,3},{3,0},{4,5},{5,6},{6,7},{7,4},{8,9},{9,10},{10,1... | collective-permute-start | bytes 184328 | tf_op jit(solution)/shard_map/ppermute | solution.py:38
  28.7 4.1 %collective-permute-start.9 = (bf16[4,32,240]{2,1,0:T(8,128)(2,1)S(1)}, bf16[4,32,240]{2,1,0:T(8,128)(2,1)S(1)}, u32[]{:S(2)}, u32[]{:S(2)}) collective-permute-start(bf16[4,32,240]{2,1,0:T(8,128)(2,1)S(1)} %get-tuple-element.25), channel_id=1, source_target_pairs={{0,2},{1,3},{2,0},{3,1},{4,6},{5,7},{6,4},{7,5},{8,10},{9,11},{10,... | collective-permute-start | bytes 184328 | tf_op jit(solution)/shard_map/ppermute | solution.py:38
  32.8 0.9 %my_sums.1.own_ref = f32[4,32,240]{2,1,0:T(8,128)S(1)} custom-call(s32[4,32]{1,0:T(4,128)S(1)} %bitcast.3, f32[64,32,240]{2,1,0:T(8,128)S(1)} %get-tuple-element.27.clim_ref, f32[4,32,32,240]{3,2,1,0:T(8,128)S(1)} %get-tuple-element.21.fore_ref, f32[4,32,32,240]{3,2,1,0:T(8,128)S(1)} %get-tuple-element.22.obs_ref, f32[4,32,240]{2,1,0:T(8,128)S(1)} %get-tuple-element.23.error_ref), custom_call_target="tpu_custom_call" | custom-call | bytes 3000000 | tf_op jit(solution)/shard_map/my_sums/pallas_call | solution.py:352
  33.7 0.0 collective-permute-done.8.one_ref
  33.8 2.0 %collective-permute-done.9.two_ref = bf16[4,32,240]{2,1,0:T(8,128)(2,1)S(1)} collective-permute-done((bf16[4,32,240]{2,1,0:T(8,128)(2,1)S(1)}, bf16[4,32,240]{2,1,0:T(8,128)(2,1)S(1)}, u32[]{:S(2)}, u32[]{:S(2)}) %collective-permute-start.9) | collective-permute-done | bytes 61472 | tf_op jit(solution)/shard_map/ppermute | solution.py:38
  35.7 1.3 %collective-permute-done.10.three_ref = bf16[4,32,240]{2,1,0:T(8,128)(2,1)S(1)} collective-permute-done((bf16[4,32,240]{2,1,0:T(8,128)(2,1)S(1)}, bf16[4,32,240]{2,1,0:T(8,128)(2,1)S(1)}, u32[]{:S(2)}, u32[]{:S(2)}) %collective-permute-start.10) | collective-permute-done | bytes 61472 | tf_op jit(solution)/shard_map/ppermute | solution.py:38
  37.1 1.3 %maps.1 = (f32[1,8,4,240]{3,2,1,0:T(4,128)}, f32[1,8,4,240]{3,2,1,0:T(4,128)}) custom-call(f32[128]{0:T(128)S(1)} %copy-done.8, bf16[4,32,240]{2,1,0:T(8,128)(2,1)S(1)} %collective-permute-done.8.one_ref, bf16[4,32,240]{2,1,0:T(8,128)(2,1)S(1)} %collective-permute-done.9.two_ref, bf16[4,32,240]{2,1,0:T(8,128)(2,1)S(1)} %collective-permute-done.10.three_ref, ...), custom_call_target="tpu_custom_call" | custom-call | bytes 3000000 | tf_op jit(solution)/shard_map/maps/pallas_call | solution.py:387
  (16 shorter events, 0.0 us)
Async XLA Ops:
  0.6 7.1 %copy-start.5 = (s32[4,10]{1,0:T(4,128)S(1)}, s32[4,10]{1,0:T(4,128)}, u32[]{:S(2)}) copy-start(s32[4,10]{1,0:T(4,128)} %index_ref.1) | copy-start | bytes 484
  0.6 7.1 %copy-start.6 = (f32[4,10]{1,0:T(4,128)S(1)}, f32[4,10]{1,0:T(4,128)}, u32[]{:S(2)}) copy-start(f32[4,10]{1,0:T(4,128)} %extent_ref.1) | copy-start | bytes 484
  0.7 7.1 %copy-start.7 = (s32[4]{0:T(128)S(1)}, s32[4]{0:T(128)}, u32[]{:S(2)}) copy-start(s32[4]{0:T(128)} %count_ref.1) | copy-start | bytes 52
  4.0 7.7 %collective-permute-start = (bf16[16,3,8,240]{3,2,1,0:T(8,128)(2,1)}, bf16[16,3,8,240]{3,2,1,0:T(8,128)(2,1)S(1)}, u32[]{:S(2)}, u32[]{:S(2)}) collective-permute-start(bf16[16,3,8,240]{3,2,1,0:T(8,128)(2,1)} %get-tuple-element.16.cross_own), channel_id=1, source_target_pairs={{4,8},{8,4},{5,9},{9,5},{6,10},{10,6},{7,11},{11,7},{12,16},{16,12... | collective-permute-start | bytes 552968 | tf_op jit(solution)/shard_map/ppermute | solution.py:405
  7.7 4.0 %copy-start.2 = (bf16[16,3,8,240]{3,2,1,0:T(8,128)(2,1)S(1)}, bf16[16,3,8,240]{3,2,1,0:T(8,128)(2,1)}, u32[]{:S(2)}) copy-start(bf16[16,3,8,240]{3,2,1,0:T(8,128)(2,1)} %get-tuple-element.16.cross_own) | copy-start | bytes 552964
  7.7 4.0 %copy-start.3 = (bf16[16,3,8,240]{3,2,1,0:T(8,128)(2,1)S(1)}, bf16[16,3,8,240]{3,2,1,0:T(8,128)(2,1)}, u32[]{:S(2)}) copy-start(bf16[16,3,8,240]{3,2,1,0:T(8,128)(2,1)} %get-tuple-element.18.inner_own) | copy-start | bytes 552964
  7.7 4.0 %collective-permute-start.1 = (bf16[16,3,8,240]{3,2,1,0:T(8,128)(2,1)}, bf16[16,3,8,240]{3,2,1,0:T(8,128)(2,1)S(1)}, u32[]{:S(2)}, u32[]{:S(2)}) collective-permute-start(bf16[16,3,8,240]{3,2,1,0:T(8,128)(2,1)} %get-tuple-element.18.inner_own), channel_id=1, source_target_pairs={{0,4},{4,0},{8,12},{12,8},{16,20},{20,16},{24,28},{28,24},{32,36},... | collective-permute-start | bytes 552968 | tf_op jit(solution)/shard_map/ppermute | solution.py:406
  7.7 15.3 %copy-start = (bf16[32,4,8,4,240]{4,3,2,1,0:T(4,128)(2,1)S(1)}, bf16[32,4,8,4,240]{4,3,2,1,0:T(4,128)(2,1)}, u32[]{:S(2)}) copy-start(bf16[32,4,8,4,240]{4,3,2,1,0:T(4,128)(2,1)} %fore_ref.1) | copy-start | bytes 5898244
  7.8 15.3 %copy-start.1 = (bf16[32,4,8,4,240]{4,3,2,1,0:T(4,128)(2,1)S(1)}, bf16[32,4,8,4,240]{4,3,2,1,0:T(4,128)(2,1)}, u32[]{:S(2)}) copy-start(bf16[32,4,8,4,240]{4,3,2,1,0:T(4,128)(2,1)} %obs_ref.1) | copy-start | bytes 5898244
  12.2 7.2 %collective-permute-start.4 = (bf16[8,32,240]{2,1,0:T(8,128)(2,1)S(1)}, bf16[8,32,240]{2,1,0:T(8,128)(2,1)S(1)}, u32[]{:S(2)}, u32[]{:S(2)}) collective-permute-start(bf16[8,32,240]{2,1,0:T(8,128)(2,1)S(1)} %get-tuple-element.19.refs_0_), channel_id=1, source_target_pairs={{0,1},{1,2},{2,3},{3,0},{4,5},{5,6},{6,7},{7,4},{8,9},{9,10},{10,1... | collective-permute-start | bytes 368648 | tf_op jit(solution)/shard_map/ppermute | solution.py:38
  13.8 6.4 %collective-permute-start.3 = (bf16[8,32,240]{2,1,0:T(8,128)(2,1)S(1)}, bf16[8,32,240]{2,1,0:T(8,128)(2,1)S(1)}, u32[]{:S(2)}, u32[]{:S(2)}) collective-permute-start(bf16[8,32,240]{2,1,0:T(8,128)(2,1)S(1)} %get-tuple-element.20.refs_1_), channel_id=1, source_target_pairs={{0,3},{1,0},{2,1},{3,2},{4,7},{5,4},{6,5},{7,6},{8,11},{9,8},{10,9... | collective-permute-start | bytes 368648 | tf_op jit(solution)/shard_map/ppermute | solution.py:38
  15.5 8.9 %collective-permute-start.2 = (bf16[8,32,240]{2,1,0:T(8,128)(2,1)S(1)}, bf16[8,32,240]{2,1,0:T(8,128)(2,1)S(1)}, u32[]{:S(2)}, u32[]{:S(2)}) collective-permute-start(bf16[8,32,240]{2,1,0:T(8,128)(2,1)S(1)} %get-tuple-element.19.refs_0_), channel_id=1, source_target_pairs={{0,3},{1,0},{2,1},{3,2},{4,7},{5,4},{6,5},{7,6},{8,11},{9,8},{10,9... | collective-permute-start | bytes 368648 | tf_op jit(solution)/shard_map/ppermute | solution.py:38
  17.1 7.4 %collective-permute-start.5 = (bf16[8,32,240]{2,1,0:T(8,128)(2,1)S(1)}, bf16[8,32,240]{2,1,0:T(8,128)(2,1)S(1)}, u32[]{:S(2)}, u32[]{:S(2)}) collective-permute-start(bf16[8,32,240]{2,1,0:T(8,128)(2,1)S(1)} %get-tuple-element.20.refs_1_), channel_id=1, source_target_pairs={{0,1},{1,2},{2,3},{3,0},{4,5},{5,6},{6,7},{7,4},{8,9},{9,10},{10,1... | collective-permute-start | bytes 368648 | tf_op jit(solution)/shard_map/ppermute | solution.py:38
  19.4 6.8 %collective-permute-start.6 = (bf16[8,32,240]{2,1,0:T(8,128)(2,1)S(1)}, bf16[8,32,240]{2,1,0:T(8,128)(2,1)S(1)}, u32[]{:S(2)}, u32[]{:S(2)}) collective-permute-start(bf16[8,32,240]{2,1,0:T(8,128)(2,1)S(1)} %collective-permute-done.4.refs_4_), channel_id=1, source_target_pairs={{0,1},{1,2},{2,3},{3,0},{4,5},{5,6},{6,7},{7,4},{8,9},{9,10},{10,1... | collective-permute-start | bytes 368648 | tf_op jit(solution)/shard_map/ppermute | solution.py:38
  20.1 6.0 %collective-permute-start.7 = (bf16[8,32,240]{2,1,0:T(8,128)(2,1)S(1)}, bf16[8,32,240]{2,1,0:T(8,128)(2,1)S(1)}, u32[]{:S(2)}, u32[]{:S(2)}) collective-permute-start(bf16[8,32,240]{2,1,0:T(8,128)(2,1)S(1)} %collective-permute-done.3.refs_3_), channel_id=1, source_target_pairs={{0,3},{1,0},{2,1},{3,2},{4,7},{5,4},{6,5},{7,6},{8,11},{9,8},{10,9... | collective-permute-start | bytes 368648 | tf_op jit(solution)/shard_map/ppermute | solution.py:38
  24.4 1.7 %copy-start.4 = (s32[32,4]{0,1:T(4,128)S(1)}, s32[32,4]{0,1:T(4,128)}, u32[]{:S(2)}) copy-start(s32[32,4]{0,1:T(4,128)} %param.12) | copy-start | bytes 1540
  28.1 5.6 %collective-permute-start.8 = (bf16[4,32,240]{2,1,0:T(8,128)(2,1)S(1)}, bf16[4,32,240]{2,1,0:T(8,128)(2,1)S(1)}, u32[]{:S(2)}, u32[]{:S(2)}) collective-permute-start(bf16[4,32,240]{2,1,0:T(8,128)(2,1)S(1)} %get-tuple-element.24), channel_id=1, source_target_pairs={{0,1},{1,2},{2,3},{3,0},{4,5},{5,6},{6,7},{7,4},{8,9},{9,10},{10,1... | collective-permute-start | bytes 184328 | tf_op jit(solution)/shard_map/ppermute | solution.py:38
  28.7 7.1 %collective-permute-start.9 = (bf16[4,32,240]{2,1,0:T(8,128)(2,1)S(1)}, bf16[4,32,240]{2,1,0:T(8,128)(2,1)S(1)}, u32[]{:S(2)}, u32[]{:S(2)}) collective-permute-start(bf16[4,32,240]{2,1,0:T(8,128)(2,1)S(1)} %get-tuple-element.25), channel_id=1, source_target_pairs={{0,2},{1,3},{2,0},{3,1},{4,6},{5,7},{6,4},{7,5},{8,10},{9,11},{10,... | collective-permute-start | bytes 184328 | tf_op jit(solution)/shard_map/ppermute | solution.py:38
  32.8 4.3 %collective-permute-start.10 = (bf16[4,32,240]{2,1,0:T(8,128)(2,1)S(1)}, bf16[4,32,240]{2,1,0:T(8,128)(2,1)S(1)}, u32[]{:S(2)}, u32[]{:S(2)}) collective-permute-start(bf16[4,32,240]{2,1,0:T(8,128)(2,1)S(1)} %get-tuple-element.26), channel_id=1, source_target_pairs={{0,3},{1,0},{2,1},{3,2},{4,7},{5,4},{6,5},{7,6},{8,11},{9,8},{10,9... | collective-permute-start | bytes 184328 | tf_op jit(solution)/shard_map/ppermute | solution.py:38
  32.8 4.3 %copy-start.8 = (f32[128]{0:T(128)S(1)}, f32[128]{0:T(128)}, u32[]{:S(2)}) copy-start(f32[128]{0:T(128)} %constant.2.clone.scale_ref) | copy-start | bytes 1540

commit v7 on v6

--- a/solution.py
+++ b/solution.py
@@ -25,7 +25,7 @@
 DAYS = 32
 SLOTS = 4
 FLAT = VARS * TILE
-EDGE_LIMIT = 57
+EDGE_LIMIT = 52
 MID_LIMIT = 50
 CODE_RATE = 10.0
 CODE_BASE = 120.0
@@ -165,6 +165,7 @@
 def decode(code):
     wide = code.astype(jnp.float32)
     size = (jnp.log2(jnp.abs(wide)) + CODE_BASE) * (1.0 / CODE_RATE)
+    size = jnp.where(jnp.abs(wide) > 2.0**-CODE_BASE, size, 0.0)
     return jnp.where(wide < 0, -size, size)
 
 
@@ -287,6 +288,7 @@
     wide = code.astype(jnp.float32)
     size = jnp.maximum(jnp.abs(wide), SUM_FLOOR)
     root = jnp.exp2(jnp.log2(size) * (1.0 / 6.0)) * (1.0 / SUM_SCALE)
+    root = jnp.where(wide == 0, 0.0, root)
     return jnp.where(wide < 0, -root, root)
 
 
@@ -310,7 +312,7 @@
             )
 
         zero = jnp.zeros((half, DEST_MERIDIANS), jnp.float32)
-        sums = lax.fori_loop(0, DAYS, step, (zero,) * 3, unroll=8)
+        sums = lax.fori_loop(0, DAYS, step, (zero,) * 3, unroll=16)
         for n, value in enumerate(sums):
             out_ref[n + 1, some] = kept(value)
     out_ref[0] = kept(error_ref[k])
@@ -328,7 +330,15 @@
         lead_sums(k, bins_ref, clim_ref, fore_ref, obs_ref, error_ref, out_ref, encode_sum)
 
 
-def mine_kernel(bins_ref, clim_ref, fore_ref, obs_ref, error_ref, out_ref):
+def mine_kernel(
+    bins_ref, scale_ref, clim_ref, fore_ref, obs_ref, error_ref, out_ref, scale_out
+):
+    lat = lax.axis_index("lat")
+    line = lax.broadcasted_iota(jnp.int32, (FLAT, DEST_MERIDIANS), 0)
+    scale = jnp.zeros((FLAT, DEST_MERIDIANS), jnp.float32)
+    for t in range(TILE):
+        scale = jnp.where(line % TILE == t, scale_ref[lat * TILE + t], scale)
+    scale_out[...] = scale
     lead_sums(0, bins_ref, clim_ref, fore_ref, obs_ref, error_ref, out_ref, lambda value: value)
 
 
@@ -347,52 +357,53 @@
     )(bins, near, low, high, fore, obs, error)
 
 
-def my_sums(bins, clim, fore, obs, error):
-    vmem = pl.BlockSpec(memory_space=pltpu.VMEM)
-    return pl.pallas_call(
-        mine_kernel,
-        in_specs=[pl.BlockSpec(memory_space=pltpu.SMEM)] + [vmem] * 4,
-        out_specs=vmem,
-        out_shape=jax.ShapeDtypeStruct((4, FLAT, DEST_MERIDIANS), jnp.float32),
-        compiler_params=params(16),
-        cost_estimate=cost(1),
-        name="my_sums",
-    )(bins, clim, fore, obs, error)
-
-
-def maps_kernel(scale_ref, one_ref, two_ref, three_ref, own_ref, rmse_ref, acc_ref):
-    lat = lax.axis_index("lat")
-    total = own_ref[...]
-    for code_ref in (one_ref, two_ref, three_ref):
-        total = total + decode_sum(code_ref[...])
-    line = lax.broadcasted_iota(jnp.int32, (FLAT, DEST_MERIDIANS), 0)
-    scale = jnp.zeros((FLAT, DEST_MERIDIANS), jnp.float32)
-    for t in range(TILE):
-        scale = jnp.where(line % TILE == t, scale_ref[lat * TILE + t], scale)
-    days = DAYS * SLOTS
-    rmse = jnp.sqrt(scale * total[0] / days)
-    acc = total[1] / jnp.sqrt(total[2] * total[3] + 1e-06)
-    rmse_ref[0] = rmse.reshape(VARS, TILE, DEST_MERIDIANS)
-    acc_ref[0] = acc.reshape(VARS, TILE, DEST_MERIDIANS)
-
-
-def maps(one, two, three, own):
+def lat_weights():
     phi = (np.arange(DEST_PARALLELS, dtype=np.float32) + np.float32(0.5)) * np.float32(
         math.pi / DEST_PARALLELS
     ) - np.float32(0.5 * math.pi)
     cosine = np.cos(phi).astype(np.float32)
-    scale = jnp.asarray(cosine / cosine.mean(dtype=np.float32))
+    return jnp.asarray(cosine / cosine.mean(dtype=np.float32))
+
+
+def my_sums(bins, clim, fore, obs, error):
+    smem = pl.BlockSpec(memory_space=pltpu.SMEM)
+    vmem = pl.BlockSpec(memory_space=pltpu.VMEM)
+    return pl.pallas_call(
+        mine_kernel,
+        in_specs=[smem] * 2 + [vmem] * 4,
+        out_specs=[vmem] * 2,
+        out_shape=[
+            jax.ShapeDtypeStruct((4, FLAT, DEST_MERIDIANS), jnp.float32),
+            jax.ShapeDtypeStruct((FLAT, DEST_MERIDIANS), jnp.float32),
+        ],
+        compiler_params=params(20),
+        cost_estimate=cost(1),
+        name="my_sums",
+    )(bins, lat_weights(), clim, fore, obs, error)
+
+
+def maps_kernel(one_ref, two_ref, three_ref, own_ref, scale_ref, rmse_ref, acc_ref):
+    total = own_ref[...]
+    for code_ref in (one_ref, two_ref, three_ref):
+        total = total + decode_sum(code_ref[...])
+    rmse = jnp.sqrt(scale_ref[...] * total[0] / (DAYS * SLOTS))
+    acc = total[1] / jnp.sqrt(total[2] * total[3] + 1e-06)
+    rmse_ref[0] = rmse.reshape(VARS, TILE, DEST_MERIDIANS)
+    acc_ref[0] = acc.reshape(VARS, TILE, DEST_MERIDIANS)
+
+
+def maps(*arrays):
     vmem = pl.BlockSpec(memory_space=pltpu.VMEM)
     shape = jax.ShapeDtypeStruct((1, VARS, TILE, DEST_MERIDIANS), jnp.float32)
     return pl.pallas_call(
         maps_kernel,
-        in_specs=[pl.BlockSpec(memory_space=pltpu.SMEM)] + [vmem] * 4,
+        in_specs=[vmem] * 5,
         out_specs=[vmem] * 2,
         out_shape=[shape] * 2,
         compiler_params=params(8),
         cost_estimate=cost(1),
         name="maps",
-    )(scale, one, two, three, own)
+    )(*arrays)
 
 
 def body(normals, index, extent, count, bins, prognosis, analysis):
@@ -421,8 +432,8 @@
     two = shifted(to_two, 2)
     one = shifted(to_one, 1)
     three = shifted(to_three, 3)
-    mine = my_sums(wanted, clim, fore, obs, error)
-    return tuple(maps(one, two, three, mine))
+    mine, scale = my_sums(wanted, clim, fore, obs, error)
+    return tuple(maps(one, two, three, mine, scale))
 
 
 def solution(mesh):

time: 38.6 us -> 37.2 us (0.964)
  Pallas kernels: 13.7 us -> 12.5 us
    pallas_call x1, Pallas kernels: 3.31 us -> 2.64 us  [edge_rows(): pl.pallas_call(edge_kernel, in_specs=[pl.BlockSpec(memory_space=pl.ANY)],...]
    pallas_call x2, Pallas kernels: 2.27 us -> 1.73 us  [the longest x1 0.9 us: my_sums(): pl.pallas_call(mine_kernel, in_specs=[smem] * 2 + [vmem] * 4, out_specs=[...]
  transfers between devices with their start and end apart: 11 -> 11, of which waited for: 5 -> 5; matrix products, arithmetic and copies ran while one was open for 0% -> 0% of each run, Pallas kernels for 17% -> 18%
where the time goes in v7:
time: 37.2 us; the launch traced here: 37.1 us
  starting transfers between devices  17 us (46%)
  Pallas kernels  12.5 us (34%)
  waiting for transfers between devices  6.82 us (18%)
  between operations  0.8 us (2%)
    ppermute x9, starting transfers between devices, shifted(): lax.ppermute(value, 'slot', [(i, (i + step) % slots) for i in range(slots)])  13.2 us
    ppermute x9, waiting for transfers between devices, shifted(): lax.ppermute(value, 'slot', [(i, (i + step) % slots) for i in range(slots)])  6.82 us
    pallas_call x1, Pallas kernels, mid_rows(): pl.pallas_call(mid_kernel, in_specs=[hbm] * 4, out_specs=[vmem] * 2, out_...  3.92 us
    ppermute x1, starting transfers between devices, body(): cross = lax.ppermute(cross_own, ('lat', 'slot'), meets)  3.74 us
    pallas_call x1, Pallas kernels, edge_rows(): pl.pallas_call(edge_kernel, in_specs=[pl.BlockSpec(memory_space=pl.ANY)],...  2.64 us
    pallas_call x1, Pallas kernels, other_sums(): pl.pallas_call(others_kernel, in_specs=[pl.BlockSpec(memory_space=pltpu.S...  1.9 us
    pallas_call x1, Pallas kernels, relaid_days(): pl.pallas_call(days_kernel, in_specs=[vmem] * 2, out_specs=[vmem] * 3, ou...  1.31 us
    pallas_call x1, Pallas kernels, my_sums(): pl.pallas_call(mine_kernel, in_specs=[smem] * 2 + [vmem] * 4, out_specs=[...  0.9 us
  transfers between devices with their start and end apart: 11, of which 5 were waited for; matrix products, arithmetic and copies ran while one was open for 0% of the time, Pallas kernels for 18%

profile of v7, /device:TPU:24, one launch (start us, length us, event | category | flops | bytes accessed | tf_op | source)
XLA Modules:
  0.0 37.1 jit_solution(16131458902830404971)
XLA Ops:
  0.7 2.6 %edge_rows.1 = (bf16[16,3,8,240]{3,2,1,0:T(8,128)(2,1)S(1)}, bf16[16,3,8,240]{3,2,1,0:T(8,128)(2,1)S(1)}) custom-call(bf16[16,22,8,1440]{3,2,1,0:T(8,128)(2,1)} %bitcast.4), custom_call_target="tpu_custom_call" | custom-call | bytes 6000000 | tf_op jit(solution)/shard_map/edge_rows/pallas_call | solution.py:89
  3.3 3.7 %collective-permute-start = (bf16[16,3,8,240]{3,2,1,0:T(8,128)(2,1)S(1)}, bf16[16,3,8,240]{3,2,1,0:T(8,128)(2,1)S(1)}, u32[]{:S(2)}, u32[]{:S(2)}) collective-permute-start(bf16[16,3,8,240]{3,2,1,0:T(8,128)(2,1)S(1)} %get-tuple-element.18.cross_own), channel_id=1, source_target_pairs={{4,8},{8,4},{5,9},{9,5},{6,10},{10,6},{7,11},{11,7},{12,16},{16,12... | collective-permute-start | bytes 552968 | tf_op jit(solution)/shard_map/ppermute | solution.py:416
  7.0 0.0 collective-permute-start.1
  7.1 0.0 copy-start
  7.1 0.0 copy-start.1
  7.1 3.9 %mid_rows.1 = (bf16[16,16,8,240]{3,2,1,0:T(8,128)(2,1)S(1)}, bf16[96,224]{1,0:T(8,128)(2,1)S(1)}) custom-call(bf16[16,22,8,1440]{3,2,1,0:T(8,128)(2,1)} %bitcast.5, s32[4,10]{1,0:T(4,128)S(1)} %copy-done.3, f32[4,10]{1,0:T(4,128)S(1)} %copy-done.4, s32[4]{0:T(128)S(1)} %copy-done.5), custom_call_target="tpu_custom_call" | custom-call | bytes 12000000 | tf_op jit(solution)/shard_map/mid_rows/pallas_call | solution.py:137
  11.0 0.0 collective-permute-done.cross_ref
  11.0 0.0 collective-permute-done.1.inner_ref
  11.0 0.5 %climate.1 = (bf16[8,32,240]{2,1,0:T(8,128)(2,1)S(1)}, bf16[8,32,240]{2,1,0:T(8,128)(2,1)S(1)}) custom-call(bf16[96,224]{1,0:T(8,128)(2,1)S(1)} %get-tuple-element.17.weights_ref, bf16[16,3,8,240]{3,2,1,0:T(8,128)(2,1)S(1)} %collective-permute-done.cross_ref, bf16[16,3,8,240]{3,2,1,0:T(8,128)(2,1)S(1)} %get-tuple-element.18.cross_own, ...), custom_call_target="tpu_custom_call" | custom-call | bytes 3000000 | tf_op jit(solution)/shard_map/climate/pallas_call | solution.py:219
  11.5 1.6 %collective-permute-start.4 = (bf16[8,32,240]{2,1,0:T(8,128)(2,1)S(1)}, bf16[8,32,240]{2,1,0:T(8,128)(2,1)S(1)}, u32[]{:S(2)}, u32[]{:S(2)}) collective-permute-start(bf16[8,32,240]{2,1,0:T(8,128)(2,1)S(1)} %get-tuple-element.21.refs_0_), channel_id=1, source_target_pairs={{0,1},{1,2},{2,3},{3,0},{4,5},{5,6},{6,7},{7,4},{8,9},{9,10},{10,1... | collective-permute-start | bytes 368648 | tf_op jit(solution)/shard_map/ppermute | solution.py:38
  13.1 1.8 %collective-permute-start.3 = (bf16[8,32,240]{2,1,0:T(8,128)(2,1)S(1)}, bf16[8,32,240]{2,1,0:T(8,128)(2,1)S(1)}, u32[]{:S(2)}, u32[]{:S(2)}) collective-permute-start(bf16[8,32,240]{2,1,0:T(8,128)(2,1)S(1)} %get-tuple-element.22.refs_1_), channel_id=1, source_target_pairs={{0,3},{1,0},{2,1},{3,2},{4,7},{5,4},{6,5},{7,6},{8,11},{9,8},{10,9... | collective-permute-start | bytes 368648 | tf_op jit(solution)/shard_map/ppermute | solution.py:38
  14.8 1.5 %collective-permute-start.2 = (bf16[8,32,240]{2,1,0:T(8,128)(2,1)S(1)}, bf16[8,32,240]{2,1,0:T(8,128)(2,1)S(1)}, u32[]{:S(2)}, u32[]{:S(2)}) collective-permute-start(bf16[8,32,240]{2,1,0:T(8,128)(2,1)S(1)} %get-tuple-element.21.refs_0_), channel_id=1, source_target_pairs={{0,3},{1,0},{2,1},{3,2},{4,7},{5,4},{6,5},{7,6},{8,11},{9,8},{10,9... | collective-permute-start | bytes 368648 | tf_op jit(solution)/shard_map/ppermute | solution.py:38
  16.3 0.5 %collective-permute-start.5 = (bf16[8,32,240]{2,1,0:T(8,128)(2,1)S(1)}, bf16[8,32,240]{2,1,0:T(8,128)(2,1)S(1)}, u32[]{:S(2)}, u32[]{:S(2)}) collective-permute-start(bf16[8,32,240]{2,1,0:T(8,128)(2,1)S(1)} %get-tuple-element.22.refs_1_), channel_id=1, source_target_pairs={{0,1},{1,2},{2,3},{3,0},{4,5},{5,6},{6,7},{7,4},{8,9},{9,10},{10,1... | collective-permute-start | bytes 368648 | tf_op jit(solution)/shard_map/ppermute | solution.py:38
  16.8 1.8 %collective-permute-done.4.refs_4_ = bf16[8,32,240]{2,1,0:T(8,128)(2,1)S(1)} collective-permute-done((bf16[8,32,240]{2,1,0:T(8,128)(2,1)S(1)}, bf16[8,32,240]{2,1,0:T(8,128)(2,1)S(1)}, u32[]{:S(2)}, u32[]{:S(2)}) %collective-permute-start.4) | collective-permute-done | bytes 122912 | tf_op jit(solution)/shard_map/ppermute | solution.py:38
  18.7 0.3 collective-permute-start.6
  18.9 0.5 %collective-permute-done.3.refs_3_ = bf16[8,32,240]{2,1,0:T(8,128)(2,1)S(1)} collective-permute-done((bf16[8,32,240]{2,1,0:T(8,128)(2,1)S(1)}, bf16[8,32,240]{2,1,0:T(8,128)(2,1)S(1)}, u32[]{:S(2)}, u32[]{:S(2)}) %collective-permute-start.3) | collective-permute-done | bytes 122912 | tf_op jit(solution)/shard_map/ppermute | solution.py:38
  19.4 3.0 %collective-permute-start.7 = (bf16[8,32,240]{2,1,0:T(8,128)(2,1)S(1)}, bf16[8,32,240]{2,1,0:T(8,128)(2,1)S(1)}, u32[]{:S(2)}, u32[]{:S(2)}) collective-permute-start(bf16[8,32,240]{2,1,0:T(8,128)(2,1)S(1)} %collective-permute-done.3.refs_3_), channel_id=1, source_target_pairs={{0,3},{1,0},{2,1},{3,2},{4,7},{5,4},{6,5},{7,6},{8,11},{9,8},{10,9... | collective-permute-start | bytes 368648 | tf_op jit(solution)/shard_map/ppermute | solution.py:38
  22.4 1.3 %days.1 = (f32[4,32,32,240]{3,2,1,0:T(8,128)S(1)}, f32[4,32,32,240]{3,2,1,0:T(8,128)S(1)}, f32[4,32,240]{2,1,0:T(8,128)S(1)}) custom-call(bf16[32,4,8,4,240]{4,3,2,1,0:T(4,128)(2,1)S(1)} %copy-done, bf16[32,4,8,4,240]{4,3,2,1,0:T(4,128)(2,1)S(1)} %copy-done.1), custom_call_target="tpu_custom_call" | custom-call | bytes 6000000 | tf_op jit(solution)/shard_map/days/pallas_call | solution.py:250
  23.7 0.0 copy-start.2
  23.7 0.0 collective-permute-done.2.refs_2_
  23.7 0.0 collective-permute-done.5.refs_5_
  23.7 0.5 %decode.1.near_ref = f32[48,32,240]{2,1,0:T(8,128)S(1)} custom-call(bf16[8,32,240]{2,1,0:T(8,128)(2,1)S(1)} %get-tuple-element.21.refs_0_, bf16[8,32,240]{2,1,0:T(8,128)(2,1)S(1)} %get-tuple-element.22.refs_1_, bf16[8,32,240]{2,1,0:T(8,128)(2,1)S(1)} %collective-permute-done.2.refs_2_, bf16[8,32,240]{2,1,0:T(8,128)(2,1)S(1)} %collective-permute-done.3.refs_3_, ...), custom_call_target="tpu_custom_call" | custom-call | bytes 3000000 | tf_op jit(solution)/shard_map/decode/pallas_call | solution.py:269
  24.3 1.2 %collective-permute-done.6.low_ref = bf16[8,32,240]{2,1,0:T(8,128)(2,1)S(1)} collective-permute-done((bf16[8,32,240]{2,1,0:T(8,128)(2,1)S(1)}, bf16[8,32,240]{2,1,0:T(8,128)(2,1)S(1)}, u32[]{:S(2)}, u32[]{:S(2)}) %collective-permute-start.6) | collective-permute-done | bytes 122912 | tf_op jit(solution)/shard_map/ppermute | solution.py:38
  25.4 0.0 collective-permute-done.7.high_ref
  25.4 1.9 %other_sums.1 = (bf16[4,32,240]{2,1,0:T(8,128)(2,1)S(1)}, bf16[4,32,240]{2,1,0:T(8,128)(2,1)S(1)}, bf16[4,32,240]{2,1,0:T(8,128)(2,1)S(1)}, f32[64,32,240]{2,1,0:T(8,128)S(1)}) custom-call(s32[4,32]{1,0:T(4,128)S(1)} %bitcast.2, f32[48,32,240]{2,1,0:T(8,128)S(1)} %decode.1.near_ref, bf16[8,32,240]{2,1,0:T(8,128)(2,1)S(1)} %collective-permute-done.6.low_ref, ...), custom_call_target="tpu_custom_call" | custom-call | bytes 9000000 | tf_op jit(solution)/shard_map/other_sums/pallas_call | solution.py:349
  27.3 0.5 %collective-permute-start.8 = (bf16[4,32,240]{2,1,0:T(8,128)(2,1)S(1)}, bf16[4,32,240]{2,1,0:T(8,128)(2,1)S(1)}, u32[]{:S(2)}, u32[]{:S(2)}) collective-permute-start(bf16[4,32,240]{2,1,0:T(8,128)(2,1)S(1)} %get-tuple-element.26), channel_id=1, source_target_pairs={{0,1},{1,2},{2,3},{3,0},{4,5},{5,6},{6,7},{7,4},{8,9},{9,10},{10,1... | collective-permute-start | bytes 184328 | tf_op jit(solution)/shard_map/ppermute | solution.py:38
  27.9 4.1 %collective-permute-start.9 = (bf16[4,32,240]{2,1,0:T(8,128)(2,1)S(1)}, bf16[4,32,240]{2,1,0:T(8,128)(2,1)S(1)}, u32[]{:S(2)}, u32[]{:S(2)}) collective-permute-start(bf16[4,32,240]{2,1,0:T(8,128)(2,1)S(1)} %get-tuple-element.27), channel_id=1, source_target_pairs={{0,2},{1,3},{2,0},{3,1},{4,6},{5,7},{6,4},{7,5},{8,10},{9,11},{10,... | collective-permute-start | bytes 184328 | tf_op jit(solution)/shard_map/ppermute | solution.py:38
  32.0 0.9 %my_sums.1 = (f32[4,32,240]{2,1,0:T(8,128)S(1)}, f32[32,240]{1,0:T(8,128)S(1)}) custom-call(s32[4,32]{1,0:T(4,128)S(1)} %bitcast.3, f32[128]{0:T(128)S(1)} %copy-done.6, f32[64,32,240]{2,1,0:T(8,128)S(1)} %get-tuple-element.29.clim_ref, f32[4,32,32,240]{3,2,1,0:T(8,128)S(1)} %get-tuple-element.23.fore_ref, f32[4,32,32,240]{3,2,1,0:T(8,128)S(1)} %get-tuple-element.24.obs_ref, ...), custom_call_target="tpu_custom_call" | custom-call | bytes 3000000 | tf_op jit(solution)/shard_map/my_sums/pallas_call | solution.py:371
  32.9 0.0 collective-permute-done.8.one_ref
  32.9 2.0 %collective-permute-done.9.two_ref = bf16[4,32,240]{2,1,0:T(8,128)(2,1)S(1)} collective-permute-done((bf16[4,32,240]{2,1,0:T(8,128)(2,1)S(1)}, bf16[4,32,240]{2,1,0:T(8,128)(2,1)S(1)}, u32[]{:S(2)}, u32[]{:S(2)}) %collective-permute-start.9) | collective-permute-done | bytes 61472 | tf_op jit(solution)/shard_map/ppermute | solution.py:38
  35.0 1.3 %collective-permute-done.10.three_ref = bf16[4,32,240]{2,1,0:T(8,128)(2,1)S(1)} collective-permute-done((bf16[4,32,240]{2,1,0:T(8,128)(2,1)S(1)}, bf16[4,32,240]{2,1,0:T(8,128)(2,1)S(1)}, u32[]{:S(2)}, u32[]{:S(2)}) %collective-permute-start.10) | collective-permute-done | bytes 61472 | tf_op jit(solution)/shard_map/ppermute | solution.py:38
  36.3 0.8 %maps.1 = (f32[1,8,4,240]{3,2,1,0:T(4,128)}, f32[1,8,4,240]{3,2,1,0:T(4,128)}) custom-call(bf16[4,32,240]{2,1,0:T(8,128)(2,1)S(1)} %collective-permute-done.8.one_ref, bf16[4,32,240]{2,1,0:T(8,128)(2,1)S(1)} %collective-permute-done.9.two_ref, bf16[4,32,240]{2,1,0:T(8,128)(2,1)S(1)} %collective-permute-done.10.three_ref, ...), custom_call_target="tpu_custom_call" | custom-call | bytes 3000000 | tf_op jit(solution)/shard_map/maps/pallas_call | solution.py:398
  (12 shorter events, 0.0 us)
Async XLA Ops:
  0.6 6.4 %copy-start.3 = (s32[4,10]{1,0:T(4,128)S(1)}, s32[4,10]{1,0:T(4,128)}, u32[]{:S(2)}) copy-start(s32[4,10]{1,0:T(4,128)} %index_ref.1) | copy-start | bytes 484
  0.6 6.4 %copy-start.4 = (f32[4,10]{1,0:T(4,128)S(1)}, f32[4,10]{1,0:T(4,128)}, u32[]{:S(2)}) copy-start(f32[4,10]{1,0:T(4,128)} %extent_ref.1) | copy-start | bytes 484
  0.7 6.4 %copy-start.5 = (s32[4]{0:T(128)S(1)}, s32[4]{0:T(128)}, u32[]{:S(2)}) copy-start(s32[4]{0:T(128)} %count_ref.1) | copy-start | bytes 52
  3.3 7.7 %collective-permute-start = (bf16[16,3,8,240]{3,2,1,0:T(8,128)(2,1)S(1)}, bf16[16,3,8,240]{3,2,1,0:T(8,128)(2,1)S(1)}, u32[]{:S(2)}, u32[]{:S(2)}) collective-permute-start(bf16[16,3,8,240]{3,2,1,0:T(8,128)(2,1)S(1)} %get-tuple-element.18.cross_own), channel_id=1, source_target_pairs={{4,8},{8,4},{5,9},{9,5},{6,10},{10,6},{7,11},{11,7},{12,16},{16,12... | collective-permute-start | bytes 552968 | tf_op jit(solution)/shard_map/ppermute | solution.py:416
  7.0 4.0 %collective-permute-start.1 = (bf16[16,3,8,240]{3,2,1,0:T(8,128)(2,1)S(1)}, bf16[16,3,8,240]{3,2,1,0:T(8,128)(2,1)S(1)}, u32[]{:S(2)}, u32[]{:S(2)}) collective-permute-start(bf16[16,3,8,240]{3,2,1,0:T(8,128)(2,1)S(1)} %get-tuple-element.20.inner_own), channel_id=1, source_target_pairs={{0,4},{4,0},{8,12},{12,8},{16,20},{20,16},{24,28},{28,24},{32,36},... | collective-permute-start | bytes 552968 | tf_op jit(solution)/shard_map/ppermute | solution.py:417
  7.1 15.3 %copy-start = (bf16[32,4,8,4,240]{4,3,2,1,0:T(4,128)(2,1)S(1)}, bf16[32,4,8,4,240]{4,3,2,1,0:T(4,128)(2,1)}, u32[]{:S(2)}) copy-start(bf16[32,4,8,4,240]{4,3,2,1,0:T(4,128)(2,1)} %fore_ref.1) | copy-start | bytes 5898244
  7.1 15.3 %copy-start.1 = (bf16[32,4,8,4,240]{4,3,2,1,0:T(4,128)(2,1)S(1)}, bf16[32,4,8,4,240]{4,3,2,1,0:T(4,128)(2,1)}, u32[]{:S(2)}) copy-start(bf16[32,4,8,4,240]{4,3,2,1,0:T(4,128)(2,1)} %obs_ref.1) | copy-start | bytes 5898244
  11.5 7.2 %collective-permute-start.4 = (bf16[8,32,240]{2,1,0:T(8,128)(2,1)S(1)}, bf16[8,32,240]{2,1,0:T(8,128)(2,1)S(1)}, u32[]{:S(2)}, u32[]{:S(2)}) collective-permute-start(bf16[8,32,240]{2,1,0:T(8,128)(2,1)S(1)} %get-tuple-element.21.refs_0_), channel_id=1, source_target_pairs={{0,1},{1,2},{2,3},{3,0},{4,5},{5,6},{6,7},{7,4},{8,9},{9,10},{10,1... | collective-permute-start | bytes 368648 | tf_op jit(solution)/shard_map/ppermute | solution.py:38
  13.1 6.4 %collective-permute-start.3 = (bf16[8,32,240]{2,1,0:T(8,128)(2,1)S(1)}, bf16[8,32,240]{2,1,0:T(8,128)(2,1)S(1)}, u32[]{:S(2)}, u32[]{:S(2)}) collective-permute-start(bf16[8,32,240]{2,1,0:T(8,128)(2,1)S(1)} %get-tuple-element.22.refs_1_), channel_id=1, source_target_pairs={{0,3},{1,0},{2,1},{3,2},{4,7},{5,4},{6,5},{7,6},{8,11},{9,8},{10,9... | collective-permute-start | bytes 368648 | tf_op jit(solution)/shard_map/ppermute | solution.py:38
  14.8 8.9 %collective-permute-start.2 = (bf16[8,32,240]{2,1,0:T(8,128)(2,1)S(1)}, bf16[8,32,240]{2,1,0:T(8,128)(2,1)S(1)}, u32[]{:S(2)}, u32[]{:S(2)}) collective-permute-start(bf16[8,32,240]{2,1,0:T(8,128)(2,1)S(1)} %get-tuple-element.21.refs_0_), channel_id=1, source_target_pairs={{0,3},{1,0},{2,1},{3,2},{4,7},{5,4},{6,5},{7,6},{8,11},{9,8},{10,9... | collective-permute-start | bytes 368648 | tf_op jit(solution)/shard_map/ppermute | solution.py:38
  16.3 7.4 %collective-permute-start.5 = (bf16[8,32,240]{2,1,0:T(8,128)(2,1)S(1)}, bf16[8,32,240]{2,1,0:T(8,128)(2,1)S(1)}, u32[]{:S(2)}, u32[]{:S(2)}) collective-permute-start(bf16[8,32,240]{2,1,0:T(8,128)(2,1)S(1)} %get-tuple-element.22.refs_1_), channel_id=1, source_target_pairs={{0,1},{1,2},{2,3},{3,0},{4,5},{5,6},{6,7},{7,4},{8,9},{9,10},{10,1... | collective-permute-start | bytes 368648 | tf_op jit(solution)/shard_map/ppermute | solution.py:38
  18.7 6.7 %collective-permute-start.6 = (bf16[8,32,240]{2,1,0:T(8,128)(2,1)S(1)}, bf16[8,32,240]{2,1,0:T(8,128)(2,1)S(1)}, u32[]{:S(2)}, u32[]{:S(2)}) collective-permute-start(bf16[8,32,240]{2,1,0:T(8,128)(2,1)S(1)} %collective-permute-done.4.refs_4_), channel_id=1, source_target_pairs={{0,1},{1,2},{2,3},{3,0},{4,5},{5,6},{6,7},{7,4},{8,9},{9,10},{10,1... | collective-permute-start | bytes 368648 | tf_op jit(solution)/shard_map/ppermute | solution.py:38
  19.4 6.0 %collective-permute-start.7 = (bf16[8,32,240]{2,1,0:T(8,128)(2,1)S(1)}, bf16[8,32,240]{2,1,0:T(8,128)(2,1)S(1)}, u32[]{:S(2)}, u32[]{:S(2)}) collective-permute-start(bf16[8,32,240]{2,1,0:T(8,128)(2,1)S(1)} %collective-permute-done.3.refs_3_), channel_id=1, source_target_pairs={{0,3},{1,0},{2,1},{3,2},{4,7},{5,4},{6,5},{7,6},{8,11},{9,8},{10,9... | collective-permute-start | bytes 368648 | tf_op jit(solution)/shard_map/ppermute | solution.py:38
  23.7 1.7 %copy-start.2 = (s32[32,4]{0,1:T(4,128)S(1)}, s32[32,4]{0,1:T(4,128)}, u32[]{:S(2)}) copy-start(s32[32,4]{0,1:T(4,128)} %param.12) | copy-start | bytes 1540
  25.4 6.6 %copy-start.6 = (f32[128]{0:T(128)S(1)}, f32[128]{0:T(128)}, u32[]{:S(2)}) copy-start(f32[128]{0:T(128)} %constant.2.clone.scale_ref) | copy-start | bytes 1540
  27.3 5.6 %collective-permute-start.8 = (bf16[4,32,240]{2,1,0:T(8,128)(2,1)S(1)}, bf16[4,32,240]{2,1,0:T(8,128)(2,1)S(1)}, u32[]{:S(2)}, u32[]{:S(2)}) collective-permute-start(bf16[4,32,240]{2,1,0:T(8,128)(2,1)S(1)} %get-tuple-element.26), channel_id=1, source_target_pairs={{0,1},{1,2},{2,3},{3,0},{4,5},{5,6},{6,7},{7,4},{8,9},{9,10},{10,1... | collective-permute-start | bytes 184328 | tf_op jit(solution)/shard_map/ppermute | solution.py:38
  27.9 7.1 %collective-permute-start.9 = (bf16[4,32,240]{2,1,0:T(8,128)(2,1)S(1)}, bf16[4,32,240]{2,1,0:T(8,128)(2,1)S(1)}, u32[]{:S(2)}, u32[]{:S(2)}) collective-permute-start(bf16[4,32,240]{2,1,0:T(8,128)(2,1)S(1)} %get-tuple-element.27), channel_id=1, source_target_pairs={{0,2},{1,3},{2,0},{3,1},{4,6},{5,7},{6,4},{7,5},{8,10},{9,11},{10,... | collective-permute-start | bytes 184328 | tf_op jit(solution)/shard_map/ppermute | solution.py:38
  32.0 4.3 %collective-permute-start.10 = (bf16[4,32,240]{2,1,0:T(8,128)(2,1)S(1)}, bf16[4,32,240]{2,1,0:T(8,128)(2,1)S(1)}, u32[]{:S(2)}, u32[]{:S(2)}) collective-permute-start(bf16[4,32,240]{2,1,0:T(8,128)(2,1)S(1)} %get-tuple-element.28), channel_id=1, source_target_pairs={{0,3},{1,0},{2,1},{3,2},{4,7},{5,4},{6,5},{7,6},{8,11},{9,8},{10,9... | collective-permute-start | bytes 184328 | tf_op jit(solution)/shard_map/ppermute | solution.py:38

commit v8 on v7

--- a/solution.py
+++ b/solution.py
@@ -382,10 +382,25 @@
     )(bins, lat_weights(), clim, fore, obs, error)
 
 
-def maps_kernel(one_ref, two_ref, three_ref, own_ref, scale_ref, rmse_ref, acc_ref):
-    total = own_ref[...]
-    for code_ref in (one_ref, two_ref, three_ref):
-        total = total + decode_sum(code_ref[...])
+def joined_kernel(one_ref, two_ref, own_ref, out_ref):
+    out_ref[...] = own_ref[...] + decode_sum(one_ref[...]) + decode_sum(two_ref[...])
+
+
+def joined(one, two, own):
+    vmem = pl.BlockSpec(memory_space=pltpu.VMEM)
+    return pl.pallas_call(
+        joined_kernel,
+        in_specs=[vmem] * 3,
+        out_specs=vmem,
+        out_shape=jax.ShapeDtypeStruct((4, FLAT, DEST_MERIDIANS), jnp.float32),
+        compiler_params=params(8),
+        cost_estimate=cost(1),
+        name="joined",
+    )(one, two, own)
+
+
+def maps_kernel(three_ref, joined_ref, scale_ref, rmse_ref, acc_ref):
+    total = joined_ref[...] + decode_sum(three_ref[...])
     rmse = jnp.sqrt(scale_ref[...] * total[0] / (DAYS * SLOTS))
     acc = total[1] / jnp.sqrt(total[2] * total[3] + 1e-06)
     rmse_ref[0] = rmse.reshape(VARS, TILE, DEST_MERIDIANS)
@@ -397,7 +412,7 @@
     shape = jax.ShapeDtypeStruct((1, VARS, TILE, DEST_MERIDIANS), jnp.float32)
     return pl.pallas_call(
         maps_kernel,
-        in_specs=[vmem] * 5,
+        in_specs=[vmem] * 3,
         out_specs=[vmem] * 2,
         out_shape=[shape] * 2,
         compiler_params=params(8),
@@ -433,7 +448,7 @@
     one = shifted(to_one, 1)
     three = shifted(to_three, 3)
     mine, scale = my_sums(wanted, clim, fore, obs, error)
-    return tuple(maps(one, two, three, mine, scale))
+    return tuple(maps(three, joined(one, two, mine), scale))
 
 
 def solution(mesh):

time: 37.2 us -> 37.1 us (level)
    pallas_call x1 -> x2, Pallas kernels: 0.82 us -> 0.84 us  [the longest x1 0.72 us: maps(): pl.pallas_call(maps_kernel, in_specs=[vmem] * 3, out_specs=[vmem] * 2, ou...]
where the time goes in v8:
time: 37.1 us; the launch traced here: 37 us
  starting transfers between devices  17 us (46%)
  Pallas kernels  12.5 us (34%)
  waiting for transfers between devices  6.7 us (18%)
  between operations  0.8 us (2%)
    ppermute x9, starting transfers between devices, shifted(): lax.ppermute(value, 'slot', [(i, (i + step) % slots) for i in range(slots)])  13.2 us
    ppermute x9, waiting for transfers between devices, shifted(): lax.ppermute(value, 'slot', [(i, (i + step) % slots) for i in range(slots)])  6.69 us
    pallas_call x1, Pallas kernels, mid_rows(): pl.pallas_call(mid_kernel, in_specs=[hbm] * 4, out_specs=[vmem] * 2, out_...  3.92 us
    ppermute x1, starting transfers between devices, body(): cross = lax.ppermute(cross_own, ('lat', 'slot'), meets)  3.74 us
    pallas_call x1, Pallas kernels, edge_rows(): pl.pallas_call(edge_kernel, in_specs=[pl.BlockSpec(memory_space=pl.ANY)],...  2.64 us
    pallas_call x1, Pallas kernels, other_sums(): pl.pallas_call(others_kernel, in_specs=[pl.BlockSpec(memory_space=pltpu.S...  1.9 us
    pallas_call x1, Pallas kernels, relaid_days(): pl.pallas_call(days_kernel, in_specs=[vmem] * 2, out_specs=[vmem] * 3, ou...  1.31 us
    pallas_call x1, Pallas kernels, my_sums(): pl.pallas_call(mine_kernel, in_specs=[smem] * 2 + [vmem] * 4, out_specs=[...  0.9 us
  transfers between devices with their start and end apart: 11, of which 5 were waited for; matrix products, arithmetic and copies ran while one was open for 0% of the time, Pallas kernels for 18%

profile of v8, /device:TPU:24, one launch (start us, length us, event | category | flops | bytes accessed | tf_op | source)
XLA Modules:
  0.0 37.0 jit_solution(8562398251433511455)
XLA Ops:
  0.7 2.6 %edge_rows.1 = (bf16[16,3,8,240]{3,2,1,0:T(8,128)(2,1)S(1)}, bf16[16,3,8,240]{3,2,1,0:T(8,128)(2,1)S(1)}) custom-call(bf16[16,22,8,1440]{3,2,1,0:T(8,128)(2,1)} %bitcast.4), custom_call_target="tpu_custom_call" | custom-call | bytes 6000000 | tf_op jit(solution)/shard_map/edge_rows/pallas_call | solution.py:89
  3.3 3.7 %collective-permute-start = (bf16[16,3,8,240]{3,2,1,0:T(8,128)(2,1)S(1)}, bf16[16,3,8,240]{3,2,1,0:T(8,128)(2,1)S(1)}, u32[]{:S(2)}, u32[]{:S(2)}) collective-permute-start(bf16[16,3,8,240]{3,2,1,0:T(8,128)(2,1)S(1)} %get-tuple-element.18.cross_own), channel_id=1, source_target_pairs={{4,8},{8,4},{5,9},{9,5},{6,10},{10,6},{7,11},{11,7},{12,16},{16,12... | collective-permute-start | bytes 552968 | tf_op jit(solution)/shard_map/ppermute | solution.py:431
  7.0 0.0 collective-permute-start.1
  7.1 0.0 copy-start
  7.1 0.0 copy-start.1
  7.1 3.9 %mid_rows.1 = (bf16[16,16,8,240]{3,2,1,0:T(8,128)(2,1)S(1)}, bf16[96,224]{1,0:T(8,128)(2,1)S(1)}) custom-call(bf16[16,22,8,1440]{3,2,1,0:T(8,128)(2,1)} %bitcast.5, s32[4,10]{1,0:T(4,128)S(1)} %copy-done.3, f32[4,10]{1,0:T(4,128)S(1)} %copy-done.4, s32[4]{0:T(128)S(1)} %copy-done.5), custom_call_target="tpu_custom_call" | custom-call | bytes 12000000 | tf_op jit(solution)/shard_map/mid_rows/pallas_call | solution.py:137
  11.0 0.0 collective-permute-done.cross_ref
  11.0 0.5 %climate.1 = (bf16[8,32,240]{2,1,0:T(8,128)(2,1)S(1)}, bf16[8,32,240]{2,1,0:T(8,128)(2,1)S(1)}) custom-call(bf16[96,224]{1,0:T(8,128)(2,1)S(1)} %get-tuple-element.17.weights_ref, bf16[16,3,8,240]{3,2,1,0:T(8,128)(2,1)S(1)} %collective-permute-done.cross_ref, bf16[16,3,8,240]{3,2,1,0:T(8,128)(2,1)S(1)} %get-tuple-element.18.cross_own, ...), custom_call_target="tpu_custom_call" | custom-call | bytes 3000000 | tf_op jit(solution)/shard_map/climate/pallas_call | solution.py:219
  11.5 1.6 %collective-permute-start.4 = (bf16[8,32,240]{2,1,0:T(8,128)(2,1)S(1)}, bf16[8,32,240]{2,1,0:T(8,128)(2,1)S(1)}, u32[]{:S(2)}, u32[]{:S(2)}) collective-permute-start(bf16[8,32,240]{2,1,0:T(8,128)(2,1)S(1)} %get-tuple-element.21.refs_0_), channel_id=1, source_target_pairs={{0,1},{1,2},{2,3},{3,0},{4,5},{5,6},{6,7},{7,4},{8,9},{9,10},{10,1... | collective-permute-start | bytes 368648 | tf_op jit(solution)/shard_map/ppermute | solution.py:38
  13.1 1.8 %collective-permute-start.3 = (bf16[8,32,240]{2,1,0:T(8,128)(2,1)S(1)}, bf16[8,32,240]{2,1,0:T(8,128)(2,1)S(1)}, u32[]{:S(2)}, u32[]{:S(2)}) collective-permute-start(bf16[8,32,240]{2,1,0:T(8,128)(2,1)S(1)} %get-tuple-element.22.refs_1_), channel_id=1, source_target_pairs={{0,3},{1,0},{2,1},{3,2},{4,7},{5,4},{6,5},{7,6},{8,11},{9,8},{10,9... | collective-permute-start | bytes 368648 | tf_op jit(solution)/shard_map/ppermute | solution.py:38
  14.8 1.5 %collective-permute-start.2 = (bf16[8,32,240]{2,1,0:T(8,128)(2,1)S(1)}, bf16[8,32,240]{2,1,0:T(8,128)(2,1)S(1)}, u32[]{:S(2)}, u32[]{:S(2)}) collective-permute-start(bf16[8,32,240]{2,1,0:T(8,128)(2,1)S(1)} %get-tuple-element.21.refs_0_), channel_id=1, source_target_pairs={{0,3},{1,0},{2,1},{3,2},{4,7},{5,4},{6,5},{7,6},{8,11},{9,8},{10,9... | collective-permute-start | bytes 368648 | tf_op jit(solution)/shard_map/ppermute | solution.py:38
  16.3 0.5 %collective-permute-start.5 = (bf16[8,32,240]{2,1,0:T(8,128)(2,1)S(1)}, bf16[8,32,240]{2,1,0:T(8,128)(2,1)S(1)}, u32[]{:S(2)}, u32[]{:S(2)}) collective-permute-start(bf16[8,32,240]{2,1,0:T(8,128)(2,1)S(1)} %get-tuple-element.22.refs_1_), channel_id=1, source_target_pairs={{0,1},{1,2},{2,3},{3,0},{4,5},{5,6},{6,7},{7,4},{8,9},{9,10},{10,1... | collective-permute-start | bytes 368648 | tf_op jit(solution)/shard_map/ppermute | solution.py:38
  16.8 1.8 %collective-permute-done.4.refs_4_ = bf16[8,32,240]{2,1,0:T(8,128)(2,1)S(1)} collective-permute-done((bf16[8,32,240]{2,1,0:T(8,128)(2,1)S(1)}, bf16[8,32,240]{2,1,0:T(8,128)(2,1)S(1)}, u32[]{:S(2)}, u32[]{:S(2)}) %collective-permute-start.4) | collective-permute-done | bytes 122912 | tf_op jit(solution)/shard_map/ppermute | solution.py:38
  18.7 0.3 collective-permute-start.6
  18.9 0.5 %collective-permute-done.3.refs_3_ = bf16[8,32,240]{2,1,0:T(8,128)(2,1)S(1)} collective-permute-done((bf16[8,32,240]{2,1,0:T(8,128)(2,1)S(1)}, bf16[8,32,240]{2,1,0:T(8,128)(2,1)S(1)}, u32[]{:S(2)}, u32[]{:S(2)}) %collective-permute-start.3) | collective-permute-done | bytes 122912 | tf_op jit(solution)/shard_map/ppermute | solution.py:38
  19.4 3.0 %collective-permute-start.7 = (bf16[8,32,240]{2,1,0:T(8,128)(2,1)S(1)}, bf16[8,32,240]{2,1,0:T(8,128)(2,1)S(1)}, u32[]{:S(2)}, u32[]{:S(2)}) collective-permute-start(bf16[8,32,240]{2,1,0:T(8,128)(2,1)S(1)} %collective-permute-done.3.refs_3_), channel_id=1, source_target_pairs={{0,3},{1,0},{2,1},{3,2},{4,7},{5,4},{6,5},{7,6},{8,11},{9,8},{10,9... | collective-permute-start | bytes 368648 | tf_op jit(solution)/shard_map/ppermute | solution.py:38
  22.4 1.3 %days.1 = (f32[4,32,32,240]{3,2,1,0:T(8,128)S(1)}, f32[4,32,32,240]{3,2,1,0:T(8,128)S(1)}, f32[4,32,240]{2,1,0:T(8,128)S(1)}) custom-call(bf16[32,4,8,4,240]{4,3,2,1,0:T(4,128)(2,1)S(1)} %copy-done, bf16[32,4,8,4,240]{4,3,2,1,0:T(4,128)(2,1)S(1)} %copy-done.1), custom_call_target="tpu_custom_call" | custom-call | bytes 6000000 | tf_op jit(solution)/shard_map/days/pallas_call | solution.py:250
  23.7 0.0 copy-start.2
  23.7 0.0 collective-permute-done.2.refs_2_
  23.7 0.0 collective-permute-done.5.refs_5_
  23.7 0.5 %decode.1.near_ref = f32[48,32,240]{2,1,0:T(8,128)S(1)} custom-call(bf16[8,32,240]{2,1,0:T(8,128)(2,1)S(1)} %get-tuple-element.21.refs_0_, bf16[8,32,240]{2,1,0:T(8,128)(2,1)S(1)} %get-tuple-element.22.refs_1_, bf16[8,32,240]{2,1,0:T(8,128)(2,1)S(1)} %collective-permute-done.2.refs_2_, bf16[8,32,240]{2,1,0:T(8,128)(2,1)S(1)} %collective-permute-done.3.refs_3_, ...), custom_call_target="tpu_custom_call" | custom-call | bytes 3000000 | tf_op jit(solution)/shard_map/decode/pallas_call | solution.py:269
  24.3 1.2 %collective-permute-done.6.low_ref = bf16[8,32,240]{2,1,0:T(8,128)(2,1)S(1)} collective-permute-done((bf16[8,32,240]{2,1,0:T(8,128)(2,1)S(1)}, bf16[8,32,240]{2,1,0:T(8,128)(2,1)S(1)}, u32[]{:S(2)}, u32[]{:S(2)}) %collective-permute-start.6) | collective-permute-done | bytes 122912 | tf_op jit(solution)/shard_map/ppermute | solution.py:38
  25.4 0.0 collective-permute-done.7.high_ref
  25.4 1.9 %other_sums.1 = (bf16[4,32,240]{2,1,0:T(8,128)(2,1)S(1)}, bf16[4,32,240]{2,1,0:T(8,128)(2,1)S(1)}, bf16[4,32,240]{2,1,0:T(8,128)(2,1)S(1)}, f32[64,32,240]{2,1,0:T(8,128)S(1)}) custom-call(s32[4,32]{1,0:T(4,128)S(1)} %bitcast.2, f32[48,32,240]{2,1,0:T(8,128)S(1)} %decode.1.near_ref, bf16[8,32,240]{2,1,0:T(8,128)(2,1)S(1)} %collective-permute-done.6.low_ref, ...), custom_call_target="tpu_custom_call" | custom-call | bytes 9000000 | tf_op jit(solution)/shard_map/other_sums/pallas_call | solution.py:349
  27.3 0.5 %collective-permute-start.9 = (bf16[4,32,240]{2,1,0:T(8,128)(2,1)S(1)}, bf16[4,32,240]{2,1,0:T(8,128)(2,1)S(1)}, u32[]{:S(2)}, u32[]{:S(2)}) collective-permute-start(bf16[4,32,240]{2,1,0:T(8,128)(2,1)S(1)} %get-tuple-element.27), channel_id=1, source_target_pairs={{0,1},{1,2},{2,3},{3,0},{4,5},{5,6},{6,7},{7,4},{8,9},{9,10},{10,1... | collective-permute-start | bytes 184328 | tf_op jit(solution)/shard_map/ppermute | solution.py:38
  27.9 4.1 %collective-permute-start.10 = (bf16[4,32,240]{2,1,0:T(8,128)(2,1)S(1)}, bf16[4,32,240]{2,1,0:T(8,128)(2,1)S(1)}, u32[]{:S(2)}, u32[]{:S(2)}) collective-permute-start(bf16[4,32,240]{2,1,0:T(8,128)(2,1)S(1)} %get-tuple-element.28), channel_id=1, source_target_pairs={{0,2},{1,3},{2,0},{3,1},{4,6},{5,7},{6,4},{7,5},{8,10},{9,11},{10,... | collective-permute-start | bytes 184328 | tf_op jit(solution)/shard_map/ppermute | solution.py:38
  32.0 0.9 %my_sums.1 = (f32[4,32,240]{2,1,0:T(8,128)S(1)}, f32[32,240]{1,0:T(8,128)S(1)}) custom-call(s32[4,32]{1,0:T(4,128)S(1)} %bitcast.3, f32[128]{0:T(128)S(1)} %copy-done.6, f32[64,32,240]{2,1,0:T(8,128)S(1)} %get-tuple-element.29.clim_ref, f32[4,32,32,240]{3,2,1,0:T(8,128)S(1)} %get-tuple-element.23.fore_ref, f32[4,32,32,240]{3,2,1,0:T(8,128)S(1)} %get-tuple-element.24.obs_ref, ...), custom_call_target="tpu_custom_call" | custom-call | bytes 3000000 | tf_op jit(solution)/shard_map/my_sums/pallas_call | solution.py:371
  32.9 0.0 collective-permute-done.9.one_ref
  32.9 2.0 %collective-permute-done.10.two_ref = bf16[4,32,240]{2,1,0:T(8,128)(2,1)S(1)} collective-permute-done((bf16[4,32,240]{2,1,0:T(8,128)(2,1)S(1)}, bf16[4,32,240]{2,1,0:T(8,128)(2,1)S(1)}, u32[]{:S(2)}, u32[]{:S(2)}) %collective-permute-start.10) | collective-permute-done | bytes 61472 | tf_op jit(solution)/shard_map/ppermute | solution.py:38
  35.0 0.1 joined.1.joined_ref
  35.1 1.2 %collective-permute-done.8.three_ref = bf16[4,32,240]{2,1,0:T(8,128)(2,1)S(1)} collective-permute-done((bf16[4,32,240]{2,1,0:T(8,128)(2,1)S(1)}, bf16[4,32,240]{2,1,0:T(8,128)(2,1)S(1)}, u32[]{:S(2)}, u32[]{:S(2)}) %collective-permute-start.8) | collective-permute-done | bytes 61472 | tf_op jit(solution)/shard_map/ppermute | solution.py:38
  36.3 0.7 %maps.1 = (f32[1,8,4,240]{3,2,1,0:T(4,128)}, f32[1,8,4,240]{3,2,1,0:T(4,128)}) custom-call(bf16[4,32,240]{2,1,0:T(8,128)(2,1)S(1)} %collective-permute-done.8.three_ref, f32[4,32,240]{2,1,0:T(8,128)S(1)} %joined.1.joined_ref, f32[32,240]{1,0:T(8,128)S(1)} %get-tuple-element.31.scale_ref), custom_call_target="tpu_custom_call" | custom-call | bytes 3000000 | tf_op jit(solution)/shard_map/maps/pallas_call | solution.py:413
  (13 shorter events, 0.0 us)
Async XLA Ops:
  0.6 6.4 %copy-start.3 = (s32[4,10]{1,0:T(4,128)S(1)}, s32[4,10]{1,0:T(4,128)}, u32[]{:S(2)}) copy-start(s32[4,10]{1,0:T(4,128)} %index_ref.1) | copy-start | bytes 484
  0.6 6.4 %copy-start.4 = (f32[4,10]{1,0:T(4,128)S(1)}, f32[4,10]{1,0:T(4,128)}, u32[]{:S(2)}) copy-start(f32[4,10]{1,0:T(4,128)} %extent_ref.1) | copy-start | bytes 484
  0.7 6.4 %copy-start.5 = (s32[4]{0:T(128)S(1)}, s32[4]{0:T(128)}, u32[]{:S(2)}) copy-start(s32[4]{0:T(128)} %count_ref.1) | copy-start | bytes 52
  3.3 7.7 %collective-permute-start = (bf16[16,3,8,240]{3,2,1,0:T(8,128)(2,1)S(1)}, bf16[16,3,8,240]{3,2,1,0:T(8,128)(2,1)S(1)}, u32[]{:S(2)}, u32[]{:S(2)}) collective-permute-start(bf16[16,3,8,240]{3,2,1,0:T(8,128)(2,1)S(1)} %get-tuple-element.18.cross_own), channel_id=1, source_target_pairs={{4,8},{8,4},{5,9},{9,5},{6,10},{10,6},{7,11},{11,7},{12,16},{16,12... | collective-permute-start | bytes 552968 | tf_op jit(solution)/shard_map/ppermute | solution.py:431
  7.0 4.0 %collective-permute-start.1 = (bf16[16,3,8,240]{3,2,1,0:T(8,128)(2,1)S(1)}, bf16[16,3,8,240]{3,2,1,0:T(8,128)(2,1)S(1)}, u32[]{:S(2)}, u32[]{:S(2)}) collective-permute-start(bf16[16,3,8,240]{3,2,1,0:T(8,128)(2,1)S(1)} %get-tuple-element.20.inner_own), channel_id=1, source_target_pairs={{0,4},{4,0},{8,12},{12,8},{16,20},{20,16},{24,28},{28,24},{32,36},... | collective-permute-start | bytes 552968 | tf_op jit(solution)/shard_map/ppermute | solution.py:432
  7.1 15.3 %copy-start = (bf16[32,4,8,4,240]{4,3,2,1,0:T(4,128)(2,1)S(1)}, bf16[32,4,8,4,240]{4,3,2,1,0:T(4,128)(2,1)}, u32[]{:S(2)}) copy-start(bf16[32,4,8,4,240]{4,3,2,1,0:T(4,128)(2,1)} %fore_ref.1) | copy-start | bytes 5898244
  7.1 15.3 %copy-start.1 = (bf16[32,4,8,4,240]{4,3,2,1,0:T(4,128)(2,1)S(1)}, bf16[32,4,8,4,240]{4,3,2,1,0:T(4,128)(2,1)}, u32[]{:S(2)}) copy-start(bf16[32,4,8,4,240]{4,3,2,1,0:T(4,128)(2,1)} %obs_ref.1) | copy-start | bytes 5898244
  11.5 7.2 %collective-permute-start.4 = (bf16[8,32,240]{2,1,0:T(8,128)(2,1)S(1)}, bf16[8,32,240]{2,1,0:T(8,128)(2,1)S(1)}, u32[]{:S(2)}, u32[]{:S(2)}) collective-permute-start(bf16[8,32,240]{2,1,0:T(8,128)(2,1)S(1)} %get-tuple-element.21.refs_0_), channel_id=1, source_target_pairs={{0,1},{1,2},{2,3},{3,0},{4,5},{5,6},{6,7},{7,4},{8,9},{9,10},{10,1... | collective-permute-start | bytes 368648 | tf_op jit(solution)/shard_map/ppermute | solution.py:38
  13.1 6.4 %collective-permute-start.3 = (bf16[8,32,240]{2,1,0:T(8,128)(2,1)S(1)}, bf16[8,32,240]{2,1,0:T(8,128)(2,1)S(1)}, u32[]{:S(2)}, u32[]{:S(2)}) collective-permute-start(bf16[8,32,240]{2,1,0:T(8,128)(2,1)S(1)} %get-tuple-element.22.refs_1_), channel_id=1, source_target_pairs={{0,3},{1,0},{2,1},{3,2},{4,7},{5,4},{6,5},{7,6},{8,11},{9,8},{10,9... | collective-permute-start | bytes 368648 | tf_op jit(solution)/shard_map/ppermute | solution.py:38
  14.8 8.9 %collective-permute-start.2 = (bf16[8,32,240]{2,1,0:T(8,128)(2,1)S(1)}, bf16[8,32,240]{2,1,0:T(8,128)(2,1)S(1)}, u32[]{:S(2)}, u32[]{:S(2)}) collective-permute-start(bf16[8,32,240]{2,1,0:T(8,128)(2,1)S(1)} %get-tuple-element.21.refs_0_), channel_id=1, source_target_pairs={{0,3},{1,0},{2,1},{3,2},{4,7},{5,4},{6,5},{7,6},{8,11},{9,8},{10,9... | collective-permute-start | bytes 368648 | tf_op jit(solution)/shard_map/ppermute | solution.py:38
  16.3 7.4 %collective-permute-start.5 = (bf16[8,32,240]{2,1,0:T(8,128)(2,1)S(1)}, bf16[8,32,240]{2,1,0:T(8,128)(2,1)S(1)}, u32[]{:S(2)}, u32[]{:S(2)}) collective-permute-start(bf16[8,32,240]{2,1,0:T(8,128)(2,1)S(1)} %get-tuple-element.22.refs_1_), channel_id=1, source_target_pairs={{0,1},{1,2},{2,3},{3,0},{4,5},{5,6},{6,7},{7,4},{8,9},{9,10},{10,1... | collective-permute-start | bytes 368648 | tf_op jit(solution)/shard_map/ppermute | solution.py:38
  18.7 6.7 %collective-permute-start.6 = (bf16[8,32,240]{2,1,0:T(8,128)(2,1)S(1)}, bf16[8,32,240]{2,1,0:T(8,128)(2,1)S(1)}, u32[]{:S(2)}, u32[]{:S(2)}) collective-permute-start(bf16[8,32,240]{2,1,0:T(8,128)(2,1)S(1)} %collective-permute-done.4.refs_4_), channel_id=1, source_target_pairs={{0,1},{1,2},{2,3},{3,0},{4,5},{5,6},{6,7},{7,4},{8,9},{9,10},{10,1... | collective-permute-start | bytes 368648 | tf_op jit(solution)/shard_map/ppermute | solution.py:38
  19.4 6.0 %collective-permute-start.7 = (bf16[8,32,240]{2,1,0:T(8,128)(2,1)S(1)}, bf16[8,32,240]{2,1,0:T(8,128)(2,1)S(1)}, u32[]{:S(2)}, u32[]{:S(2)}) collective-permute-start(bf16[8,32,240]{2,1,0:T(8,128)(2,1)S(1)} %collective-permute-done.3.refs_3_), channel_id=1, source_target_pairs={{0,3},{1,0},{2,1},{3,2},{4,7},{5,4},{6,5},{7,6},{8,11},{9,8},{10,9... | collective-permute-start | bytes 368648 | tf_op jit(solution)/shard_map/ppermute | solution.py:38
  23.7 1.7 %copy-start.2 = (s32[32,4]{0,1:T(4,128)S(1)}, s32[32,4]{0,1:T(4,128)}, u32[]{:S(2)}) copy-start(s32[32,4]{0,1:T(4,128)} %param.12) | copy-start | bytes 1540
  25.4 6.6 %copy-start.6 = (f32[128]{0:T(128)S(1)}, f32[128]{0:T(128)}, u32[]{:S(2)}) copy-start(f32[128]{0:T(128)} %constant.2.clone.scale_ref) | copy-start | bytes 1540
  27.3 5.6 %collective-permute-start.9 = (bf16[4,32,240]{2,1,0:T(8,128)(2,1)S(1)}, bf16[4,32,240]{2,1,0:T(8,128)(2,1)S(1)}, u32[]{:S(2)}, u32[]{:S(2)}) collective-permute-start(bf16[4,32,240]{2,1,0:T(8,128)(2,1)S(1)} %get-tuple-element.27), channel_id=1, source_target_pairs={{0,1},{1,2},{2,3},{3,0},{4,5},{5,6},{6,7},{7,4},{8,9},{9,10},{10,1... | collective-permute-start | bytes 184328 | tf_op jit(solution)/shard_map/ppermute | solution.py:38
  27.9 7.1 %collective-permute-start.10 = (bf16[4,32,240]{2,1,0:T(8,128)(2,1)S(1)}, bf16[4,32,240]{2,1,0:T(8,128)(2,1)S(1)}, u32[]{:S(2)}, u32[]{:S(2)}) collective-permute-start(bf16[4,32,240]{2,1,0:T(8,128)(2,1)S(1)} %get-tuple-element.28), channel_id=1, source_target_pairs={{0,2},{1,3},{2,0},{3,1},{4,6},{5,7},{6,4},{7,5},{8,10},{9,11},{10,... | collective-permute-start | bytes 184328 | tf_op jit(solution)/shard_map/ppermute | solution.py:38
  32.0 4.3 %collective-permute-start.8 = (bf16[4,32,240]{2,1,0:T(8,128)(2,1)S(1)}, bf16[4,32,240]{2,1,0:T(8,128)(2,1)S(1)}, u32[]{:S(2)}, u32[]{:S(2)}) collective-permute-start(bf16[4,32,240]{2,1,0:T(8,128)(2,1)S(1)} %get-tuple-element.26), channel_id=1, source_target_pairs={{0,3},{1,0},{2,1},{3,2},{4,7},{5,4},{6,5},{7,6},{8,11},{9,8},{10,9... | collective-permute-start | bytes 184328 | tf_op jit(solution)/shard_map/ppermute | solution.py:38
